TPU v7x, 32 devices: a whole 2x2x4 slice. The times are simulated.
32 devices in a mesh: walk: 2 (over core), det: 4 (over y, x), exc: 4 (over z).
Axes of the slice: x: 2, y: 2, z: 4, core: 2. Of those that a mesh axis runs over, the one named last changes fastest.
Arguments:
- inverse: bfloat16 [128, 128, 128], P(('walk', 'det', 'exc')), may hold values from -0.5 to 0.5
- virt_ref: bfloat16 [128, 128], replicated, may hold values from -6 to 6
- new_rows: bfloat16 [128, 128], P(('walk', 'det', 'exc')), may hold values from -6 to 6
- moved_electron: int32 [128], P(('walk', 'det', 'exc')), may hold values from 0 to 127
- coefficient: float32 [16384], P(('det', 'exc')), may hold values from -0.046875 to 0.046875
- occ_list: int32 [4, 16384], P(None, ('det', 'exc')), may hold values from 0 to 127
- virt_list: int32 [4, 16384], P(None, ('det', 'exc')), may hold values from 0 to 127
- exc_rank: int32 [16384], P(('det', 'exc')), may hold values from 1 to 4
Outputs:
- amplitude: float32 [128], P(('walk', 'det', 'exc'))
- ci_grad: float32 [16384], P(('det', 'exc'))
- orb_grad: float32 [128, 128], P('walk')
All inputs are finite; a program needn't handle non-finite values.
Results may differ from a plain program's by a relative error of at most 0.0015.
The roundings to bfloat16 on the way count: a program that leaves them out, or rounds other values in their place, can miss the bound.
Values may be sent and summed in bfloat16 or wider, within the bound.
No kernel may reach another device: no remote copies, remote signals or barrier semaphores. Data moves between devices by JAX's collectives and lax.ppermute only.
A program may use at most 64 MiB of HBM per device.

v0:
```python
import math

import jax
import jax.numpy as jnp
from jax import lax
from jax.sharding import PartitionSpec as P


def minor_det(cells):
    top_a = cells[0] * cells[5] - cells[4] * cells[1]
    top_b = cells[0] * cells[6] - cells[4] * cells[2]
    top_c = cells[0] * cells[7] - cells[4] * cells[3]
    top_d = cells[1] * cells[6] - cells[5] * cells[2]
    top_e = cells[1] * cells[7] - cells[5] * cells[3]
    top_f = cells[2] * cells[7] - cells[6] * cells[3]
    low_f = cells[10] * cells[15] - cells[14] * cells[11]
    low_e = cells[9] * cells[15] - cells[13] * cells[11]
    low_d = cells[9] * cells[14] - cells[13] * cells[10]
    low_c = cells[8] * cells[15] - cells[12] * cells[11]
    low_b = cells[8] * cells[14] - cells[12] * cells[10]
    low_a = cells[8] * cells[13] - cells[12] * cells[9]
    return (
        top_a * low_f
        - top_b * low_e
        + top_c * low_d
        + top_d * low_c
        - top_e * low_b
        + top_f * low_a
    )


def build_minor(entries, exc_rank):
    cells = []
    for row_pos in range(4):
        for col_pos in range(4):
            inside = (exc_rank > row_pos) & (exc_rank > col_pos)
            filler = jnp.float32(1.0 if row_pos == col_pos else 0.0)
            cells.append(jnp.where(inside[None, :], entries[:, row_pos * 4 + col_pos, :], filler))
    return cells


def select_entries(tables, occ_list, virt_list):
    walkers, nocc, nvirt = tables.shape
    count = occ_list.shape[1]
    width = math.gcd(count, max(128, 8192 // walkers))
    steps_count = count // width
    occ_blocks = occ_list.reshape(4, steps_count, width).transpose(1, 0, 2)
    virt_blocks = virt_list.reshape(4, steps_count, width).transpose(1, 0, 2)
    rows_iota = jnp.arange(nocc, dtype=jnp.int32)
    cols_iota = jnp.arange(nvirt, dtype=jnp.int32)

    def one_block(lists):
        occ_part, virt_part = lists
        virt_hot = (cols_iota[:, None, None] == virt_part[None, :, :]).astype(jnp.bfloat16)
        columns = jnp.einsum("wpv,vbi->wpbi", tables, virt_hot, preferred_element_type=jnp.float32)
        picked = []
        for slot in range(4):
            hit = rows_iota[:, None] == occ_part[slot][None, :]
            picked.append(jnp.sum(jnp.where(hit[None, :, None, :], columns, 0.0), axis=1))
        return jnp.stack(picked, axis=1).reshape(walkers, 16, width)

    gathered = lax.map(one_block, (occ_blocks, virt_blocks))
    return gathered.transpose(1, 2, 0, 3).reshape(walkers, 16, count)


def orbital_grad(weighted, occ_list, virt_list, nocc, nvirt):
    count = occ_list.shape[1]
    slots = weighted.reshape(4, 4, count)
    rows_iota = jnp.arange(nocc, dtype=jnp.int32)
    spread = jnp.zeros((nocc, 4, count), jnp.float32)
    for slot in range(4):
        hit = rows_iota[:, None, None] == occ_list[slot][None, None, :]
        spread = spread + jnp.where(hit, slots[slot][None, :, :], 0.0)
    virt_hot = (jnp.arange(nvirt, dtype=jnp.int32)[:, None, None] == virt_list[None, :, :]).astype(
        jnp.float32
    )
    return jnp.einsum("pbi,qbi->pq", spread, virt_hot, precision=lax.Precision.HIGHEST)


def ratios_and_puller(entries, exc_rank):
    return jax.vjp(lambda values: minor_det(build_minor(values, exc_rank)), entries)


def per_device(
    inverse, virt_ref, new_rows, moved_electron, coefficient, occ_list, virt_list, exc_rank
):
    nocc = inverse.shape[1]
    nvirt = virt_ref.shape[1]
    tab_count = inverse.shape[0]
    displaced = jnp.arange(nocc, dtype=jnp.int32)[None, :, None] == moved_electron[:, None, None]
    basis = jnp.where(displaced, new_rows[:, None, :], virt_ref[None, :, :])
    tables = jnp.einsum("wji,wiv->wjv", inverse, basis, preferred_element_type=jnp.float32).astype(
        jnp.bfloat16
    )
    total_walkers = tab_count * lax.axis_size("walk") * lax.axis_size(("det", "exc"))
    entries = select_entries(
        lax.all_gather(tables, ("det", "exc"), axis=0, tiled=True), occ_list, virt_list
    )
    ratios, puller = ratios_and_puller(entries, exc_rank)
    partial_value = jnp.dot(ratios, coefficient, precision=lax.Precision.HIGHEST)
    amplitude = 1.0 + lax.psum(partial_value, ("det", "exc"))
    weight = amplitude / (amplitude * amplitude + 1.0)
    grad_part = jnp.dot(weight, ratios, precision=lax.Precision.HIGHEST)
    cof_sum = jnp.sum(puller(jnp.broadcast_to(weight[:, None], ratios.shape))[0], axis=0)
    amp_mine = lax.dynamic_slice_in_dim(
        amplitude, lax.axis_index(("det", "exc")) * tab_count, tab_count, 0
    )
    ci_grad = lax.psum(grad_part, "walk") / total_walkers
    weighted = cof_sum * coefficient[None, :] / total_walkers
    orbital = orbital_grad(weighted, occ_list, virt_list, nocc, nvirt)
    summed = lax.psum(orbital, ("walk", "det", "exc"))
    share = nocc // lax.axis_size("walk")
    orb_grad = lax.dynamic_slice_in_dim(summed, lax.axis_index("walk") * share, share, 0)
    return (amp_mine, ci_grad, orb_grad)


def solution(mesh):
    return jax.shard_map(
        per_device,
        mesh=mesh,
        in_specs=(
            P(("walk", "det", "exc"), None, None),
            P(),
            P(("walk", "det", "exc"), None),
            P(("walk", "det", "exc")),
            P(("det", "exc")),
            P(None, ("det", "exc")),
            P(None, ("det", "exc")),
            P(("det", "exc")),
        ),
        out_specs=(P(("walk", "det", "exc")), P(("det", "exc")), P("walk", None)),
        check_vma=False,
    )
```

profile of v0, /device:TPU:0, one launch (start us, length us, event | category | flops | bytes accessed | tf_op | source)
XLA Modules:
  0.0 350.4 jit_solution(1757928485655057289)
XLA Ops:
  7.2 0.8 iota_compare_fusion.13
  8.0 0.9 copy.99
  8.9 0.9 fusion.19
  9.8 0.8 copy.100
  10.7 0.7 fusion.43
  11.4 0.9 fusion.46
  12.3 0.9 iota_compare_fusion.9
  13.2 0.8 iota_compare_fusion.11
  14.0 60.3 %all-gather.2.cloned.1.call-done = bf16[64,128,128]{2,1,0:T(8,128)(2,1)} async-done(((bf16[4,128,128]{2,1,0:T(8,128)(2,1)}), bf16[64,128,128]{2,1,0:T(8,128)(2,1)}) %all-gather.2.cloned.1.call-update) | async-done | bytes 2097168 | tf_op jit(solution)/shard_map/all_gather | solution.py:97
  74.3 89.1 %while.13 = (s32[]{:T(128)}, f32[8,64,16,128]{3,1,2,0:T(8,128)}, s32[8,4,128]{2,1,0:T(4,128)}, s32[8,4,128]{2,1,0:T(4,128)}, bf16[64,128,128]{2,1,0:T(8,128)(2,1)}, /*index=5*/s32[]{:T(128)}) while((s32[]{:T(128)}, f32[8,64,16,128]{3,1,2,0:T(8,128)}, s32[8,4,128]{2,1,0:T(4,128)}, s32[8,4,128]{2,1,0:T(4,128)}, ...), condition=%wide.region_5.6_spmd.clone.clone, body=%wide.region_0.5_spmd.clone.clone.sunk | while | flops 1107689472 | bytes 4866137 | solution.py:62
  75.0 0.7 dynamic-slice_bitcast_fusion.2
  75.7 8.8 %fusion.54 = (f32[64,4,128]{2,0,1:T(8,128)S(1)}, f32[64,4,128]{2,0,1:T(8,128)S(1)}, f32[64,4,128]{2,0,1:T(8,128)S(1)}, f32[64,4,128]{2,0,1:T(8,128)S(1)}) fusion(pred[128,128]{1,0:T(8,128)(4,1)S(1)} %get-tuple-element.237, pred[128,128]{1,0:T(8,128)(4,1)S(1)} %get-tuple-element.238, pred[128,128]{1,0:T(8,128)(4,1)S(1)} %get-tuple-element.241, ...), kind=kOutput, calls=%fused_computation.5.clone.1 | convolution fusion | flops 1107230720 | bytes 2689024 | tf_op jit(solution)/shard_map/while/body/eval_jaxpr/wpv,vbi->wpbi/dot_general | solution.py:55
  84.6 0.8 constant_dynamic-update-slice_fusion.2
  86.2 0.7 dynamic-slice_bitcast_fusion.2
  86.9 8.8 %fusion.54 = (f32[64,4,128]{2,0,1:T(8,128)S(1)}, f32[64,4,128]{2,0,1:T(8,128)S(1)}, f32[64,4,128]{2,0,1:T(8,128)S(1)}, f32[64,4,128]{2,0,1:T(8,128)S(1)}) fusion(pred[128,128]{1,0:T(8,128)(4,1)S(1)} %get-tuple-element.237, pred[128,128]{1,0:T(8,128)(4,1)S(1)} %get-tuple-element.238, pred[128,128]{1,0:T(8,128)(4,1)S(1)} %get-tuple-element.241, ...), kind=kOutput, calls=%fused_computation.5.clone.1 | convolution fusion | flops 1107230720 | bytes 2689024 | tf_op jit(solution)/shard_map/while/body/eval_jaxpr/wpv,vbi->wpbi/dot_general | solution.py:55
  95.7 0.8 constant_dynamic-update-slice_fusion.2
  97.3 0.7 dynamic-slice_bitcast_fusion.2
  98.0 8.8 %fusion.54 = (f32[64,4,128]{2,0,1:T(8,128)S(1)}, f32[64,4,128]{2,0,1:T(8,128)S(1)}, f32[64,4,128]{2,0,1:T(8,128)S(1)}, f32[64,4,128]{2,0,1:T(8,128)S(1)}) fusion(pred[128,128]{1,0:T(8,128)(4,1)S(1)} %get-tuple-element.237, pred[128,128]{1,0:T(8,128)(4,1)S(1)} %get-tuple-element.238, pred[128,128]{1,0:T(8,128)(4,1)S(1)} %get-tuple-element.241, ...), kind=kOutput, calls=%fused_computation.5.clone.1 | convolution fusion | flops 1107230720 | bytes 2689024 | tf_op jit(solution)/shard_map/while/body/eval_jaxpr/wpv,vbi->wpbi/dot_general | solution.py:55
  106.8 0.9 constant_dynamic-update-slice_fusion.2
  108.5 0.7 dynamic-slice_bitcast_fusion.2
  109.1 8.8 %fusion.54 = (f32[64,4,128]{2,0,1:T(8,128)S(1)}, f32[64,4,128]{2,0,1:T(8,128)S(1)}, f32[64,4,128]{2,0,1:T(8,128)S(1)}, f32[64,4,128]{2,0,1:T(8,128)S(1)}) fusion(pred[128,128]{1,0:T(8,128)(4,1)S(1)} %get-tuple-element.237, pred[128,128]{1,0:T(8,128)(4,1)S(1)} %get-tuple-element.238, pred[128,128]{1,0:T(8,128)(4,1)S(1)} %get-tuple-element.241, ...), kind=kOutput, calls=%fused_computation.5.clone.1 | convolution fusion | flops 1107230720 | bytes 2689024 | tf_op jit(solution)/shard_map/while/body/eval_jaxpr/wpv,vbi->wpbi/dot_general | solution.py:55
  118.0 0.9 constant_dynamic-update-slice_fusion.2
  119.6 0.7 dynamic-slice_bitcast_fusion.2
  120.3 8.8 %fusion.54 = (f32[64,4,128]{2,0,1:T(8,128)S(1)}, f32[64,4,128]{2,0,1:T(8,128)S(1)}, f32[64,4,128]{2,0,1:T(8,128)S(1)}, f32[64,4,128]{2,0,1:T(8,128)S(1)}) fusion(pred[128,128]{1,0:T(8,128)(4,1)S(1)} %get-tuple-element.237, pred[128,128]{1,0:T(8,128)(4,1)S(1)} %get-tuple-element.238, pred[128,128]{1,0:T(8,128)(4,1)S(1)} %get-tuple-element.241, ...), kind=kOutput, calls=%fused_computation.5.clone.1 | convolution fusion | flops 1107230720 | bytes 2689024 | tf_op jit(solution)/shard_map/while/body/eval_jaxpr/wpv,vbi->wpbi/dot_general | solution.py:55
  129.2 0.8 constant_dynamic-update-slice_fusion.2
  130.7 0.7 dynamic-slice_bitcast_fusion.2
  131.4 8.8 %fusion.54 = (f32[64,4,128]{2,0,1:T(8,128)S(1)}, f32[64,4,128]{2,0,1:T(8,128)S(1)}, f32[64,4,128]{2,0,1:T(8,128)S(1)}, f32[64,4,128]{2,0,1:T(8,128)S(1)}) fusion(pred[128,128]{1,0:T(8,128)(4,1)S(1)} %get-tuple-element.237, pred[128,128]{1,0:T(8,128)(4,1)S(1)} %get-tuple-element.238, pred[128,128]{1,0:T(8,128)(4,1)S(1)} %get-tuple-element.241, ...), kind=kOutput, calls=%fused_computation.5.clone.1 | convolution fusion | flops 1107230720 | bytes 2689024 | tf_op jit(solution)/shard_map/while/body/eval_jaxpr/wpv,vbi->wpbi/dot_general | solution.py:55
  140.3 0.8 constant_dynamic-update-slice_fusion.2
  141.9 0.7 dynamic-slice_bitcast_fusion.2
  142.6 8.8 %fusion.54 = (f32[64,4,128]{2,0,1:T(8,128)S(1)}, f32[64,4,128]{2,0,1:T(8,128)S(1)}, f32[64,4,128]{2,0,1:T(8,128)S(1)}, f32[64,4,128]{2,0,1:T(8,128)S(1)}) fusion(pred[128,128]{1,0:T(8,128)(4,1)S(1)} %get-tuple-element.237, pred[128,128]{1,0:T(8,128)(4,1)S(1)} %get-tuple-element.238, pred[128,128]{1,0:T(8,128)(4,1)S(1)} %get-tuple-element.241, ...), kind=kOutput, calls=%fused_computation.5.clone.1 | convolution fusion | flops 1107230720 | bytes 2689024 | tf_op jit(solution)/shard_map/while/body/eval_jaxpr/wpv,vbi->wpbi/dot_general | solution.py:55
  151.4 0.8 constant_dynamic-update-slice_fusion.2
  153.0 0.7 dynamic-slice_bitcast_fusion.2
  153.7 8.8 %fusion.54 = (f32[64,4,128]{2,0,1:T(8,128)S(1)}, f32[64,4,128]{2,0,1:T(8,128)S(1)}, f32[64,4,128]{2,0,1:T(8,128)S(1)}, f32[64,4,128]{2,0,1:T(8,128)S(1)}) fusion(pred[128,128]{1,0:T(8,128)(4,1)S(1)} %get-tuple-element.237, pred[128,128]{1,0:T(8,128)(4,1)S(1)} %get-tuple-element.238, pred[128,128]{1,0:T(8,128)(4,1)S(1)} %get-tuple-element.241, ...), kind=kOutput, calls=%fused_computation.5.clone.1 | convolution fusion | flops 1107230720 | bytes 2689024 | tf_op jit(solution)/shard_map/while/body/eval_jaxpr/wpv,vbi->wpbi/dot_general | solution.py:55
  162.5 0.8 constant_dynamic-update-slice_fusion.2
  163.4 2.8 copy_bitcast_fusion
  166.2 1.9 copy-done.1
  169.0 39.6 %psum.21 = f32[64]{0:T(128)S(1)} all-reduce(f32[64]{0:T(128)S(1)} %convolution_bitcast_fusion), channel_id=1, replica_groups=mesh['walk'=2,'det'=4,'exc'=4] {'det','exc'}, use_global_device_ids=true, to_apply=%region_6.7 | all-reduce | flops 64 | bytes 512 | tf_op jit(solution)/shard_map/psum | solution.py:101
  209.1 0.8 fusion.37
  210.0 1.9 add_select_fusion.7
  211.9 1.9 add_select_fusion.15
  215.7 1.0 add_select_fusion.9
  216.8 1.0 add_select_fusion.12
  217.8 1.7 add_select_fusion.11
  219.5 2.6 psum.22
  222.1 2.3 add_reduce_fusion
  224.6 2.8 fusion.20
  228.6 113.6 %all-reduce.18.cloned.1.call-done = f32[128,128]{1,0:T(8,128)} async-done(((f32[128,128]{1,0:T(8,128)}), f32[128,128]{1,0:T(8,128)}) %all-reduce.18.cloned.1.call-update) | async-done | bytes 65552 | tf_op jit(solution)/shard_map/psum | solution.py:111
  342.2 1.4 constant_dynamic-slice_fusion.1
  (88 shorter events, 10.8 us)
Async XLA Ops:
  7.2 1.7 copy-start
  7.2 67.1 %all-gather.2.cloned.1.call-start = ((), (), s32[]{:S(2)}) async-start(), calls=%async_computation | async-start | bytes 2228224 | tf_op jit(solution)/shard_map/all_gather | solution.py:97
  10.6 331.6 %all-reduce.18.cloned.1.call-start = ((), (), s32[]{:S(2)}) async-start(), calls=%async_computation.1 | async-start | bytes 131072 | tf_op jit(solution)/shard_map/psum | solution.py:111
  11.4 204.0 %copy-start.8 = (pred[1024]{0:T(1024)(128)(4,1)}, pred[1024]{0:T(1024)(128)(4,1)S(1)}, u32[]{:S(2)}) copy-start(pred[1024]{0:T(1024)(128)(4,1)S(1)} %get-tuple-element.145) | copy-start | bytes 3076
  11.4 204.4 %copy-start.10 = (pred[1024]{0:T(1024)(128)(4,1)}, pred[1024]{0:T(1024)(128)(4,1)S(1)}, u32[]{:S(2)}) copy-start(pred[1024]{0:T(1024)(128)(4,1)S(1)} %get-tuple-element.179) | copy-start | bytes 3076
  11.4 204.3 %copy-start.7 = (pred[1024]{0:T(1024)(128)(4,1)}, pred[1024]{0:T(1024)(128)(4,1)S(1)}, u32[]{:S(2)}) copy-start(pred[1024]{0:T(1024)(128)(4,1)S(1)} %get-tuple-element.184) | copy-start | bytes 3076
  166.1 2.0 copy-start.1
  166.2 2.5 copy-start.11
  208.6 5.2 %copy-start.2 = (f32[64,16,1024]{2,0,1:T(8,128)S(1)}, f32[64,16,1024]{2,0,1:T(8,128)}, u32[]{:S(2)}) copy-start(f32[64,16,1024]{2,0,1:T(8,128)} %copy-done.1) | copy-start | bytes 12582916
  215.7 2.0 copy-start.9
  217.8 6.7 %copy-start.12 = (f32[1024]{0:T(1024)S(1)}, f32[1024]{0:T(1024)}, u32[]{:S(2)}) copy-start(f32[1024]{0:T(1024)} %param.14) | copy-start | bytes 12292
  222.1 2.4 copy-start.3
  222.1 2.5 copy-start.4
  222.1 2.5 copy-start.5
  222.1 2.5 copy-start.6
  222.1 2.5 copy-start.13
  224.5 3.5 %copy-start.14 = (f32[64]{0:T(128)S(1)}, f32[64]{0:T(128)}, u32[]{:S(2)}) copy-start(f32[64]{0:T(128)} %get-tuple-element.187) | copy-start | bytes 772
Sparse Core Ops, SparseCore 0:
  10.8 63.4 all-gather.1
  227.5 114.5 all-reduce.17
where the time goes:
time: 353 us; the launch traced here: 350 us
  waiting for transfers between devices  174 us (49%)
  matrix products  75.2 us (21%)
  blocking collectives  42.2 us (12%)
  local copies, waits for them, and re-layouts  27 us (8%)
  other arithmetic  17.4 us (5%)
  between operations  14.3 us (4%)
    psum x1, waiting for transfers between devices, per_device(): summed = lax.psum(orbital, ('walk', 'det', 'exc'))  114 us
    dot_general x8, matrix products, one_block(): jnp.einsum('wpv,vbi->wpbi', tables, virt_hot, preferred_element_type=jnp....  70.4 us
    all_gather x1, waiting for transfers between devices, per_device(): lax.all_gather(tables, ('det', 'exc'), axis=0, tiled=True)  60.3 us
    psum x1, blocking collectives, per_device(): amplitude = 1.0 + lax.psum(partial_value, ('det', 'exc'))  39.6 us
    select_n x11, other arithmetic, build_minor(): jnp.where(inside[None, :], entries[:, row_pos * 4 + col_pos, :], filler)  9.44 us
  transfers between devices with their start and end apart: 2, of which 2 were waited for; matrix products, arithmetic and copies ran while one was open for 1% of the time, Pallas kernels for 0%

commit v1 on v0

v1 whole, which is shorter than its diff:
```python
import jax
import jax.numpy as jnp
from jax import lax
from jax.experimental import pallas as pl
from jax.experimental.pallas import tpu as pltpu
from jax.sharding import PartitionSpec as P

TILE = 256
DET_AXES = ("det", "exc")
ALL_AXES = ("walk", "det", "exc")


def pair_products(x, y):
    return (
        x[0] * y[1] - y[0] * x[1],
        x[0] * y[2] - y[0] * x[2],
        x[0] * y[3] - y[0] * x[3],
        x[1] * y[2] - y[1] * x[2],
        x[1] * y[3] - y[1] * x[3],
        x[2] * y[3] - y[2] * x[3],
    )


def cofactor_rows(x, y, q):
    qa, qb, qc, qd, qe, qf = q
    dx = (
        y[1] * qa + y[2] * qb + y[3] * qc,
        y[2] * qd + y[3] * qe - y[0] * qa,
        y[3] * qf - y[0] * qb - y[1] * qd,
        -(y[0] * qc + y[1] * qe + y[2] * qf),
    )
    dy = (
        -(x[1] * qa + x[2] * qb + x[3] * qc),
        x[0] * qa - x[2] * qd - x[3] * qe,
        x[0] * qb + x[1] * qd - x[3] * qf,
        x[0] * qc + x[1] * qe + x[2] * qf,
    )
    return dx, dy


def masked_cells(entries, rank):
    cells = []
    for a in range(4):
        row = []
        for b in range(4):
            fill = jnp.float32(1.0 if a == b else 0.0)
            row.append(jnp.where(rank > max(a, b), entries[b][a * 8 : a * 8 + 8], fill))
        cells.append(row)
    return cells


def halves(row):
    top = jnp.broadcast_to(row[:, :128], (4, 128))
    low = jnp.broadcast_to(row[:, 128:], (4, 128))
    return jnp.concatenate([top, low], axis=0)


def walker_sum(x):
    x = x + pltpu.roll(x, 1, 0)
    return x + pltpu.roll(x, 2, 0)


def kernel(
    walkers_total, moved_ref, inv_ref, virt_ref, rows_ref, pay_ref, amp_ref, ci_ref, orb_ref,
    tab, ent, rat, acc,
):
    nblk, _, width = pay_ref.shape
    per_block = width // TILE
    tiles = nblk * per_block
    iota16 = lax.broadcasted_iota(jnp.int32, (16, TILE), 0).astype(jnp.int16)
    one = jnp.ones((16, TILE), jnp.bfloat16)
    zero = jnp.zeros((16, TILE), jnp.bfloat16)

    for w in range(4):
        here = lax.broadcasted_iota(jnp.int32, (128, 128), 0) == moved_ref[w]
        basis = jnp.where(
            here,
            jnp.broadcast_to(rows_ref[w : w + 1, :].astype(jnp.float32), (128, 128)),
            virt_ref[...].astype(jnp.float32),
        ).astype(jnp.bfloat16)
        tab[w * 128 : (w + 1) * 128, :] = jnp.dot(
            inv_ref[w], basis, preferred_element_type=jnp.float32
        ).astype(jnp.bfloat16)

    def load(t):
        block = t // per_block
        lanes = pl.ds(pl.multiple_of((t % per_block) * TILE, TILE), TILE)
        rows = pay_ref[block, :, lanes]
        codes = rows[0:4].astype(jnp.int32)
        occ = jnp.right_shift(codes, 7)
        virt = jnp.bitwise_and(codes, 127)
        return occ, virt, rows[4:5], rows[5:6]

    def spread16(row):
        return jnp.broadcast_to(row, (16, TILE)).astype(jnp.int16)

    def one_hot(v16):
        parts = [jnp.where(v16 == iota16 + jnp.int16(16 * k), one, zero) for k in range(8)]
        return jnp.concatenate(parts, axis=0)

    srow = lax.broadcasted_iota(jnp.int32, (32, 512), 0)
    scol = lax.broadcasted_iota(jnp.int32, (32, 512), 1)
    pick = (jnp.right_shift(scol, 8) == (jnp.right_shift(srow, 2) & 1)) & (
        (jnp.right_shift(scol, 4) & 15) == (srow & 3) * 4 + jnp.right_shift(srow, 3)
    )
    gather_rows = jnp.where(pick, 1.0, 0.0).astype(jnp.bfloat16)

    acc[...] = jnp.zeros_like(acc)
    orb_ref[...] = jnp.zeros_like(orb_ref)

    def forward(t, total):
        occ, virt, rank, coef = load(t)
        occ16 = [spread16(occ[a : a + 1]) for a in range(4)]
        bits = [
            [(o & jnp.int16(bit)) != 0 for bit in (64, 32, 16)]
            + [(o & jnp.int16(15)) == iota16]
            for o in occ16
        ]
        entries = []
        for b in range(4):
            hot = one_hot(spread16(virt[b : b + 1]))
            picked = []
            for w in range(4):
                cols = jnp.dot(
                    tab[w * 128 : (w + 1) * 128, :], hot, preferred_element_type=jnp.float32
                ).astype(jnp.bfloat16)
                parts = [cols[16 * k : 16 * k + 16] for k in range(8)]
                for a in range(4):
                    level = parts
                    for step in range(3):
                        half = len(level) // 2
                        level = [
                            jnp.where(bits[a][step], level[k + half], level[k])
                            for k in range(half)
                        ]
                    picked.append(jnp.where(bits[a][3], level[0], zero))
            stack = jnp.concatenate(picked, axis=0)
            stack = jnp.concatenate([stack[:, :128], stack[:, 128:]], axis=0)
            got = jnp.dot(gather_rows, stack, preferred_element_type=jnp.float32)
            ent[t, b] = got
            entries.append(got)
        cells = masked_cells(entries, halves(rank))
        low = pair_products(cells[2], cells[3])
        top = pair_products(cells[0], cells[1])
        ratio = (
            top[0] * low[5]
            - top[1] * low[4]
            + top[2] * low[3]
            + top[3] * low[2]
            - top[4] * low[1]
            + top[5] * low[0]
        )
        rat[t] = ratio
        return total + ratio * halves(coef)

    total = lax.fori_loop(0, tiles, forward, jnp.zeros((8, 128), jnp.float32))
    lane_sum = jnp.broadcast_to(jnp.sum(total, axis=1, keepdims=True), (8, 128))
    amplitude = 1.0 + lane_sum + pltpu.roll(lane_sum, 4, 0)
    weight = amplitude / (amplitude * amplitude + 1.0)
    amp_ref[...] = amplitude
    weight = weight / walkers_total

    def backward(t, carry):
        occ, virt, rank_row, coef_row = load(t)
        rank = halves(rank_row)
        coef = halves(coef_row)
        summed = walker_sum(rat[t] * weight)
        block = t // per_block
        lane0 = pl.multiple_of((t % per_block) * TILE, TILE)
        ci_ref[block, :, pl.ds(lane0, 128)] = summed[3:4]
        ci_ref[block, :, pl.ds(lane0 + 128, 128)] = summed[7:8]

        cells = masked_cells([ent[t, b] for b in range(4)], rank)
        low = pair_products(cells[2], cells[3])
        top = pair_products(cells[0], cells[1])
        d0, d1 = cofactor_rows(
            cells[0], cells[1], (low[5], -low[4], low[3], low[2], -low[1], low[0])
        )
        d2, d3 = cofactor_rows(
            cells[2], cells[3], (top[5], -top[4], top[3], top[2], -top[1], top[0])
        )
        grads = [d0, d1, d2, d3]
        occ_half = [halves(occ[a : a + 1].astype(jnp.float32)) for a in range(4)]
        same = [[None] * 4 for _ in range(4)]
        for a in range(4):
            for c in range(a):
                same[a][c] = same[c][a] = occ_half[a] == occ_half[c]
        inside = [[rank > max(a, b) for b in range(4)] for a in range(4)]
        hot_occ = [spread16(occ[a : a + 1]) for a in range(4)]
        high_rows = []
        low_rows = []
        for b in range(4):
            plain = [
                jnp.where(inside[a][b], walker_sum(grads[a][b] * weight) * coef, 0.0)
                for a in range(4)
            ]
            high_rows.append([])
            low_rows.append([])
            for a in range(4):
                merged = plain[a]
                for c in range(4):
                    if c != a:
                        merged = merged + jnp.where(same[a][c], plain[c], 0.0)
                high = merged.astype(jnp.bfloat16).astype(jnp.float32)
                rest = merged - high
                for rows, value in ((high_rows[b], high), (low_rows[b], rest)):
                    wide = jnp.concatenate([value[3:4], value[7:8]], axis=1)
                    rows.append(jnp.broadcast_to(wide, (16, TILE)).astype(jnp.bfloat16))
        spread = [[[] for _ in range(4)] for _ in range(2)]
        for k in range(8):
            hits = [hot_occ[a] == iota16 + jnp.int16(16 * k) for a in range(4)]
            for b in range(4):
                for part, rows in enumerate((high_rows[b], low_rows[b])):
                    value = zero
                    for a in range(4):
                        value = jnp.where(hits[a], rows[a], value)
                    spread[part][b].append(value)
        out = None
        for b in range(4):
            left = jnp.concatenate(spread[0][b] + spread[1][b], axis=0)
            hot = one_hot(spread16(virt[b : b + 1]))
            got = lax.dot_general(
                left, hot, (((1,), (1,)), ((), ())), preferred_element_type=jnp.float32
            )
            out = got if out is None else out + got
        acc[...] += out
        return carry

    lax.fori_loop(0, tiles, backward, 0)
    orb_ref[...] = acc[0:128, :] + acc[128:256, :]


def per_device(
    inverse, virt_ref, new_rows, moved_electron, coefficient, occ_list, virt_list, exc_rank
):
    nocc = inverse.shape[1]
    nvirt = virt_ref.shape[1]
    walk_count = lax.axis_size("walk")
    blocks = lax.axis_size(DET_AXES)
    local = coefficient.shape[0]
    ndet = local * blocks
    walkers_total = inverse.shape[0] * walk_count * blocks
    payload = jnp.concatenate(
        [
            (occ_list * 128 + virt_list).astype(jnp.float32),
            exc_rank.astype(jnp.float32)[None],
            coefficient[None],
        ],
        axis=0,
    )
    gathered = lax.all_to_all(
        jnp.broadcast_to(payload[None], (blocks, 6, local)), DET_AXES, 0, 0
    )
    vmem = pl.BlockSpec(memory_space=pltpu.VMEM)
    tiles = ndet // TILE
    amp, ci_part, orb_part = pl.pallas_call(
        lambda *refs: kernel(float(walkers_total), *refs),
        out_shape=(
            jax.ShapeDtypeStruct((8, 128), jnp.float32),
            jax.ShapeDtypeStruct((blocks, 1, local), jnp.float32),
            jax.ShapeDtypeStruct((nocc, nvirt), jnp.float32),
        ),
        in_specs=[pl.BlockSpec(memory_space=pltpu.SMEM)] + [vmem] * 4,
        out_specs=(vmem, vmem, vmem),
        scratch_shapes=[
            pltpu.VMEM((512, 128), jnp.bfloat16),
            pltpu.VMEM((tiles, 4, 32, 128), jnp.float32),
            pltpu.VMEM((tiles, 8, 128), jnp.float32),
            pltpu.VMEM((256, 128), jnp.float32),
        ],
        compiler_params=pltpu.CompilerParams(vmem_limit_bytes=48 << 20),
    )(moved_electron, inverse, virt_ref, new_rows, gathered)

    ci_pieces = ci_part.reshape(blocks, walk_count, local // walk_count).transpose(1, 0, 2)
    orb_pieces = orb_part.reshape(walk_count, blocks, nocc * nvirt // (walk_count * blocks))
    pieces = jnp.concatenate([ci_pieces, orb_pieces], axis=2)
    everyone = walk_count * blocks
    pieces = pieces.reshape(everyone, pieces.shape[2])
    mine = jnp.sum(lax.all_to_all(pieces, ALL_AXES, 0, 0), axis=0)
    ci_mine = mine[: local // walk_count]
    orb_mine = mine[local // walk_count :]
    ci_grad = lax.all_gather(ci_mine, "walk", axis=0, tiled=True)
    orb_all = lax.all_to_all(
        jnp.broadcast_to(orb_mine[None], (blocks, orb_mine.shape[0])), DET_AXES, 0, 0
    )
    return (amp[:4, 0], ci_grad, orb_all.reshape(nocc // walk_count, nvirt))


def solution(mesh):
    return jax.shard_map(
        per_device,
        mesh=mesh,
        in_specs=(
            P(ALL_AXES, None, None),
            P(),
            P(ALL_AXES, None),
            P(ALL_AXES),
            P(DET_AXES),
            P(None, DET_AXES),
            P(None, DET_AXES),
            P(DET_AXES),
        ),
        out_specs=(P(ALL_AXES), P(DET_AXES), P("walk", None)),
        check_vma=False,
    )
```

time: 353 us -> 151 us (0.43)
  waiting for transfers between devices: 174 us -> 4.93 us
  Pallas kernels: 0 us -> 101 us
  matrix products: 75.2 us -> 0 us
  local copies, waits for them, and re-layouts: 27 us -> 2.72 us
  other arithmetic: 17.4 us -> 1.73 us
  between operations: 14.3 us -> 0.75 us
  blocking collectives: 42.2 us -> 35.8 us
    psum x1 -> x0, waiting for transfers between devices: 114 us -> none  [per_device(): summed = lax.psum(orbital, ('walk', 'det', 'exc'))]
    pallas_call x0 -> x1, Pallas kernels: none -> 101 us  [per_device(): pl.pallas_call(lambda *refs: kernel(float(walkers_total), *refs), out_sha...]
    dot_general x12 -> x0, matrix products: 75.2 us -> none  [the longest x8 70.4 us: one_block(): jnp.einsum('wpv,vbi->wpbi', tables, virt_hot, preferred_element_type=jnp....]
    all_gather x1 -> x0, waiting for transfers between devices: 60.3 us -> none  [per_device(): lax.all_gather(tables, ('det', 'exc'), axis=0, tiled=True)]
    psum x2 -> x0, blocking collectives: 42.2 us -> none  [the longest x1 39.6 us: per_device(): amplitude = 1.0 + lax.psum(partial_value, ('det', 'exc'))]
    all_to_all x0 -> x2, blocking collectives: none -> 34.1 us  [the longest x1 24.4 us: per_device(): lax.all_to_all(jnp.broadcast_to(payload[None], (blocks, 6, local)), DET_A...]
    select_n x11 -> x0, other arithmetic: 9.44 us -> none  [build_minor(): jnp.where(inside[None, :], entries[:, row_pos * 4 + col_pos, :], filler)]
    dynamic_slice x10 -> x0, local copies, waits for them, and re-layouts: 7.41 us -> none  [the longest x8 5.46 us: select_entries(): gathered = lax.map(one_block, (occ_blocks, virt_blocks))]
  transfers between devices with their start and end apart: 2 -> 1, of which waited for: 2 -> 1; matrix products, arithmetic and copies ran while one was open for 1% -> 0% of each run, Pallas kernels for 0% -> 0%
where the time goes in v1:
time: 151 us
  Pallas kernels  101 us (67%)
  blocking collectives  35.8 us (24%)
  waiting for transfers between devices  4.93 us (3%)
  starting transfers between devices  3.5 us (2%)
  local copies, waits for them, and re-layouts  2.72 us (2%)
  other arithmetic  1.73 us (1%)
    pallas_call x1, Pallas kernels, per_device(): pl.pallas_call(lambda *refs: kernel(float(walkers_total), *refs), out_sha...  101 us
    all_to_all x1, blocking collectives, per_device(): lax.all_to_all(jnp.broadcast_to(payload[None], (blocks, 6, local)), DET_A...  24.4 us
    all_to_all x1, blocking collectives, per_device(): mine = jnp.sum(lax.all_to_all(pieces, ALL_AXES, 0, 0), axis=0)  9.62 us
    all_to_all x1, waiting for transfers between devices, per_device(): lax.all_to_all(jnp.broadcast_to(orb_mine[None], (blocks, orb_mine.shape[0...  4.93 us
    all_to_all x1, starting transfers between devices, per_device(): lax.all_to_all(jnp.broadcast_to(orb_mine[None], (blocks, orb_mine.shape[0...  3.5 us
  transfers between devices with their start and end apart: 1, of which 1 were waited for; matrix products, arithmetic and copies ran while one was open for 0% of the time, Pallas kernels for 0%

profile of v1, /device:TPU:0, one launch (start us, length us, event | category | flops | bytes accessed | tf_op | source)
XLA Modules:
  0.0 150.7 jit_solution(159242016955019474)
XLA Ops:
  0.6 0.7 convert_element_type.7
  1.3 0.0 copy-start.4
  1.3 0.8 add_convert_fusion
  2.1 0.0 copy-done.4
  2.2 0.0 copy-start
  2.2 0.0 copy-start.1
  2.2 0.0 copy-start.2
  2.2 0.0 copy-start.3
  2.2 24.4 %all_to_all.20.refs_4_ = f32[16,6,1024]{2,1,0:T(8,128)S(1)} all-to-all(f32[16,6,1024]{2,1,0:T(8,128)S(1)} %broadcast_in_dim.20), channel_id=1, replica_groups=mesh['walk'=2,'det'=4,'exc'=4] {'det','exc'}, dimensions={0} | all-to-all | bytes 786432 | tf_op jit(solution)/shard_map/all_to_all | solution.py:251
  26.6 0.0 copy-done
  26.6 0.0 copy-done.1
  26.6 0.0 copy-done.2
  26.7 0.0 copy-done.3
  26.7 101.3 %shard_map.103 = (f32[8,128]{1,0:T(8,128)S(1)}, f32[16,1,1024]{2,1,0:T(1,128)S(1)}, f32[128,128]{1,0:T(8,128)S(1)}) custom-call(s32[4]{0:T(128)S(1)} %copy-done.3, bf16[4,128,128]{2,1,0:T(8,128)(2,1)S(1)} %copy-done, bf16[128,128]{1,0:T(8,128)(2,1)S(1)} %copy-done.1, bf16[4,128]{1,0:T(4,128)(2,1)S(1)} %copy-done.2, f32[16,6,1024]{2,1,0:T(8,128)S(1)} %all_to_all.20.refs_4_), custom_call_target="tpu_custom_call" | custom-call | tf_op jit(solution)/shard_map/pallas_call | solution.py:256
  127.9 0.2 reduce.2
  128.1 0.1 reshape.27
  128.2 0.1 all_to_all.14
  128.3 9.6 %all_to_all.21 = f32[32,1,1024]{2,1,0:T(1,128)S(1)} all-to-all(f32[32,1,1024]{2,1,0:T(1,128)S(1)} %all_to_all.14), channel_id=1, replica_groups=mesh['walk'=2,'det'=4,'exc'=4] {'walk','det','exc'}, dimensions={0} | all-to-all | bytes 262144 | tf_op jit(solution)/shard_map/all_to_all | solution.py:279
  137.9 0.1 reduce_sum.9
  138.0 0.6 broadcast_in_dim.21
  138.7 3.5 %all-to-all-start.2 = ((f32[16,1,512]{2,1,0:T(1,128)}), f32[16,1,512]{2,1,0:T(1,128)S(1)}, u32[]{:S(2)}, u32[]{:S(2)}) async-start(f32[16,1,512]{2,1,0:T(1,128)} %broadcast_in_dim.21), calls=%async_computation.2 | async-start | bytes 65536 | tf_op jit(solution)/shard_map/all_to_all | solution.py:283
  142.2 0.6 slice_reduce_fusion
  142.8 1.8 %all-gather = f32[2,1,512]{2,1,0:T(1,128)S(1)} all-gather(f32[1,1,512]{2,1,0:T(1,128)S(1)} %bitcast.12), channel_id=1, replica_groups=mesh['walk'=2,'det'=4,'exc'=4] {'walk'}, dimensions={0}, use_global_device_ids=true | all-gather | bytes 6144 | tf_op jit(solution)/shard_map/all_gather | solution.py:282
  144.6 4.9 %all-to-all-done.2 = f32[16,1,512]{2,1,0:T(1,128)S(1)} async-done(((f32[16,1,512]{2,1,0:T(1,128)}), f32[16,1,512]{2,1,0:T(1,128)S(1)}, u32[]{:S(2)}, u32[]{:S(2)}) %all-to-all-start.2) | async-done | bytes 32800 | tf_op jit(solution)/shard_map/all_to_all | solution.py:283
  149.5 0.6 copy.16
  150.1 0.6 copy.17
  (6 shorter events, 0.1 us)
Async XLA Ops:
  1.3 0.8 copy-start.4
  2.2 24.5 %copy-start = (bf16[4,128,128]{2,1,0:T(8,128)(2,1)S(1)}, bf16[4,128,128]{2,1,0:T(8,128)(2,1)}, u32[]{:S(2)}) copy-start(bf16[4,128,128]{2,1,0:T(8,128)(2,1)} %refs_1_.1) | copy-start | bytes 393220
  2.2 24.5 %copy-start.1 = (bf16[128,128]{1,0:T(8,128)(2,1)S(1)}, bf16[128,128]{1,0:T(8,128)(2,1)}, u32[]{:S(2)}) copy-start(bf16[128,128]{1,0:T(8,128)(2,1)} %refs_2_.1) | copy-start | bytes 98308
  2.2 24.5 %copy-start.2 = (bf16[4,128]{1,0:T(4,128)(2,1)S(1)}, bf16[4,128]{1,0:T(4,128)(2,1)}, u32[]{:S(2)}) copy-start(bf16[4,128]{1,0:T(4,128)(2,1)} %refs_3_.1) | copy-start | bytes 3076
  2.2 24.5 %copy-start.3 = (s32[4]{0:T(128)S(1)}, s32[4]{0:T(128)}, u32[]{:S(2)}) copy-start(s32[4]{0:T(128)} %refs_0_.1) | copy-start | bytes 52
  138.7 10.8 %all-to-all-start.2 = ((f32[16,1,512]{2,1,0:T(1,128)}), f32[16,1,512]{2,1,0:T(1,128)S(1)}, u32[]{:S(2)}, u32[]{:S(2)}) async-start(f32[16,1,512]{2,1,0:T(1,128)} %broadcast_in_dim.21), calls=%async_computation.2 | async-start | bytes 65536 | tf_op jit(solution)/shard_map/all_to_all | solution.py:283

commit v2 on v0

v2 whole, which is shorter than its diff:
```python
import jax
import jax.numpy as jnp
from jax import lax
from jax.experimental import pallas as pl
from jax.experimental.pallas import tpu as pltpu
from jax.sharding import PartitionSpec as P

TILE = 256
LANES = 128
DET_AXES = ("det", "exc")
ALL_AXES = ("walk", "det", "exc")
FINE = 64.0


def pair_products(x, y):
    return (
        x[0] * y[1] - y[0] * x[1],
        x[0] * y[2] - y[0] * x[2],
        x[0] * y[3] - y[0] * x[3],
        x[1] * y[2] - y[1] * x[2],
        x[1] * y[3] - y[1] * x[3],
        x[2] * y[3] - y[2] * x[3],
    )


def cofactor_rows(x, y, q):
    qa, qb, qc, qd, qe, qf = q
    dx = (
        y[1] * qa + y[2] * qb + y[3] * qc,
        y[2] * qd + y[3] * qe - y[0] * qa,
        y[3] * qf - y[0] * qb - y[1] * qd,
        -(y[0] * qc + y[1] * qe + y[2] * qf),
    )
    dy = (
        -(x[1] * qa + x[2] * qb + x[3] * qc),
        x[0] * qa - x[2] * qd - x[3] * qe,
        x[0] * qb + x[1] * qd - x[3] * qf,
        x[0] * qc + x[1] * qe + x[2] * qf,
    )
    return dx, dy


def masked_cells(entries, rank):
    cells = []
    for a in range(4):
        row = []
        for b in range(4):
            fill = jnp.float32(1.0 if a == b else 0.0)
            row.append(jnp.where(rank > max(a, b), entries[b][a], fill))
        cells.append(row)
    return cells


def determinant(top, low):
    return (
        top[0] * low[5]
        - top[1] * low[4]
        + top[2] * low[3]
        + top[3] * low[2]
        - top[4] * low[1]
        + top[5] * low[0]
    )


def rows8(row):
    return jnp.broadcast_to(row, (8, row.shape[1]))


def rows16(row):
    return jnp.broadcast_to(row, (16, row.shape[1])).astype(jnp.int16)


def iota16():
    return lax.broadcasted_iota(jnp.int32, (16, TILE), 0).astype(jnp.int16)


def one_hot(v16, values):
    base = iota16()
    zero = jnp.zeros((16, TILE), jnp.bfloat16)
    hits = [v16 == base + jnp.int16(16 * k) for k in range(8)]
    parts = [
        jnp.where(hit, jnp.full((16, TILE), value, jnp.bfloat16), zero)
        for value in values
        for hit in hits
    ]
    return jnp.concatenate(parts, axis=0)


def load_lists(pay_ref, t):
    per_block = pay_ref.shape[2] // TILE
    lanes = pl.ds(pl.multiple_of((t % per_block) * TILE, TILE), TILE)
    rows = pay_ref[t // per_block, :, lanes]
    codes = rows[0:4].astype(jnp.int32)
    return jnp.right_shift(codes, 7), jnp.bitwise_and(codes, 127), rows[4:5], rows[5:6]


def power_scale(top):
    scale = jnp.ones_like(top)
    back = jnp.ones_like(top)
    for k in (64, 32, 16, 8, 4, 2, 1):
        big = top >= 2.0 ** (5 + k)
        small = top < 2.0 ** (6 - k)
        up = jnp.float32(2.0**k)
        down = jnp.float32(2.0**-k)
        step = jnp.where(big, down, jnp.where(small, up, 1.0))
        undo = jnp.where(big, up, jnp.where(small, down, 1.0))
        top = top * step
        scale = scale * step
        back = back * undo
    return scale, back


def select_kernel(
    inv_ref, inv2_ref, aux_ref, aux2_ref, virt_ref, pay_ref, ent_ref, amp_ref, wide, tab
):
    nblk, _, width = pay_ref.shape
    tiles = nblk * width // TILE
    sub = lax.broadcasted_iota(jnp.int32, (8, LANES), 0)
    rows_of = lax.broadcasted_iota(jnp.int32, (128, LANES), 0).astype(jnp.float32)
    tops = jnp.zeros((8, LANES), jnp.float32)
    for w in range(8):
        inv, aux = (inv_ref, aux_ref) if w < 4 else (inv2_ref, aux2_ref)
        aux_rows = aux[...].astype(jnp.float32)
        fresh = jnp.broadcast_to(aux_rows[w % 4 : w % 4 + 1], (128, LANES))
        moved = jnp.broadcast_to(aux_rows[w % 4 + 4 : w % 4 + 5], (128, LANES))
        basis = jnp.where(rows_of == moved, fresh, virt_ref[...].astype(jnp.float32))
        table = jnp.dot(
            inv[w % 4], basis.astype(jnp.bfloat16), preferred_element_type=jnp.float32
        )
        table = table.astype(jnp.bfloat16).astype(jnp.float32)
        wide[pl.ds(w, 128, stride=8), :] = table
        tops = jnp.where(sub == w, jnp.max(jnp.abs(table)), tops)
    scale, back = power_scale(tops)
    for k in range(16):
        block = wide[64 * k : 64 * k + 64, :] * jnp.concatenate([scale] * 8, axis=0)
        coarse = block.astype(jnp.float8_e4m3fn)
        rest = (block - coarse.astype(jnp.float32)) * FINE
        tab[64 * k : 64 * k + 64, 0:128] = coarse
        tab[64 * k : 64 * k + 64, 128:256] = rest.astype(jnp.float8_e4m3fn)

    def forward(t, total):
        occ, virt, rank, coef = load_lists(pay_ref, t)
        occ16 = [rows16(occ[a : a + 1]) for a in range(4)]
        bits = [[(o & jnp.int16(bit)) != 0 for bit in (2, 4, 8, 16, 32, 64)] for o in occ16]
        odd = [(rows8(occ[a : a + 1]) & 1) != 0 for a in range(4)]
        entries = [[None] * 4 for _ in range(4)]
        for b in range(4):
            hot = one_hot(rows16(virt[b : b + 1]), (1.0, 1.0 / FINE)).astype(jnp.float8_e4m3fn)
            cols = jnp.dot(tab[...], hot, preferred_element_type=jnp.float32)
            cols = cols.astype(jnp.bfloat16)
            parts = [cols[16 * k : 16 * k + 16] for k in range(64)]
            for a in range(4):
                level = parts
                for step in range(6):
                    level = [
                        jnp.where(bits[a][step], level[2 * k + 1], level[2 * k])
                        for k in range(len(level) // 2)
                    ]
                last = level[0].astype(jnp.float32)
                last = jnp.where(odd[a], last[8:16], last[0:8])
                entries[b][a] = [
                    last[:, h * LANES : (h + 1) * LANES] * back for h in range(TILE // LANES)
                ]
        for h in range(TILE // LANES):
            lanes = slice(h * LANES, (h + 1) * LANES)
            mine = [[entries[b][a][h] for a in range(4)] for b in range(4)]
            for b in range(4):
                for a in range(0, 4, 2):
                    pair = jnp.concatenate([mine[b][a], mine[b][a + 1]], axis=0)
                    ent_ref[t * (TILE // LANES) + h, b, a // 2] = pair.astype(jnp.bfloat16)
            cells = masked_cells(mine, rows8(rank[:, lanes]))
            ratio = determinant(
                pair_products(cells[0], cells[1]), pair_products(cells[2], cells[3])
            )
            total = total + ratio * rows8(coef[:, lanes])
        return total

    total = lax.fori_loop(0, tiles, forward, jnp.zeros((8, LANES), jnp.float32))
    amp_ref[...] = jnp.broadcast_to(jnp.sum(total, axis=1, keepdims=True), (8, LANES))


def all_rows_sum(x):
    x = x + pltpu.roll(x, 4, 0)
    x = x + pltpu.roll(x, 2, 0)
    return x + pltpu.roll(x, 1, 0)


def gradient_kernel(
    walkers_total, part_ref, part2_ref, ent_ref, pay_ref, amp_ref, ci_ref, orb_ref, acc
):
    nblk, _, width = pay_ref.shape
    per_block = width // TILE
    tiles = nblk * per_block
    zero = jnp.zeros((16, TILE), jnp.bfloat16)
    amplitude = 1.0 + part_ref[...] + pltpu.roll(part2_ref[...], 4, 0)
    amp_ref[...] = amplitude
    weight = amplitude / (amplitude * amplitude + 1.0) / walkers_total
    acc[...] = jnp.zeros_like(acc)

    def backward(t, carry):
        occ, virt, rank_row, coef_row = load_lists(pay_ref, t)
        occ16 = [rows16(occ[a : a + 1]) for a in range(4)]
        high = [[[] for _ in range(4)] for _ in range(4)]
        rest = [[[] for _ in range(4)] for _ in range(4)]
        for h in range(TILE // LANES):
            lanes = slice(h * LANES, (h + 1) * LANES)
            rank = rows8(rank_row[:, lanes])
            coef = rows8(coef_row[:, lanes])
            entries = []
            for b in range(4):
                row = []
                for a in range(0, 4, 2):
                    pair = ent_ref[t * (TILE // LANES) + h, b, a // 2].astype(jnp.float32)
                    row += [pair[0:8], pair[8:16]]
                entries.append(row)
            cells = masked_cells(entries, rank)
            low = pair_products(cells[2], cells[3])
            top = pair_products(cells[0], cells[1])
            summed = all_rows_sum(determinant(top, low) * weight)
            lane0 = pl.multiple_of((t % per_block) * TILE, TILE) + h * LANES
            ci_ref[t // per_block, :, pl.ds(lane0, LANES)] = summed[0:1]
            d0, d1 = cofactor_rows(
                cells[0], cells[1], (low[5], -low[4], low[3], low[2], -low[1], low[0])
            )
            d2, d3 = cofactor_rows(
                cells[2], cells[3], (top[5], -top[4], top[3], top[2], -top[1], top[0])
            )
            grads = [d0, d1, d2, d3]
            occ8 = [rows8(occ[a : a + 1, lanes]) for a in range(4)]
            same = {(a, c): occ8[a] == occ8[c] for a in range(4) for c in range(a)}
            for b in range(4):
                plain = [
                    jnp.where(
                        rank > max(a, b), all_rows_sum(grads[a][b] * weight) * coef, 0.0
                    )
                    for a in range(4)
                ]
                for a in range(4):
                    merged = plain[a]
                    for c in range(4):
                        if c != a:
                            hit = same[max(a, c), min(a, c)]
                            merged = merged + jnp.where(hit, plain[c], 0.0)
                    both = jnp.concatenate([merged, merged], axis=0)
                    coarse = both.astype(jnp.bfloat16)
                    high[b][a].append(coarse)
                    rest[b][a].append((both - coarse.astype(jnp.float32)).astype(jnp.bfloat16))
        out = None
        for b in range(4):
            left = []
            for rows in (high[b], rest[b]):
                wide = [jnp.concatenate(rows[a], axis=1) for a in range(4)]
                for k in range(8):
                    value = zero
                    for a in range(4):
                        value = jnp.where(
                            occ16[a] == iota16() + jnp.int16(16 * k), wide[a], value
                        )
                    left.append(value)
            left = jnp.concatenate(left, axis=0)
            hot = one_hot(rows16(virt[b : b + 1]), (1.0,))
            got = lax.dot_general(
                left, hot, (((1,), (1,)), ((), ())), preferred_element_type=jnp.float32
            )
            out = got if out is None else out + got
        acc[...] += out
        return carry

    lax.fori_loop(0, tiles, backward, 0)
    orb_ref[...] = acc[0:128, :] + acc[128:256, :]


def per_device(
    inverse, virt_ref, new_rows, moved_electron, coefficient, occ_list, virt_list, exc_rank
):
    nocc = inverse.shape[1]
    nvirt = virt_ref.shape[1]
    walk_count = lax.axis_size("walk")
    blocks = lax.axis_size(DET_AXES)
    everyone = walk_count * blocks
    local = coefficient.shape[0]
    half = local // 2
    ndet = half * blocks
    walkers_total = inverse.shape[0] * everyone
    partner = [(u, u ^ 1) for u in range(walk_count)]

    aux = jnp.concatenate(
        [
            new_rows,
            jnp.broadcast_to(moved_electron[:, None], (4, nvirt)).astype(jnp.bfloat16),
        ],
        axis=0,
    )
    inverse2 = lax.ppermute(inverse, "walk", partner)
    aux2 = lax.ppermute(aux, "walk", partner)
    payload = jnp.concatenate(
        [
            (occ_list * 128 + virt_list).astype(jnp.float32),
            exc_rank.astype(jnp.float32)[None],
            coefficient[None],
        ],
        axis=0,
    )
    start = (lax.axis_index("walk") & 1) * half
    payload = lax.dynamic_slice_in_dim(payload, start, half, 1)
    gathered = lax.all_to_all(jnp.broadcast_to(payload[None], (blocks, 6, half)), DET_AXES, 0, 0)

    vmem = pl.BlockSpec(memory_space=pltpu.VMEM)
    lane_tiles = ndet // LANES
    params = pltpu.CompilerParams(vmem_limit_bytes=32 << 20)
    entries, part = pl.pallas_call(
        select_kernel,
        out_shape=(
            jax.ShapeDtypeStruct((lane_tiles, 4, 2, 16, LANES), jnp.bfloat16),
            jax.ShapeDtypeStruct((8, LANES), jnp.float32),
        ),
        in_specs=[vmem] * 6,
        out_specs=(vmem, vmem),
        scratch_shapes=[
            pltpu.VMEM((1024, LANES), jnp.float32),
            pltpu.VMEM((1024, 2 * LANES), jnp.float8_e4m3fn),
        ],
        compiler_params=params,
    )(inverse, inverse2, aux, aux2, virt_ref, gathered)
    part2 = lax.ppermute(part, "walk", partner)
    amp, ci_part, orb_part = pl.pallas_call(
        lambda *refs: gradient_kernel(float(walkers_total), *refs),
        out_shape=(
            jax.ShapeDtypeStruct((8, LANES), jnp.float32),
            jax.ShapeDtypeStruct((blocks, 1, half), jnp.float32),
            jax.ShapeDtypeStruct((nocc, nvirt), jnp.float32),
        ),
        in_specs=[vmem] * 4,
        out_specs=(vmem, vmem, vmem),
        scratch_shapes=[pltpu.VMEM((256, LANES), jnp.float32)],
        compiler_params=params,
    )(part, part2, entries, gathered)

    ci_size = half // walk_count
    orb_size = nocc * nvirt // everyone
    ci_pieces = ci_part.reshape(blocks, walk_count, ci_size).transpose(1, 0, 2)
    orb_pieces = orb_part.reshape(walk_count, blocks, orb_size)
    pieces = jnp.concatenate([orb_pieces, ci_pieces], axis=2).reshape(everyone, -1)
    pieces = lax.all_to_all(pieces, ALL_AXES, 0, 0)
    pieces = pieces.reshape(walk_count // 2, 2, blocks, -1)
    orb_mine = jnp.sum(pieces[..., :orb_size], axis=(0, 1, 2))
    ci_mine = jnp.sum(pieces[..., orb_size:], axis=(0, 2))
    orb_all = lax.all_to_all(
        jnp.broadcast_to(orb_mine[None], (blocks, orb_size)), DET_AXES, 0, 0
    )
    ci_grad = lax.all_gather(ci_mine, "walk", axis=1).reshape(local)
    return (amp[:4, 0], ci_grad, orb_all.reshape(nocc // walk_count, nvirt))


def solution(mesh):
    return jax.shard_map(
        per_device,
        mesh=mesh,
        in_specs=(
            P(ALL_AXES, None, None),
            P(),
            P(ALL_AXES, None),
            P(ALL_AXES),
            P(DET_AXES),
            P(None, DET_AXES),
            P(None, DET_AXES),
            P(DET_AXES),
        ),
        out_specs=(P(ALL_AXES), P(DET_AXES), P("walk", None)),
        check_vma=False,
    )
```

time: 353 us -> 86.4 us (0.24)
  waiting for transfers between devices: 174 us -> 21.6 us
  matrix products: 75.2 us -> 0 us
  blocking collectives: 42.2 us -> 1.78 us
  Pallas kernels: 0 us -> 37.3 us
  local copies, waits for them, and re-layouts: 27 us -> 5.66 us
  starting transfers between devices: 0.08 us -> 14.9 us
  other arithmetic: 17.4 us -> 3.78 us
  between operations: 14.3 us -> 0.73 us
    psum x1 -> x0, waiting for transfers between devices: 114 us -> none  [per_device(): summed = lax.psum(orbital, ('walk', 'det', 'exc'))]
    dot_general x12 -> x0, matrix products: 75.2 us -> none  [the longest x8 70.4 us: one_block(): jnp.einsum('wpv,vbi->wpbi', tables, virt_hot, preferred_element_type=jnp....]
    all_gather x1 -> x0, waiting for transfers between devices: 60.3 us -> none  [per_device(): lax.all_gather(tables, ('det', 'exc'), axis=0, tiled=True)]
    psum x2 -> x0, blocking collectives: 42.2 us -> none  [the longest x1 39.6 us: per_device(): amplitude = 1.0 + lax.psum(partial_value, ('det', 'exc'))]
    pallas_call x0 -> x2, Pallas kernels: none -> 37.3 us  [the longest x1 22.7 us: per_device(): pl.pallas_call(select_kernel, out_shape=(jax.ShapeDtypeStruct((lane_tiles...]
    all_to_all x0 -> x3, waiting for transfers between devices: none -> 19.6 us  [the longest x1 7.69 us: per_device(): lax.all_to_all(jnp.broadcast_to(payload[None], (blocks, 6, half)), DET_AX...]
    all_to_all x0 -> x3, starting transfers between devices: none -> 14.4 us  [the longest x1 8.31 us: per_device(): lax.all_to_all(jnp.broadcast_to(payload[None], (blocks, 6, half)), DET_AX...]
    select_n x11 -> x0, other arithmetic: 9.44 us -> none  [build_minor(): jnp.where(inside[None, :], entries[:, row_pos * 4 + col_pos, :], filler)]
  transfers between devices with their start and end apart: 2 -> 6, of which waited for: 2 -> 5; matrix products, arithmetic and copies ran while one was open for 1% -> 3% of each run, Pallas kernels for 0% -> 0%
where the time goes in v2:
time: 86.4 us; the launch traced here: 85.8 us
  Pallas kernels  37.3 us (43%)
  waiting for transfers between devices  21.6 us (25%)
  starting transfers between devices  14.9 us (17%)
  local copies, waits for them, and re-layouts  5.66 us (7%)
  other arithmetic  3.78 us (4%)
  blocking collectives  1.78 us (2%)
    pallas_call x1, Pallas kernels, per_device(): pl.pallas_call(select_kernel, out_shape=(jax.ShapeDtypeStruct((lane_tiles...  22.7 us
    pallas_call x1, Pallas kernels, per_device(): pl.pallas_call(lambda *refs: gradient_kernel(float(walkers_total), *refs)...  14.6 us
    all_to_all x1, starting transfers between devices, per_device(): lax.all_to_all(jnp.broadcast_to(payload[None], (blocks, 6, half)), DET_AX...  8.31 us
    all_to_all x1, waiting for transfers between devices, per_device(): lax.all_to_all(jnp.broadcast_to(payload[None], (blocks, 6, half)), DET_AX...  7.69 us
    all_to_all x1, waiting for transfers between devices, per_device(): pieces = lax.all_to_all(pieces, ALL_AXES, 0, 0)  7.05 us
    all_to_all x1, waiting for transfers between devices, per_device(): lax.all_to_all(jnp.broadcast_to(orb_mine[None], (blocks, orb_size)), DET_...  4.91 us
    all_to_all x1, starting transfers between devices, per_device(): lax.all_to_all(jnp.broadcast_to(orb_mine[None], (blocks, orb_size)), DET_...  3.5 us
    unnamed x6, local copies, waits for them, and re-layouts  2.87 us
  transfers between devices with their start and end apart: 6, of which 5 were waited for; matrix products, arithmetic and copies ran while one was open for 3% of the time, Pallas kernels for 0%

profile of v2, /device:TPU:0, one launch (start us, length us, event | category | flops | bytes accessed | tf_op | source)
XLA Modules:
  0.0 85.8 jit_solution(13294181984114285334)
XLA Ops:
  0.6 0.7 convert_element_type.12
  1.3 0.7 add_convert_fusion
  2.1 0.8 fusion.1
  2.8 0.7 broadcast_in_dim.13
  3.5 8.3 %all-to-all-start = ((f32[16,6,512]{2,1,0:T(8,128)}), f32[16,6,512]{2,1,0:T(8,128)S(1)}, u32[]{:S(2)}, u32[]{:S(2)}) async-start(f32[16,6,512]{2,1,0:T(8,128)} %broadcast_in_dim.13), calls=%async_computation | async-start | bytes 524288 | tf_op jit(solution)/shard_map/all_to_all | solution.py:306
  11.9 0.1 collective-permute-start
  11.9 0.7 convert_element_type.10
  12.6 0.1 pad.6.clone
  12.7 0.8 pad_maximum_fusion.1.aux_ref
  13.4 0.5 collective-permute-start.1
  13.9 0.8 collective-permute-done.1.aux2_ref
  14.8 0.0 collective-permute-done.inv2_ref
  14.8 7.7 %all-to-all-done.pay_ref.refs_3_ = f32[16,6,512]{2,1,0:T(8,128)S(1)} async-done(((f32[16,6,512]{2,1,0:T(8,128)}), f32[16,6,512]{2,1,0:T(8,128)S(1)}, u32[]{:S(2)}, u32[]{:S(2)}) %all-to-all-start) | async-done | bytes 196640 | tf_op jit(solution)/shard_map/all_to_all | solution.py:306
  22.4 0.0 copy-start
  22.4 0.9 %copy-done = bf16[4,128,128]{2,1,0:T(8,128)(2,1)S(1)} copy-done((bf16[4,128,128]{2,1,0:T(8,128)(2,1)S(1)}, bf16[4,128,128]{2,1,0:T(8,128)(2,1)}, u32[]{:S(2)}) %copy-start) | copy-done | bytes 131096
  23.3 0.0 copy-start.1
  23.3 0.8 copy-done.1
  24.1 22.7 %shard_map.103 = (bf16[64,4,2,16,128]{4,3,2,1,0:T(8,128)(2,1)S(1)}, f32[8,128]{1,0:T(8,128)S(1)}) custom-call(bf16[4,128,128]{2,1,0:T(8,128)(2,1)S(1)} %copy-done, bf16[4,128,128]{2,1,0:T(8,128)(2,1)S(1)} %collective-permute-done.inv2_ref, bf16[8,128]{1,0:T(8,128)(2,1)S(1)} %pad_maximum_fusion.1.aux_ref, bf16[8,128]{1,0:T(8,128)(2,1)S(1)} %collective-permute-done.1.aux2_ref, ...), custom_call_target="tpu_custom_call" | custom-call | tf_op jit(solution)/shard_map/pallas_call | solution.py:311
  46.8 0.0 collective-permute-start.2
  46.8 1.2 %collective-permute-done.2.refs_1_ = f32[8,128]{1,0:T(8,128)S(1)} collective-permute-done((f32[8,128]{1,0:T(8,128)S(1)}, f32[8,128]{1,0:T(8,128)S(1)}, u32[]{:S(2)}, u32[]{:S(2)}) %collective-permute-start.2) | collective-permute-done | bytes 4128 | tf_op jit(solution)/shard_map/ppermute | solution.py:325
  48.0 14.6 %shard_map.104 = (f32[8,128]{1,0:T(8,128)S(1)}, f32[16,1,512]{2,1,0:T(1,128)S(1)}, f32[128,128]{1,0:T(8,128)S(1)}) custom-call(f32[8,128]{1,0:T(8,128)S(1)} %get-tuple-element.8.refs_0_, f32[8,128]{1,0:T(8,128)S(1)} %collective-permute-done.2.refs_1_, bf16[64,4,2,16,128]{4,3,2,1,0:T(8,128)(2,1)S(1)} %get-tuple-element.9.refs_2_, ...), custom_call_target="tpu_custom_call" | custom-call | tf_op jit(solution)/shard_map/pallas_call | solution.py:326
  62.6 0.1 reduce.1
  62.7 0.7 all_to_all.14
  63.4 2.5 %all-to-all-start.1 = ((f32[32,1,768]{2,1,0:T(1,128)}), f32[32,1,768]{2,1,0:T(1,128)S(1)}, u32[]{:S(2)}, u32[]{:S(2)}) async-start(f32[32,1,768]{2,1,0:T(1,128)} %all_to_all.14), calls=%async_computation.1 | async-start | bytes 196608 | tf_op jit(solution)/shard_map/all_to_all | solution.py:344
  66.0 0.6 slice_reduce_fusion.2
  66.6 7.1 %all-to-all-done.1 = f32[32,1,768]{2,1,0:T(1,128)S(1)} async-done(((f32[32,1,768]{2,1,0:T(1,128)}), f32[32,1,768]{2,1,0:T(1,128)S(1)}, u32[]{:S(2)}, u32[]{:S(2)}) %all-to-all-start.1) | async-done | bytes 98336 | tf_op jit(solution)/shard_map/all_to_all | solution.py:344
  73.6 0.1 slice_reduce_fusion
  73.7 0.6 broadcast_in_dim.28
  74.3 3.5 %all-to-all-start.2 = ((f32[16,1,512]{2,1,0:T(1,128)}), f32[16,1,512]{2,1,0:T(1,128)S(1)}, u32[]{:S(2)}, u32[]{:S(2)}) async-start(f32[16,1,512]{2,1,0:T(1,128)} %broadcast_in_dim.28), calls=%async_computation.2 | async-start | bytes 65536 | tf_op jit(solution)/shard_map/all_to_all | solution.py:348
  77.9 1.8 %all-gather = f32[2,512]{1,0:T(2,128)S(1)} all-gather(f32[2,256]{1,0:T(2,128)S(1)} %slice_reduce_fusion.1), channel_id=2, replica_groups=mesh['walk'=2,'det'=4,'exc'=4] {'walk'}, dimensions={1}, use_global_device_ids=true | all-gather | bytes 6144 | tf_op jit(solution)/shard_map/all_gather | solution.py:351
  79.7 0.6 copy.14
  80.3 4.9 %all-to-all-done.2 = f32[16,1,512]{2,1,0:T(1,128)S(1)} async-done(((f32[16,1,512]{2,1,0:T(1,128)}), f32[16,1,512]{2,1,0:T(1,128)S(1)}, u32[]{:S(2)}, u32[]{:S(2)}) %all-to-all-start.2) | async-done | bytes 32800 | tf_op jit(solution)/shard_map/all_to_all | solution.py:348
  85.2 0.6 copy.16
  (5 shorter events, 0.1 us)
Async XLA Ops:
  3.5 18.9 %all-to-all-start = ((f32[16,6,512]{2,1,0:T(8,128)}), f32[16,6,512]{2,1,0:T(8,128)S(1)}, u32[]{:S(2)}, u32[]{:S(2)}) async-start(f32[16,6,512]{2,1,0:T(8,128)} %broadcast_in_dim.13), calls=%async_computation | async-start | bytes 524288 | tf_op jit(solution)/shard_map/all_to_all | solution.py:306
  11.9 2.9 %collective-permute-start = (bf16[4,128,128]{2,1,0:T(8,128)(2,1)}, bf16[4,128,128]{2,1,0:T(8,128)(2,1)S(1)}, u32[]{:S(2)}, u32[]{:S(2)}) collective-permute-start(bf16[4,128,128]{2,1,0:T(8,128)(2,1)} %inv_ref.1), channel_id=1, source_target_pairs={{0,16},{16,0},{1,17},{17,1},{2,18},{18,2},{3,19},{19,3},{4,20},{20... | collective-permute-start | bytes 393224 | tf_op jit(solution)/shard_map/ppermute | solution.py:294
  13.4 1.3 %collective-permute-start.1 = (bf16[8,128]{1,0:T(8,128)(2,1)S(1)}, bf16[8,128]{1,0:T(8,128)(2,1)S(1)}, u32[]{:S(2)}, u32[]{:S(2)}) collective-permute-start(bf16[8,128]{1,0:T(8,128)(2,1)S(1)} %pad_maximum_fusion.1.aux_ref), channel_id=1, source_target_pairs={{0,16},{16,0},{1,17},{17,1},{2,18},{18,2},{3,19},{19,3},{4,20},{20... | collective-permute-start | bytes 6152 | tf_op jit(solution)/shard_map/ppermute | solution.py:295
  22.4 0.9 %copy-start = (bf16[4,128,128]{2,1,0:T(8,128)(2,1)S(1)}, bf16[4,128,128]{2,1,0:T(8,128)(2,1)}, u32[]{:S(2)}) copy-start(bf16[4,128,128]{2,1,0:T(8,128)(2,1)} %inv_ref.1) | copy-start | bytes 393220
  23.3 0.8 copy-start.1
  46.8 1.2 %collective-permute-start.2 = (f32[8,128]{1,0:T(8,128)S(1)}, f32[8,128]{1,0:T(8,128)S(1)}, u32[]{:S(2)}, u32[]{:S(2)}) collective-permute-start(f32[8,128]{1,0:T(8,128)S(1)} %get-tuple-element.8.refs_0_), channel_id=1, source_target_pairs={{0,16},{16,0},{1,17},{17,1},{2,18},{18,2},{3,19},{19,3},{4,20},{20... | collective-permute-start | bytes 12296 | tf_op jit(solution)/shard_map/ppermute | solution.py:325
  63.4 10.2 %all-to-all-start.1 = ((f32[32,1,768]{2,1,0:T(1,128)}), f32[32,1,768]{2,1,0:T(1,128)S(1)}, u32[]{:S(2)}, u32[]{:S(2)}) async-start(f32[32,1,768]{2,1,0:T(1,128)} %all_to_all.14), calls=%async_computation.1 | async-start | bytes 196608 | tf_op jit(solution)/shard_map/all_to_all | solution.py:344
  74.3 10.8 %all-to-all-start.2 = ((f32[16,1,512]{2,1,0:T(1,128)}), f32[16,1,512]{2,1,0:T(1,128)S(1)}, u32[]{:S(2)}, u32[]{:S(2)}) async-start(f32[16,1,512]{2,1,0:T(1,128)} %broadcast_in_dim.28), calls=%async_computation.2 | async-start | bytes 65536 | tf_op jit(solution)/shard_map/all_to_all | solution.py:348

commit v3 on v2

--- a/solution.py
+++ b/solution.py
@@ -110,11 +110,26 @@
     return scale, back
 
 
-def select_kernel(
-    inv_ref, inv2_ref, aux_ref, aux2_ref, virt_ref, pay_ref, ent_ref, amp_ref, wide, tab
-):
-    nblk, _, width = pay_ref.shape
-    tiles = nblk * width // TILE
+def payload_kernel(occ_ref, virt_ref, rank_ref, coef_ref, rows_ref, moved_ref, pay_ref, aux_ref):
+    blocks, _, half = pay_ref.shape
+    start = pl.multiple_of((lax.axis_index("walk") & 1) * half, LANES)
+    lanes = pl.ds(start, half)
+    codes = (occ_ref[:, lanes] * 128 + virt_ref[:, lanes]).astype(jnp.float32)
+    rank = rank_ref[:, lanes].astype(jnp.float32)
+    coef = coef_ref[:, lanes]
+    rows = jnp.concatenate([codes, rank, coef], axis=0)
+    for k in range(blocks):
+        pay_ref[k] = rows
+    sub = lax.broadcasted_iota(jnp.int32, (4, LANES), 0)
+    moved = jnp.zeros((4, LANES), jnp.float32)
+    for w in range(4):
+        moved = jnp.where(sub == w, moved_ref[w].astype(jnp.float32), moved)
+    aux_ref[...] = jnp.concatenate(
+        [rows_ref[...].astype(jnp.float32), moved], axis=0
+    ).astype(jnp.bfloat16)
+
+
+def table_kernel(inv_ref, inv2_ref, aux_ref, aux2_ref, virt_ref, tab, back_ref, wide):
     sub = lax.broadcasted_iota(jnp.int32, (8, LANES), 0)
     rows_of = lax.broadcasted_iota(jnp.int32, (128, LANES), 0).astype(jnp.float32)
     tops = jnp.zeros((8, LANES), jnp.float32)
@@ -131,12 +146,19 @@
         wide[pl.ds(w, 128, stride=8), :] = table
         tops = jnp.where(sub == w, jnp.max(jnp.abs(table)), tops)
     scale, back = power_scale(tops)
+    back_ref[...] = back
     for k in range(16):
         block = wide[64 * k : 64 * k + 64, :] * jnp.concatenate([scale] * 8, axis=0)
         coarse = block.astype(jnp.float8_e4m3fn)
         rest = (block - coarse.astype(jnp.float32)) * FINE
         tab[64 * k : 64 * k + 64, 0:128] = coarse
         tab[64 * k : 64 * k + 64, 128:256] = rest.astype(jnp.float8_e4m3fn)
+
+
+def select_kernel(tab, back_ref, pay_ref, ent_ref, amp_ref):
+    nblk, _, width = pay_ref.shape
+    tiles = nblk * width // TILE
+    back = back_ref[...]
 
     def forward(t, total):
         occ, virt, rank, coef = load_lists(pay_ref, t)
@@ -175,7 +197,7 @@
             total = total + ratio * rows8(coef[:, lanes])
         return total
 
-    total = lax.fori_loop(0, tiles, forward, jnp.zeros((8, LANES), jnp.float32))
+    total = lax.fori_loop(0, tiles, forward, jnp.zeros((8, LANES), jnp.float32), unroll=2)
     amp_ref[...] = jnp.broadcast_to(jnp.sum(total, axis=1, keepdims=True), (8, LANES))
 
 
@@ -183,6 +205,29 @@
     x = x + pltpu.roll(x, 4, 0)
     x = x + pltpu.roll(x, 2, 0)
     return x + pltpu.roll(x, 1, 0)
+
+
+def fold(items, dist):
+    sub = lax.broadcasted_iota(jnp.int32, (8, LANES), 0)
+    first = (sub & dist) == 0
+    n = len(items) // 2
+    out = []
+    for x, y in zip(items[:n], items[n:]):
+        x = x + pltpu.roll(x, 8 - dist, 0)
+        y = y + pltpu.roll(y, dist, 0)
+        out.append(jnp.where(first, x, y))
+    return out
+
+
+def walker_sums(items):
+    for dist in (4, 2, 1):
+        items = fold(items, dist)
+    return items[0]
+
+
+def two_rows(x, y):
+    top = lax.broadcasted_iota(jnp.int32, (8, LANES), 0) < 4
+    return jnp.where(top, rows8(x), rows8(y))
 
 
 def gradient_kernel(
@@ -191,17 +236,22 @@
     nblk, _, width = pay_ref.shape
     per_block = width // TILE
     tiles = nblk * per_block
+    packed = len(orb_ref.shape) == 3
+    ci_rows = width // LANES * nblk // orb_ref.shape[0]
     zero = jnp.zeros((16, TILE), jnp.bfloat16)
     amplitude = 1.0 + part_ref[...] + pltpu.roll(part2_ref[...], 4, 0)
     amp_ref[...] = amplitude
     weight = amplitude / (amplitude * amplitude + 1.0) / walkers_total
-    acc[...] = jnp.zeros_like(acc)
+    sub = lax.broadcasted_iota(jnp.int32, (8, LANES), 0)
+    slot_b = sub & 3
+    limits = [
+        jnp.maximum(slot_b, jnp.right_shift(sub, 2) + 2 * g).astype(jnp.float32) for g in range(2)
+    ]
 
     def backward(t, carry):
         occ, virt, rank_row, coef_row = load_lists(pay_ref, t)
         occ16 = [rows16(occ[a : a + 1]) for a in range(4)]
-        high = [[[] for _ in range(4)] for _ in range(4)]
-        rest = [[[] for _ in range(4)] for _ in range(4)]
+        wide = [[[] for _ in range(16)] for _ in range(2)]
         for h in range(TILE // LANES):
             lanes = slice(h * LANES, (h + 1) * LANES)
             rank = rows8(rank_row[:, lanes])
@@ -214,60 +264,99 @@
                     row += [pair[0:8], pair[8:16]]
                 entries.append(row)
             cells = masked_cells(entries, rank)
-            low = pair_products(cells[2], cells[3])
+            low = [x * weight for x in pair_products(cells[2], cells[3])]
             top = pair_products(cells[0], cells[1])
-            summed = all_rows_sum(determinant(top, low) * weight)
-            lane0 = pl.multiple_of((t % per_block) * TILE, TILE) + h * LANES
-            ci_ref[t // per_block, :, pl.ds(lane0, LANES)] = summed[0:1]
+            summed = all_rows_sum(determinant(top, low))
+            block = t // per_block
+            lane_tile = (t % per_block) * (TILE // LANES) + h
+            if packed:
+                dest = lane_tile // (ci_rows) * nblk + block
+                orb_ref[dest, pl.ds(4 + lane_tile % ci_rows, 1), :] = summed[0:1]
+            else:
+                ci_ref[block, pl.ds(lane_tile, 1), :] = summed[0:1]
+            top = [x * weight for x in top]
             d0, d1 = cofactor_rows(
                 cells[0], cells[1], (low[5], -low[4], low[3], low[2], -low[1], low[0])
             )
             d2, d3 = cofactor_rows(
                 cells[2], cells[3], (top[5], -top[4], top[3], top[2], -top[1], top[0])
             )
-            grads = [d0, d1, d2, d3]
-            occ8 = [rows8(occ[a : a + 1, lanes]) for a in range(4)]
-            same = {(a, c): occ8[a] == occ8[c] for a in range(4) for c in range(a)}
-            for b in range(4):
-                plain = [
-                    jnp.where(
-                        rank > max(a, b), all_rows_sum(grads[a][b] * weight) * coef, 0.0
-                    )
-                    for a in range(4)
-                ]
-                for a in range(4):
-                    merged = plain[a]
-                    for c in range(4):
-                        if c != a:
-                            hit = same[max(a, c), min(a, c)]
-                            merged = merged + jnp.where(hit, plain[c], 0.0)
-                    both = jnp.concatenate([merged, merged], axis=0)
-                    coarse = both.astype(jnp.bfloat16)
-                    high[b][a].append(coarse)
-                    rest[b][a].append((both - coarse.astype(jnp.float32)).astype(jnp.bfloat16))
-        out = None
-        for b in range(4):
-            left = []
-            for rows in (high[b], rest[b]):
-                wide = [jnp.concatenate(rows[a], axis=1) for a in range(4)]
-                for k in range(8):
+            plain = [
+                jnp.where(rank > limits[g], walker_sums(list(x + y)) * coef, 0.0)
+                for g, (x, y) in enumerate(((d0, d1), (d2, d3)))
+            ]
+            turned = [pltpu.roll(x, 4, 0) for x in plain]
+            occ_a = two_rows(occ[0:1, lanes], occ[1:2, lanes])
+            occ_b = two_rows(occ[2:3, lanes], occ[3:4, lanes])
+            turn_a = two_rows(occ[1:2, lanes], occ[0:1, lanes])
+            turn_b = two_rows(occ[3:4, lanes], occ[2:3, lanes])
+            straight = occ_a == occ_b
+            merged = [
+                plain[0]
+                + jnp.where(occ_a == turn_a, turned[0], 0.0)
+                + jnp.where(straight, plain[1], 0.0)
+                + jnp.where(occ_a == turn_b, turned[1], 0.0),
+                plain[1]
+                + jnp.where(occ_b == turn_b, turned[1], 0.0)
+                + jnp.where(straight, plain[0], 0.0)
+                + jnp.where(occ_b == turn_a, turned[0], 0.0),
+            ]
+            for g in range(2):
+                high = merged[g].astype(jnp.bfloat16).astype(jnp.float32)
+                rest = merged[g] - high
+                for part, value in enumerate((high, rest)):
+                    for r in range(8):
+                        one = rows8(value[r : r + 1])
+                        wide[part][8 * g + r].append(
+                            jnp.concatenate([one, one], axis=0).astype(jnp.bfloat16)
+                        )
+        wide = [[jnp.concatenate(x, axis=1) for x in rows] for rows in wide]
+        left = [[None] * 16 for _ in range(4)]
+        for k in range(8):
+            hits = [occ16[a] == iota16() + jnp.int16(16 * k) for a in range(4)]
+            for part in range(2):
+                for b in range(4):
                     value = zero
                     for a in range(4):
-                        value = jnp.where(
-                            occ16[a] == iota16() + jnp.int16(16 * k), wide[a], value
-                        )
-                    left.append(value)
-            left = jnp.concatenate(left, axis=0)
-            hot = one_hot(rows16(virt[b : b + 1]), (1.0,))
-            got = lax.dot_general(
-                left, hot, (((1,), (1,)), ((), ())), preferred_element_type=jnp.float32
-            )
-            out = got if out is None else out + got
-        acc[...] += out
+                        value = jnp.where(hits[a], wide[part][4 * a + b], value)
+                    left[b][part * 8 + k] = value
+        left = jnp.concatenate([jnp.concatenate(left[b], axis=0) for b in range(4)], axis=1)
+        right = jnp.concatenate(
+            [one_hot(rows16(virt[b : b + 1]), (1.0,)) for b in range(4)], axis=1
+        )
+        acc[...] += lax.dot_general(
+            left, right, (((1,), (1,)), ((), ())), preferred_element_type=jnp.float32
+        )
         return carry
 
-    lax.fori_loop(0, tiles, backward, 0)
-    orb_ref[...] = acc[0:128, :] + acc[128:256, :]
+    acc[...] = jnp.zeros_like(acc)
+    if packed:
+        orb_ref[...] = jnp.zeros_like(orb_ref)
+    lax.fori_loop(0, tiles, backward, 0, unroll=4)
+    total = acc[0:128, :] + acc[128:256, :]
+    if packed:
+        for dest in range(orb_ref.shape[0]):
+            orb_ref[dest, 0:4, :] = total[4 * dest : 4 * dest + 4]
+    else:
+        orb_ref[...] = total
+
+
+def sums_kernel(pieces_ref, orb_ref, ci_ref):
+    everyone = pieces_ref.shape[0]
+    blocks = orb_ref.shape[0] // 4
+    totals = []
+    for parity in range(2):
+        picked = [
+            pieces_ref[s] for s in range(everyone) if (s // blocks) % 2 == parity
+        ]
+        while len(picked) > 1:
+            picked = [x + y for x, y in zip(picked[::2], picked[1::2])]
+        totals.append(picked[0])
+    both = totals[0] + totals[1]
+    pair = jnp.concatenate([both[0:4], both[0:4]], axis=0)
+    for k in range(blocks // 2):
+        orb_ref[8 * k : 8 * k + 8, :] = pair
+    ci_ref[...] = jnp.concatenate([totals[0][4:6], totals[1][4:6]], axis=0)
 
 
 def per_device(
@@ -283,52 +372,56 @@
     ndet = half * blocks
     walkers_total = inverse.shape[0] * everyone
     partner = [(u, u ^ 1) for u in range(walk_count)]
-
-    aux = jnp.concatenate(
-        [
-            new_rows,
-            jnp.broadcast_to(moved_electron[:, None], (4, nvirt)).astype(jnp.bfloat16),
-        ],
-        axis=0,
-    )
+    vmem = pl.BlockSpec(memory_space=pltpu.VMEM)
+    smem = pl.BlockSpec(memory_space=pltpu.SMEM)
+    params = pltpu.CompilerParams(vmem_limit_bytes=32 << 20)
+
     inverse2 = lax.ppermute(inverse, "walk", partner)
+    payload, aux = pl.pallas_call(
+        payload_kernel,
+        out_shape=(
+            jax.ShapeDtypeStruct((blocks, 6, half), jnp.float32),
+            jax.ShapeDtypeStruct((8, LANES), jnp.bfloat16),
+        ),
+        in_specs=[vmem] * 5 + [smem],
+        out_specs=(vmem, vmem),
+    )(occ_list, virt_list, exc_rank[None], coefficient[None], new_rows, moved_electron)
     aux2 = lax.ppermute(aux, "walk", partner)
-    payload = jnp.concatenate(
-        [
-            (occ_list * 128 + virt_list).astype(jnp.float32),
-            exc_rank.astype(jnp.float32)[None],
-            coefficient[None],
-        ],
-        axis=0,
-    )
-    start = (lax.axis_index("walk") & 1) * half
-    payload = lax.dynamic_slice_in_dim(payload, start, half, 1)
-    gathered = lax.all_to_all(jnp.broadcast_to(payload[None], (blocks, 6, half)), DET_AXES, 0, 0)
-
-    vmem = pl.BlockSpec(memory_space=pltpu.VMEM)
-    lane_tiles = ndet // LANES
-    params = pltpu.CompilerParams(vmem_limit_bytes=32 << 20)
+    gathered = lax.all_to_all(payload, DET_AXES, 0, 0)
+
+    table, back = pl.pallas_call(
+        table_kernel,
+        out_shape=(
+            jax.ShapeDtypeStruct((1024, 2 * LANES), jnp.float8_e4m3fn),
+            jax.ShapeDtypeStruct((8, LANES), jnp.float32),
+        ),
+        in_specs=[vmem] * 5,
+        out_specs=(vmem, vmem),
+        scratch_shapes=[pltpu.VMEM((1024, LANES), jnp.float32)],
+        compiler_params=params,
+    )(inverse, inverse2, aux, aux2, virt_ref)
     entries, part = pl.pallas_call(
         select_kernel,
         out_shape=(
-            jax.ShapeDtypeStruct((lane_tiles, 4, 2, 16, LANES), jnp.bfloat16),
+            jax.ShapeDtypeStruct((ndet // LANES, 4, 2, 16, LANES), jnp.bfloat16),
             jax.ShapeDtypeStruct((8, LANES), jnp.float32),
         ),
-        in_specs=[vmem] * 6,
+        in_specs=[vmem] * 3,
         out_specs=(vmem, vmem),
-        scratch_shapes=[
-            pltpu.VMEM((1024, LANES), jnp.float32),
-            pltpu.VMEM((1024, 2 * LANES), jnp.float8_e4m3fn),
-        ],
         compiler_params=params,
-    )(inverse, inverse2, aux, aux2, virt_ref, gathered)
+    )(table, back, gathered)
     part2 = lax.ppermute(part, "walk", partner)
+
+    ci_size = half // walk_count
+    orb_size = nocc * nvirt // everyone
+    packed = orb_size == 4 * LANES and ci_size == 2 * LANES and nvirt == LANES
+    orb_shape = (everyone, 8, LANES) if packed else (nocc, nvirt)
     amp, ci_part, orb_part = pl.pallas_call(
         lambda *refs: gradient_kernel(float(walkers_total), *refs),
         out_shape=(
             jax.ShapeDtypeStruct((8, LANES), jnp.float32),
-            jax.ShapeDtypeStruct((blocks, 1, half), jnp.float32),
-            jax.ShapeDtypeStruct((nocc, nvirt), jnp.float32),
+            jax.ShapeDtypeStruct((blocks, half // LANES, LANES), jnp.float32),
+            jax.ShapeDtypeStruct(orb_shape, jnp.float32),
         ),
         in_specs=[vmem] * 4,
         out_specs=(vmem, vmem, vmem),
@@ -336,18 +429,30 @@
         compiler_params=params,
     )(part, part2, entries, gathered)
 
-    ci_size = half // walk_count
-    orb_size = nocc * nvirt // everyone
-    ci_pieces = ci_part.reshape(blocks, walk_count, ci_size).transpose(1, 0, 2)
-    orb_pieces = orb_part.reshape(walk_count, blocks, orb_size)
-    pieces = jnp.concatenate([orb_pieces, ci_pieces], axis=2).reshape(everyone, -1)
-    pieces = lax.all_to_all(pieces, ALL_AXES, 0, 0)
-    pieces = pieces.reshape(walk_count // 2, 2, blocks, -1)
-    orb_mine = jnp.sum(pieces[..., :orb_size], axis=(0, 1, 2))
-    ci_mine = jnp.sum(pieces[..., orb_size:], axis=(0, 2))
-    orb_all = lax.all_to_all(
-        jnp.broadcast_to(orb_mine[None], (blocks, orb_size)), DET_AXES, 0, 0
-    )
+    if packed:
+        pieces = lax.all_to_all(orb_part, ALL_AXES, 0, 0)
+        orb_rows, ci_mine = pl.pallas_call(
+            sums_kernel,
+            out_shape=(
+                jax.ShapeDtypeStruct((blocks * 4, LANES), jnp.float32),
+                jax.ShapeDtypeStruct((4, LANES), jnp.float32),
+            ),
+            in_specs=[vmem],
+            out_specs=(vmem, vmem),
+        )(pieces)
+        ci_mine = ci_mine.reshape(2, ci_size)
+        orb_all = lax.all_to_all(orb_rows, DET_AXES, 0, 0, tiled=True)
+    else:
+        ci_pieces = ci_part.reshape(blocks, walk_count, ci_size).transpose(1, 0, 2)
+        orb_pieces = orb_part.reshape(walk_count, blocks, orb_size)
+        pieces = jnp.concatenate([orb_pieces, ci_pieces], axis=2).reshape(everyone, -1)
+        pieces = lax.all_to_all(pieces, ALL_AXES, 0, 0)
+        pieces = pieces.reshape(walk_count // 2, 2, blocks, -1)
+        orb_mine = jnp.sum(pieces[..., :orb_size], axis=(0, 1, 2))
+        ci_mine = jnp.sum(pieces[..., orb_size:], axis=(0, 2))
+        orb_all = lax.all_to_all(
+            jnp.broadcast_to(orb_mine[None], (blocks, orb_size)), DET_AXES, 0, 0
+        )
     ci_grad = lax.all_gather(ci_mine, "walk", axis=1).reshape(local)
     return (amp[:4, 0], ci_grad, orb_all.reshape(nocc // walk_count, nvirt))
 

time: 86.4 us -> 76.7 us (0.89)
  blocking collectives: 1.78 us -> 12 us
  waiting for transfers between devices: 21.6 us -> 12 us
  other arithmetic: 3.78 us -> 0 us
  Pallas kernels: 37.3 us -> 34.2 us
  starting transfers between devices: 14.9 us -> 12.4 us
    all_to_all x0 -> x1, blocking collectives: none -> 10.3 us  [per_device(): pieces = lax.all_to_all(orb_part, ALL_AXES, 0, 0)]
    all_to_all x3 -> x2, waiting for transfers between devices: 19.6 us -> 9.75 us  [the longest x1 6.12 us: per_device(): gathered = lax.all_to_all(payload, DET_AXES, 0, 0)]
    pallas_call x1, Pallas kernels: 14.6 us -> 9.83 us  [per_device(): pl.pallas_call(lambda *refs: gradient_kernel(float(walkers_total), *refs)...]
    all_to_all x3 -> x2, starting transfers between devices: 14.4 us -> 11.8 us  [the longest x1 8.31 us: per_device(): gathered = lax.all_to_all(payload, DET_AXES, 0, 0)]
    convert_element_type x3 -> x0, other arithmetic: 2.09 us -> none  [the longest x1 0.74 us: per_device(): (occ_list * 128 + virt_list).astype(jnp.float32)]
    pallas_call x1 -> x4, Pallas kernels: 22.7 us -> 24.4 us  [the longest x1 20.8 us: per_device(): pl.pallas_call(select_kernel, out_shape=(jax.ShapeDtypeStruct((ndet // LA...]
    concatenate x3 -> x0, other arithmetic: 1.52 us -> none  [the longest x1 0.76 us: per_device(): jnp.concatenate([(occ_list * 128 + virt_list).astype(jnp.float32), exc_ra...]
    broadcast_in_dim x2 -> x0, local copies, waits for them, and re-layouts: 1.35 us -> none  [the longest x1 0.72 us: per_device(): jnp.broadcast_to(payload[None], (blocks, 6, half))]
  transfers between devices with their start and end apart: 6 -> 5, of which waited for: 5 -> 4; matrix products, arithmetic and copies ran while one was open for 3% -> 3% of each run, Pallas kernels for 0% -> 1%
where the time goes in v3:
time: 76.7 us; the launch traced here: 76.2 us
  Pallas kernels  34.2 us (45%)
  starting transfers between devices  12.4 us (16%)
  waiting for transfers between devices  12 us (16%)
  blocking collectives  12 us (16%)
  local copies, waits for them, and re-layouts  4.88 us (6%)
    pallas_call x1, Pallas kernels, per_device(): pl.pallas_call(select_kernel, out_shape=(jax.ShapeDtypeStruct((ndet // LA...  20.8 us
    all_to_all x1, blocking collectives, per_device(): pieces = lax.all_to_all(orb_part, ALL_AXES, 0, 0)  10.3 us
    pallas_call x1, Pallas kernels, per_device(): pl.pallas_call(lambda *refs: gradient_kernel(float(walkers_total), *refs)...  9.83 us
    all_to_all x1, starting transfers between devices, per_device(): gathered = lax.all_to_all(payload, DET_AXES, 0, 0)  8.31 us
    all_to_all x1, waiting for transfers between devices, per_device(): gathered = lax.all_to_all(payload, DET_AXES, 0, 0)  6.12 us
    all_to_all x1, waiting for transfers between devices, per_device(): orb_all = lax.all_to_all(orb_rows, DET_AXES, 0, 0, tiled=True)  3.63 us
    unnamed x8, local copies, waits for them, and re-layouts  3.56 us
    all_to_all x1, starting transfers between devices, per_device(): orb_all = lax.all_to_all(orb_rows, DET_AXES, 0, 0, tiled=True)  3.5 us
  transfers between devices with their start and end apart: 5, of which 4 were waited for; matrix products, arithmetic and copies ran while one was open for 3% of the time, Pallas kernels for 1%

profile of v3, /device:TPU:0, one launch (start us, length us, event | category | flops | bytes accessed | tf_op | source)
XLA Modules:
  0.0 76.2 jit_solution(11012489871960020958)
XLA Ops:
  0.6 1.6 %shard_map.103 = (f32[16,6,512]{2,1,0:T(8,128)}, bf16[8,128]{1,0:T(8,128)(2,1)}) custom-call(s32[4,1024]{1,0:T(4,128)} %occ_ref.1, s32[4,1024]{1,0:T(4,128)} %virt_ref.2, s32[1,1024]{1,0:T(1,128)} %bitcast.12, f32[1,1024]{1,0:T(1,128)} %bitcast.13, bf16[4,128]{1,0:T(4,128)(2,1)} %rows_ref.1, s32[4]{0:T(128)} %moved_ref.1), custom_call_target="tpu_custom_call" | custom-call | tf_op jit(solution)/shard_map/pallas_call | solution.py:380
  2.2 8.3 %all-to-all-start = ((f32[16,6,512]{2,1,0:T(8,128)}), f32[16,6,512]{2,1,0:T(8,128)S(1)}, u32[]{:S(2)}, u32[]{:S(2)}) async-start(f32[16,6,512]{2,1,0:T(8,128)} %get-tuple-element.16), calls=%async_computation | async-start | bytes 524288 | tf_op jit(solution)/shard_map/all_to_all | solution.py:390
  10.5 0.1 collective-permute-start
  10.6 0.5 collective-permute-start.1
  11.1 1.0 %collective-permute-done.1.aux2_ref = bf16[8,128]{1,0:T(8,128)(2,1)S(1)} collective-permute-done((bf16[8,128]{1,0:T(8,128)(2,1)}, bf16[8,128]{1,0:T(8,128)(2,1)S(1)}, u32[]{:S(2)}, u32[]{:S(2)}) %collective-permute-start.1) | collective-permute-done | bytes 2080 | tf_op jit(solution)/shard_map/ppermute | solution.py:389
  12.1 0.0 collective-permute-done.inv2_ref
  12.1 0.0 copy-start
  12.1 0.9 %copy-done = bf16[4,128,128]{2,1,0:T(8,128)(2,1)S(1)} copy-done((bf16[4,128,128]{2,1,0:T(8,128)(2,1)S(1)}, bf16[4,128,128]{2,1,0:T(8,128)(2,1)}, u32[]{:S(2)}) %copy-start) | copy-done | bytes 131096
  13.0 0.0 copy-start.1
  13.0 0.8 copy-done.1
  13.8 0.0 copy-start.2
  13.8 0.7 copy-done.2
  14.5 0.5 shard_map.104
  15.0 6.1 %all-to-all-done.pay_ref.refs_3_ = f32[16,6,512]{2,1,0:T(8,128)S(1)} async-done(((f32[16,6,512]{2,1,0:T(8,128)}), f32[16,6,512]{2,1,0:T(8,128)S(1)}, u32[]{:S(2)}, u32[]{:S(2)}) %all-to-all-start) | async-done | bytes 196640 | tf_op jit(solution)/shard_map/all_to_all | solution.py:390
  21.1 20.8 %shard_map.105 = (bf16[64,4,2,16,128]{4,3,2,1,0:T(8,128)(2,1)S(1)}, f32[8,128]{1,0:T(8,128)S(1)}) custom-call(f8e4m3fn[1024,256]{1,0:T(32,128)(4,1)S(1)} %get-tuple-element.14.tab, f32[8,128]{1,0:T(8,128)S(1)} %get-tuple-element.15.back_ref, f32[16,6,512]{2,1,0:T(8,128)S(1)} %all-to-all-done.pay_ref.refs_3_), custom_call_target="tpu_custom_call" | custom-call | tf_op jit(solution)/shard_map/pallas_call | solution.py:403
  41.9 0.0 collective-permute-start.2
  41.9 1.2 %collective-permute-done.2.refs_1_ = f32[8,128]{1,0:T(8,128)S(1)} collective-permute-done((f32[8,128]{1,0:T(8,128)S(1)}, f32[8,128]{1,0:T(8,128)S(1)}, u32[]{:S(2)}, u32[]{:S(2)}) %collective-permute-start.2) | collective-permute-done | bytes 4128 | tf_op jit(solution)/shard_map/ppermute | solution.py:413
  43.1 9.8 %shard_map.106 = (f32[8,128]{1,0:T(8,128)S(1)}, f32[16,4,128]{2,1,0:T(4,128)}, f32[32,8,128]{2,1,0:T(8,128)S(1)}) custom-call(f32[8,128]{1,0:T(8,128)S(1)} %get-tuple-element.17.refs_0_, f32[8,128]{1,0:T(8,128)S(1)} %collective-permute-done.2.refs_1_, bf16[64,4,2,16,128]{4,3,2,1,0:T(8,128)(2,1)S(1)} %get-tuple-element.18.refs_2_, ...), custom_call_target="tpu_custom_call" | custom-call | tf_op jit(solution)/shard_map/pallas_call | solution.py:419
  52.9 10.3 %all_to_all.22.pieces_ref = f32[32,8,128]{2,1,0:T(8,128)} all-to-all(f32[32,8,128]{2,1,0:T(8,128)S(1)} %get-tuple-element.20), channel_id=1, replica_groups=mesh['walk'=2,'det'=4,'exc'=4] {'walk','det','exc'}, dimensions={0} | all-to-all | bytes 262144 | tf_op jit(solution)/shard_map/all_to_all | solution.py:433
  63.2 1.5 %shard_map.107 = (f32[64,128]{1,0:T(8,128)}, f32[4,128]{1,0:T(4,128)}) custom-call(f32[32,8,128]{2,1,0:T(8,128)} %all_to_all.22.pieces_ref), custom_call_target="tpu_custom_call" | custom-call | tf_op jit(solution)/shard_map/pallas_call | solution.py:434
  64.7 3.5 %all-to-all-start.2 = ((f32[16,4,128]{2,1,0:T(4,128)}), f32[16,4,128]{2,1,0:T(4,128)S(1)}, u32[]{:S(2)}, u32[]{:S(2)}) async-start(f32[16,4,128]{2,1,0:T(4,128)} %bitcast.9), calls=%async_computation.2 | async-start | bytes 65536 | tf_op jit(solution)/shard_map/all_to_all | solution.py:444
  68.2 0.6 slice_reduce_fusion
  68.8 0.7 all_gather_reshape.3
  69.5 1.8 %all_gather.3 = f32[2,2,256]{2,0,1:T(2,128)S(1)} all-gather(f32[2,1,256]{2,0,1:T(2,128)S(1)} %all_gather_reshape.3), channel_id=1, replica_groups=mesh['walk'=2,'det'=4,'exc'=4] {'walk'}, dimensions={1}, use_global_device_ids=true | all-gather | bytes 6144 | tf_op jit(solution)/shard_map/all_gather | solution.py:456
  71.3 0.6 copy.13
  71.9 3.6 %all-to-all-done.2 = f32[16,4,128]{2,1,0:T(4,128)S(1)} async-done(((f32[16,4,128]{2,1,0:T(4,128)}), f32[16,4,128]{2,1,0:T(4,128)S(1)}, u32[]{:S(2)}, u32[]{:S(2)}) %all-to-all-start.2) | async-done | bytes 32800 | tf_op jit(solution)/shard_map/all_to_all | solution.py:444
  75.5 0.6 copy.17
  (1 shorter events, 0.0 us)
Async XLA Ops:
  2.2 18.9 %all-to-all-start = ((f32[16,6,512]{2,1,0:T(8,128)}), f32[16,6,512]{2,1,0:T(8,128)S(1)}, u32[]{:S(2)}, u32[]{:S(2)}) async-start(f32[16,6,512]{2,1,0:T(8,128)} %get-tuple-element.16), calls=%async_computation | async-start | bytes 524288 | tf_op jit(solution)/shard_map/all_to_all | solution.py:390
  10.5 1.6 %collective-permute-start = (bf16[4,128,128]{2,1,0:T(8,128)(2,1)}, bf16[4,128,128]{2,1,0:T(8,128)(2,1)S(1)}, u32[]{:S(2)}, u32[]{:S(2)}) collective-permute-start(bf16[4,128,128]{2,1,0:T(8,128)(2,1)} %inv_ref.1), channel_id=1, source_target_pairs={{0,16},{16,0},{1,17},{17,1},{2,18},{18,2},{3,19},{19,3},{4,20},{20... | collective-permute-start | bytes 393224 | tf_op jit(solution)/shard_map/ppermute | solution.py:379
  10.6 1.5 %collective-permute-start.1 = (bf16[8,128]{1,0:T(8,128)(2,1)}, bf16[8,128]{1,0:T(8,128)(2,1)S(1)}, u32[]{:S(2)}, u32[]{:S(2)}) collective-permute-start(bf16[8,128]{1,0:T(8,128)(2,1)} %get-tuple-element.13.aux_ref), channel_id=1, source_target_pairs={{0,16},{16,0},{1,17},{17,1},{2,18},{18,2},{3,19},{19,3},{4,20},{20... | collective-permute-start | bytes 6152 | tf_op jit(solution)/shard_map/ppermute | solution.py:389
  12.1 0.9 %copy-start = (bf16[4,128,128]{2,1,0:T(8,128)(2,1)S(1)}, bf16[4,128,128]{2,1,0:T(8,128)(2,1)}, u32[]{:S(2)}) copy-start(bf16[4,128,128]{2,1,0:T(8,128)(2,1)} %inv_ref.1) | copy-start | bytes 393220
  13.0 0.8 copy-start.1
  13.8 0.7 copy-start.2
  41.9 1.2 %collective-permute-start.2 = (f32[8,128]{1,0:T(8,128)S(1)}, f32[8,128]{1,0:T(8,128)S(1)}, u32[]{:S(2)}, u32[]{:S(2)}) collective-permute-start(f32[8,128]{1,0:T(8,128)S(1)} %get-tuple-element.17.refs_0_), channel_id=1, source_target_pairs={{0,16},{16,0},{1,17},{17,1},{2,18},{18,2},{3,19},{19,3},{4,20},{20... | collective-permute-start | bytes 12296 | tf_op jit(solution)/shard_map/ppermute | solution.py:413
  64.7 10.8 %all-to-all-start.2 = ((f32[16,4,128]{2,1,0:T(4,128)}), f32[16,4,128]{2,1,0:T(4,128)S(1)}, u32[]{:S(2)}, u32[]{:S(2)}) async-start(f32[16,4,128]{2,1,0:T(4,128)} %bitcast.9), calls=%async_computation.2 | async-start | bytes 65536 | tf_op jit(solution)/shard_map/all_to_all | solution.py:444

commit v4 on v3

--- a/solution.py
+++ b/solution.py
@@ -143,54 +143,70 @@
             inv[w % 4], basis.astype(jnp.bfloat16), preferred_element_type=jnp.float32
         )
         table = table.astype(jnp.bfloat16).astype(jnp.float32)
-        wide[pl.ds(w, 128, stride=8), :] = table
+        wide[128 * w : 128 * w + 128, :] = table
         tops = jnp.where(sub == w, jnp.max(jnp.abs(table)), tops)
     scale, back = power_scale(tops)
     back_ref[...] = back
-    for k in range(16):
-        block = wide[64 * k : 64 * k + 64, :] * jnp.concatenate([scale] * 8, axis=0)
+    for w in range(8):
+        rows = slice(128 * w, 128 * w + 128)
+        block = wide[rows, :] * jnp.broadcast_to(scale[w : w + 1], (128, LANES))
         coarse = block.astype(jnp.float8_e4m3fn)
         rest = (block - coarse.astype(jnp.float32)) * FINE
-        tab[64 * k : 64 * k + 64, 0:128] = coarse
-        tab[64 * k : 64 * k + 64, 128:256] = rest.astype(jnp.float8_e4m3fn)
+        tab[rows, 0:128] = coarse
+        tab[rows, 128:256] = rest.astype(jnp.float8_e4m3fn)
+
+
+def cell_rows(ent_ref, lane_tile):
+    return [
+        [ent_ref[lane_tile, b, pl.ds(a, 8, stride=4), :] for a in range(4)] for b in range(4)
+    ]
 
 
 def select_kernel(tab, back_ref, pay_ref, ent_ref, amp_ref):
     nblk, _, width = pay_ref.shape
     tiles = nblk * width // TILE
-    back = back_ref[...]
+    parts = TILE // LANES
+    upper = lax.broadcasted_iota(jnp.int32, (8, LANES), 0) < 4
+    back = [
+        jnp.where(upper, rows8(back_ref[2 * q : 2 * q + 1]), rows8(back_ref[2 * q + 1 : 2 * q + 2]))
+        for q in range(4)
+    ]
 
     def forward(t, total):
         occ, virt, rank, coef = load_lists(pay_ref, t)
-        occ16 = [rows16(occ[a : a + 1]) for a in range(4)]
-        bits = [[(o & jnp.int16(bit)) != 0 for bit in (2, 4, 8, 16, 32, 64)] for o in occ16]
-        odd = [(rows8(occ[a : a + 1]) & 1) != 0 for a in range(4)]
-        entries = [[None] * 4 for _ in range(4)]
+        occ8 = jnp.concatenate([occ, occ], axis=0)
+        split = [occ8[:, h * LANES : (h + 1) * LANES] for h in range(parts)]
+        fine = [o & 7 for o in split]
+        bits = [[(o & bit) != 0 for bit in (8, 16, 32, 64)] for o in split]
         for b in range(4):
             hot = one_hot(rows16(virt[b : b + 1]), (1.0, 1.0 / FINE)).astype(jnp.float8_e4m3fn)
             cols = jnp.dot(tab[...], hot, preferred_element_type=jnp.float32)
-            cols = cols.astype(jnp.bfloat16)
-            parts = [cols[16 * k : 16 * k + 16] for k in range(64)]
-            for a in range(4):
-                level = parts
-                for step in range(6):
-                    level = [
-                        jnp.where(bits[a][step], level[2 * k + 1], level[2 * k])
-                        for k in range(len(level) // 2)
-                    ]
-                last = level[0].astype(jnp.float32)
-                last = jnp.where(odd[a], last[8:16], last[0:8])
-                entries[b][a] = [
-                    last[:, h * LANES : (h + 1) * LANES] * back for h in range(TILE // LANES)
-                ]
-        for h in range(TILE // LANES):
+            for h in range(parts):
+                lanes = slice(h * LANES, (h + 1) * LANES)
+                for q in range(4):
+                    pair = []
+                    for w in (2 * q, 2 * q + 1):
+                        level = [
+                            jnp.take_along_axis(
+                                cols[128 * w + 8 * k : 128 * w + 8 * k + 8, lanes],
+                                fine[h],
+                                axis=0,
+                                mode="promise_in_bounds",
+                            )
+                            for k in range(16)
+                        ]
+                        for step in range(4):
+                            level = [
+                                jnp.where(bits[h][step], level[2 * k + 1], level[2 * k])
+                                for k in range(len(level) // 2)
+                            ]
+                        pair.append(level[0])
+                    ent_ref[t * parts + h, b, 8 * q : 8 * q + 8, :] = (
+                        jnp.where(upper, pair[0], pair[1]) * back[q]
+                    )
+        for h in range(parts):
             lanes = slice(h * LANES, (h + 1) * LANES)
-            mine = [[entries[b][a][h] for a in range(4)] for b in range(4)]
-            for b in range(4):
-                for a in range(0, 4, 2):
-                    pair = jnp.concatenate([mine[b][a], mine[b][a + 1]], axis=0)
-                    ent_ref[t * (TILE // LANES) + h, b, a // 2] = pair.astype(jnp.bfloat16)
-            cells = masked_cells(mine, rows8(rank[:, lanes]))
+            cells = masked_cells(cell_rows(ent_ref, t * parts + h), rows8(rank[:, lanes]))
             ratio = determinant(
                 pair_products(cells[0], cells[1]), pair_products(cells[2], cells[3])
             )
@@ -256,13 +272,7 @@
             lanes = slice(h * LANES, (h + 1) * LANES)
             rank = rows8(rank_row[:, lanes])
             coef = rows8(coef_row[:, lanes])
-            entries = []
-            for b in range(4):
-                row = []
-                for a in range(0, 4, 2):
-                    pair = ent_ref[t * (TILE // LANES) + h, b, a // 2].astype(jnp.float32)
-                    row += [pair[0:8], pair[8:16]]
-                entries.append(row)
+            entries = cell_rows(ent_ref, t * (TILE // LANES) + h)
             cells = masked_cells(entries, rank)
             low = [x * weight for x in pair_products(cells[2], cells[3])]
             top = pair_products(cells[0], cells[1])
@@ -403,7 +413,7 @@
     entries, part = pl.pallas_call(
         select_kernel,
         out_shape=(
-            jax.ShapeDtypeStruct((ndet // LANES, 4, 2, 16, LANES), jnp.bfloat16),
+            jax.ShapeDtypeStruct((ndet // LANES, 4, 32, LANES), jnp.float32),
             jax.ShapeDtypeStruct((8, LANES), jnp.float32),
         ),
         in_specs=[vmem] * 3,

time: 76.7 us -> 69.3 us (0.904)
  Pallas kernels: 34.2 us -> 26.8 us
    pallas_call x1, Pallas kernels: 20.8 us -> 13.5 us  [per_device(): pl.pallas_call(select_kernel, out_shape=(jax.ShapeDtypeStruct((ndet // LA...]
where the time goes in v4:
time: 69.3 us; the launch traced here: 68.8 us
  Pallas kernels  26.8 us (39%)
  starting transfers between devices  12.4 us (18%)
  waiting for transfers between devices  12 us (17%)
  blocking collectives  12 us (17%)
  local copies, waits for them, and re-layouts  4.88 us (7%)
    pallas_call x1, Pallas kernels, per_device(): pl.pallas_call(select_kernel, out_shape=(jax.ShapeDtypeStruct((ndet // LA...  13.5 us
    all_to_all x1, blocking collectives, per_device(): pieces = lax.all_to_all(orb_part, ALL_AXES, 0, 0)  10.3 us
    pallas_call x1, Pallas kernels, per_device(): pl.pallas_call(lambda *refs: gradient_kernel(float(walkers_total), *refs)...  9.76 us
    all_to_all x1, starting transfers between devices, per_device(): gathered = lax.all_to_all(payload, DET_AXES, 0, 0)  8.31 us
    all_to_all x1, waiting for transfers between devices, per_device(): gathered = lax.all_to_all(payload, DET_AXES, 0, 0)  6.11 us
    all_to_all x1, waiting for transfers between devices, per_device(): orb_all = lax.all_to_all(orb_rows, DET_AXES, 0, 0, tiled=True)  3.63 us
    unnamed x8, local copies, waits for them, and re-layouts  3.56 us
    all_to_all x1, starting transfers between devices, per_device(): orb_all = lax.all_to_all(orb_rows, DET_AXES, 0, 0, tiled=True)  3.5 us
  transfers between devices with their start and end apart: 5, of which 4 were waited for; matrix products, arithmetic and copies ran while one was open for 3% of the time, Pallas kernels for 1%

profile of v4, /device:TPU:0, one launch (start us, length us, event | category | flops | bytes accessed | tf_op | source)
XLA Modules:
  0.0 68.8 jit_solution(12832393683063155777)
XLA Ops:
  0.6 1.6 %shard_map.103 = (f32[16,6,512]{2,1,0:T(8,128)}, bf16[8,128]{1,0:T(8,128)(2,1)}) custom-call(s32[4,1024]{1,0:T(4,128)} %occ_ref.1, s32[4,1024]{1,0:T(4,128)} %virt_ref.2, s32[1,1024]{1,0:T(1,128)} %bitcast.12, f32[1,1024]{1,0:T(1,128)} %bitcast.13, bf16[4,128]{1,0:T(4,128)(2,1)} %rows_ref.1, s32[4]{0:T(128)} %moved_ref.1), custom_call_target="tpu_custom_call" | custom-call | tf_op jit(solution)/shard_map/pallas_call | solution.py:390
  2.2 8.3 %all-to-all-start = ((f32[16,6,512]{2,1,0:T(8,128)}), f32[16,6,512]{2,1,0:T(8,128)S(1)}, u32[]{:S(2)}, u32[]{:S(2)}) async-start(f32[16,6,512]{2,1,0:T(8,128)} %get-tuple-element.16), calls=%async_computation | async-start | bytes 524288 | tf_op jit(solution)/shard_map/all_to_all | solution.py:400
  10.5 0.1 collective-permute-start
  10.6 0.5 collective-permute-start.1
  11.1 1.0 %collective-permute-done.1.aux2_ref = bf16[8,128]{1,0:T(8,128)(2,1)S(1)} collective-permute-done((bf16[8,128]{1,0:T(8,128)(2,1)}, bf16[8,128]{1,0:T(8,128)(2,1)S(1)}, u32[]{:S(2)}, u32[]{:S(2)}) %collective-permute-start.1) | collective-permute-done | bytes 2080 | tf_op jit(solution)/shard_map/ppermute | solution.py:399
  12.1 0.0 collective-permute-done.inv2_ref
  12.1 0.0 copy-start
  12.1 0.9 %copy-done = bf16[4,128,128]{2,1,0:T(8,128)(2,1)S(1)} copy-done((bf16[4,128,128]{2,1,0:T(8,128)(2,1)S(1)}, bf16[4,128,128]{2,1,0:T(8,128)(2,1)}, u32[]{:S(2)}) %copy-start) | copy-done | bytes 131096
  13.0 0.0 copy-start.1
  13.0 0.8 %copy-done.1 = bf16[128,128]{1,0:T(8,128)(2,1)S(1)} copy-done((bf16[128,128]{1,0:T(8,128)(2,1)S(1)}, bf16[128,128]{1,0:T(8,128)(2,1)}, u32[]{:S(2)}) %copy-start.1) | copy-done | bytes 32792
  13.8 0.0 copy-start.2
  13.8 0.7 copy-done.2
  14.5 0.5 shard_map.104
  15.0 6.1 %all-to-all-done.pay_ref.refs_3_ = f32[16,6,512]{2,1,0:T(8,128)S(1)} async-done(((f32[16,6,512]{2,1,0:T(8,128)}), f32[16,6,512]{2,1,0:T(8,128)S(1)}, u32[]{:S(2)}, u32[]{:S(2)}) %all-to-all-start) | async-done | bytes 196640 | tf_op jit(solution)/shard_map/all_to_all | solution.py:400
  21.1 13.5 %shard_map.105 = (f32[64,4,32,128]{3,2,1,0:T(8,128)S(1)}, f32[8,128]{1,0:T(8,128)S(1)}) custom-call(f8e4m3fn[1024,256]{1,0:T(32,128)(4,1)S(1)} %get-tuple-element.14.tab, f32[8,128]{1,0:T(8,128)S(1)} %get-tuple-element.15.back_ref, f32[16,6,512]{2,1,0:T(8,128)S(1)} %all-to-all-done.pay_ref.refs_3_), custom_call_target="tpu_custom_call" | custom-call | tf_op jit(solution)/shard_map/pallas_call | solution.py:413
  34.6 0.0 collective-permute-start.2
  34.6 1.2 %collective-permute-done.2.refs_1_ = f32[8,128]{1,0:T(8,128)S(1)} collective-permute-done((f32[8,128]{1,0:T(8,128)S(1)}, f32[8,128]{1,0:T(8,128)S(1)}, u32[]{:S(2)}, u32[]{:S(2)}) %collective-permute-start.2) | collective-permute-done | bytes 4128 | tf_op jit(solution)/shard_map/ppermute | solution.py:423
  35.7 9.8 %shard_map.106 = (f32[8,128]{1,0:T(8,128)S(1)}, f32[16,4,128]{2,1,0:T(4,128)}, f32[32,8,128]{2,1,0:T(8,128)S(1)}) custom-call(f32[8,128]{1,0:T(8,128)S(1)} %get-tuple-element.17.refs_0_, f32[8,128]{1,0:T(8,128)S(1)} %collective-permute-done.2.refs_1_, f32[64,4,32,128]{3,2,1,0:T(8,128)S(1)} %get-tuple-element.18.refs_2_, ...), custom_call_target="tpu_custom_call" | custom-call | tf_op jit(solution)/shard_map/pallas_call | solution.py:429
  45.5 10.3 %all_to_all.22.pieces_ref = f32[32,8,128]{2,1,0:T(8,128)} all-to-all(f32[32,8,128]{2,1,0:T(8,128)S(1)} %get-tuple-element.20), channel_id=1, replica_groups=mesh['walk'=2,'det'=4,'exc'=4] {'walk','det','exc'}, dimensions={0} | all-to-all | bytes 262144 | tf_op jit(solution)/shard_map/all_to_all | solution.py:443
  55.8 1.5 %shard_map.107 = (f32[64,128]{1,0:T(8,128)}, f32[4,128]{1,0:T(4,128)}) custom-call(f32[32,8,128]{2,1,0:T(8,128)} %all_to_all.22.pieces_ref), custom_call_target="tpu_custom_call" | custom-call | tf_op jit(solution)/shard_map/pallas_call | solution.py:444
  57.3 3.5 %all-to-all-start.2 = ((f32[16,4,128]{2,1,0:T(4,128)}), f32[16,4,128]{2,1,0:T(4,128)S(1)}, u32[]{:S(2)}, u32[]{:S(2)}) async-start(f32[16,4,128]{2,1,0:T(4,128)} %bitcast.9), calls=%async_computation.2 | async-start | bytes 65536 | tf_op jit(solution)/shard_map/all_to_all | solution.py:454
  60.8 0.6 slice_reduce_fusion
  61.5 0.7 %all_gather_reshape.3 = f32[2,1,256]{2,0,1:T(2,128)S(1)} reshape(f32[4,128]{1,0:T(4,128)} %get-tuple-element.21) | data formatting | bytes 4096 | tf_op jit(solution)/shard_map/all_gather;reshape | solution.py:466
  62.1 1.8 %all_gather.3 = f32[2,2,256]{2,0,1:T(2,128)S(1)} all-gather(f32[2,1,256]{2,0,1:T(2,128)S(1)} %all_gather_reshape.3), channel_id=1, replica_groups=mesh['walk'=2,'det'=4,'exc'=4] {'walk'}, dimensions={1}, use_global_device_ids=true | all-gather | bytes 6144 | tf_op jit(solution)/shard_map/all_gather | solution.py:466
  63.9 0.6 copy.13
  64.5 3.6 %all-to-all-done.2 = f32[16,4,128]{2,1,0:T(4,128)S(1)} async-done(((f32[16,4,128]{2,1,0:T(4,128)}), f32[16,4,128]{2,1,0:T(4,128)S(1)}, u32[]{:S(2)}, u32[]{:S(2)}) %all-to-all-start.2) | async-done | bytes 32800 | tf_op jit(solution)/shard_map/all_to_all | solution.py:454
  68.2 0.6 copy.17
  (1 shorter events, 0.0 us)
Async XLA Ops:
  2.2 18.9 %all-to-all-start = ((f32[16,6,512]{2,1,0:T(8,128)}), f32[16,6,512]{2,1,0:T(8,128)S(1)}, u32[]{:S(2)}, u32[]{:S(2)}) async-start(f32[16,6,512]{2,1,0:T(8,128)} %get-tuple-element.16), calls=%async_computation | async-start | bytes 524288 | tf_op jit(solution)/shard_map/all_to_all | solution.py:400
  10.5 1.6 %collective-permute-start = (bf16[4,128,128]{2,1,0:T(8,128)(2,1)}, bf16[4,128,128]{2,1,0:T(8,128)(2,1)S(1)}, u32[]{:S(2)}, u32[]{:S(2)}) collective-permute-start(bf16[4,128,128]{2,1,0:T(8,128)(2,1)} %inv_ref.1), channel_id=1, source_target_pairs={{0,16},{16,0},{1,17},{17,1},{2,18},{18,2},{3,19},{19,3},{4,20},{20... | collective-permute-start | bytes 393224 | tf_op jit(solution)/shard_map/ppermute | solution.py:389
  10.6 1.5 %collective-permute-start.1 = (bf16[8,128]{1,0:T(8,128)(2,1)}, bf16[8,128]{1,0:T(8,128)(2,1)S(1)}, u32[]{:S(2)}, u32[]{:S(2)}) collective-permute-start(bf16[8,128]{1,0:T(8,128)(2,1)} %get-tuple-element.13.aux_ref), channel_id=1, source_target_pairs={{0,16},{16,0},{1,17},{17,1},{2,18},{18,2},{3,19},{19,3},{4,20},{20... | collective-permute-start | bytes 6152 | tf_op jit(solution)/shard_map/ppermute | solution.py:399
  12.1 0.9 %copy-start = (bf16[4,128,128]{2,1,0:T(8,128)(2,1)S(1)}, bf16[4,128,128]{2,1,0:T(8,128)(2,1)}, u32[]{:S(2)}) copy-start(bf16[4,128,128]{2,1,0:T(8,128)(2,1)} %inv_ref.1) | copy-start | bytes 393220
  13.0 0.8 %copy-start.1 = (bf16[128,128]{1,0:T(8,128)(2,1)S(1)}, bf16[128,128]{1,0:T(8,128)(2,1)}, u32[]{:S(2)}) copy-start(bf16[128,128]{1,0:T(8,128)(2,1)} %virt_ref.3) | copy-start | bytes 98308
  13.8 0.7 copy-start.2
  34.6 1.2 %collective-permute-start.2 = (f32[8,128]{1,0:T(8,128)S(1)}, f32[8,128]{1,0:T(8,128)S(1)}, u32[]{:S(2)}, u32[]{:S(2)}) collective-permute-start(f32[8,128]{1,0:T(8,128)S(1)} %get-tuple-element.17.refs_0_), channel_id=1, source_target_pairs={{0,16},{16,0},{1,17},{17,1},{2,18},{18,2},{3,19},{19,3},{4,20},{20... | collective-permute-start | bytes 12296 | tf_op jit(solution)/shard_map/ppermute | solution.py:423
  57.3 10.8 %all-to-all-start.2 = ((f32[16,4,128]{2,1,0:T(4,128)}), f32[16,4,128]{2,1,0:T(4,128)S(1)}, u32[]{:S(2)}, u32[]{:S(2)}) async-start(f32[16,4,128]{2,1,0:T(4,128)} %bitcast.9), calls=%async_computation.2 | async-start | bytes 65536 | tf_op jit(solution)/shard_map/all_to_all | solution.py:454

commit v5 on v4

--- a/solution.py
+++ b/solution.py
@@ -59,6 +59,25 @@
         + top[3] * low[2]
         - top[4] * low[1]
         + top[5] * low[0]
+    )
+
+
+ROW_GATHER = lax.GatherDimensionNumbers(
+    offset_dims=(),
+    collapsed_slice_dims=(0,),
+    start_index_map=(0,),
+    operand_batching_dims=(1,),
+    start_indices_batching_dims=(1,),
+)
+
+
+def along_rows(x, index):
+    return lax.gather(
+        x,
+        index[..., None],
+        ROW_GATHER,
+        (1, 1),
+        mode=lax.GatherScatterMode.PROMISE_IN_BOUNDS,
     )
 
 
@@ -110,16 +129,18 @@
     return scale, back
 
 
-def payload_kernel(occ_ref, virt_ref, rank_ref, coef_ref, rows_ref, moved_ref, pay_ref, aux_ref):
+def payload_kernel(occ_ref, virt_ref, rank_ref, coef_ref, pay_ref):
     blocks, _, half = pay_ref.shape
     start = pl.multiple_of((lax.axis_index("walk") & 1) * half, LANES)
     lanes = pl.ds(start, half)
     codes = (occ_ref[:, lanes] * 128 + virt_ref[:, lanes]).astype(jnp.float32)
     rank = rank_ref[:, lanes].astype(jnp.float32)
-    coef = coef_ref[:, lanes]
-    rows = jnp.concatenate([codes, rank, coef], axis=0)
+    rows = jnp.concatenate([codes, rank, coef_ref[:, lanes]], axis=0)
     for k in range(blocks):
         pay_ref[k] = rows
+
+
+def aux_kernel(rows_ref, moved_ref, aux_ref):
     sub = lax.broadcasted_iota(jnp.int32, (4, LANES), 0)
     moved = jnp.zeros((4, LANES), jnp.float32)
     for w in range(4):
@@ -187,11 +208,8 @@
                     pair = []
                     for w in (2 * q, 2 * q + 1):
                         level = [
-                            jnp.take_along_axis(
-                                cols[128 * w + 8 * k : 128 * w + 8 * k + 8, lanes],
-                                fine[h],
-                                axis=0,
-                                mode="promise_in_bounds",
+                            along_rows(
+                                cols[128 * w + 8 * k : 128 * w + 8 * k + 8, lanes], fine[h]
                             )
                             for k in range(16)
                         ]
@@ -213,7 +231,7 @@
             total = total + ratio * rows8(coef[:, lanes])
         return total
 
-    total = lax.fori_loop(0, tiles, forward, jnp.zeros((8, LANES), jnp.float32), unroll=2)
+    total = lax.fori_loop(0, tiles, forward, jnp.zeros((8, LANES), jnp.float32), unroll=4)
     amp_ref[...] = jnp.broadcast_to(jnp.sum(total, axis=1, keepdims=True), (8, LANES))
 
 
@@ -241,11 +259,6 @@
     return items[0]
 
 
-def two_rows(x, y):
-    top = lax.broadcasted_iota(jnp.int32, (8, LANES), 0) < 4
-    return jnp.where(top, rows8(x), rows8(y))
-
-
 def gradient_kernel(
     walkers_total, part_ref, part2_ref, ent_ref, pay_ref, amp_ref, ci_ref, orb_ref, acc
 ):
@@ -254,20 +267,20 @@
     tiles = nblk * per_block
     packed = len(orb_ref.shape) == 3
     ci_rows = width // LANES * nblk // orb_ref.shape[0]
-    zero = jnp.zeros((16, TILE), jnp.bfloat16)
     amplitude = 1.0 + part_ref[...] + pltpu.roll(part2_ref[...], 4, 0)
     amp_ref[...] = amplitude
     weight = amplitude / (amplitude * amplitude + 1.0) / walkers_total
     sub = lax.broadcasted_iota(jnp.int32, (8, LANES), 0)
-    slot_b = sub & 3
+    slot = sub & 3
+    upper = sub < 4
     limits = [
-        jnp.maximum(slot_b, jnp.right_shift(sub, 2) + 2 * g).astype(jnp.float32) for g in range(2)
+        jnp.maximum(slot, jnp.right_shift(sub, 2) + 2 * g).astype(jnp.float32) for g in range(2)
     ]
+    others = [(sub & 4) + ((slot + shift) & 3) for shift in (1, 2, 3)]
 
     def backward(t, carry):
         occ, virt, rank_row, coef_row = load_lists(pay_ref, t)
-        occ16 = [rows16(occ[a : a + 1]) for a in range(4)]
-        wide = [[[] for _ in range(16)] for _ in range(2)]
+        left = [[[] for _ in range(16)] for _ in range(4)]
         for h in range(TILE // LANES):
             lanes = slice(h * LANES, (h + 1) * LANES)
             rank = rows8(rank_row[:, lanes])
@@ -277,13 +290,13 @@
             low = [x * weight for x in pair_products(cells[2], cells[3])]
             top = pair_products(cells[0], cells[1])
             summed = all_rows_sum(determinant(top, low))
-            block = t // per_block
+            source = t // per_block
             lane_tile = (t % per_block) * (TILE // LANES) + h
             if packed:
-                dest = lane_tile // (ci_rows) * nblk + block
+                dest = lane_tile // ci_rows * nblk + source
                 orb_ref[dest, pl.ds(4 + lane_tile % ci_rows, 1), :] = summed[0:1]
             else:
-                ci_ref[block, pl.ds(lane_tile, 1), :] = summed[0:1]
+                ci_ref[source, pl.ds(lane_tile, 1), :] = summed[0:1]
             top = [x * weight for x in top]
             d0, d1 = cofactor_rows(
                 cells[0], cells[1], (low[5], -low[4], low[3], low[2], -low[1], low[0])
@@ -291,45 +304,36 @@
             d2, d3 = cofactor_rows(
                 cells[2], cells[3], (top[5], -top[4], top[3], top[2], -top[1], top[0])
             )
-            plain = [
-                jnp.where(rank > limits[g], walker_sums(list(x + y)) * coef, 0.0)
-                for g, (x, y) in enumerate(((d0, d1), (d2, d3)))
-            ]
-            turned = [pltpu.roll(x, 4, 0) for x in plain]
-            occ_a = two_rows(occ[0:1, lanes], occ[1:2, lanes])
-            occ_b = two_rows(occ[2:3, lanes], occ[3:4, lanes])
-            turn_a = two_rows(occ[1:2, lanes], occ[0:1, lanes])
-            turn_b = two_rows(occ[3:4, lanes], occ[2:3, lanes])
-            straight = occ_a == occ_b
-            merged = [
-                plain[0]
-                + jnp.where(occ_a == turn_a, turned[0], 0.0)
-                + jnp.where(straight, plain[1], 0.0)
-                + jnp.where(occ_a == turn_b, turned[1], 0.0),
-                plain[1]
-                + jnp.where(occ_b == turn_b, turned[1], 0.0)
-                + jnp.where(straight, plain[0], 0.0)
-                + jnp.where(occ_b == turn_a, turned[0], 0.0),
-            ]
+            grads = [d0, d1, d2, d3]
+            occ_rows = jnp.concatenate([occ[:, lanes], occ[:, lanes]], axis=0)
+            same = [occ_rows == along_rows(occ_rows, other) for other in others]
+            sources = []
             for g in range(2):
-                high = merged[g].astype(jnp.bfloat16).astype(jnp.float32)
-                rest = merged[g] - high
-                for part, value in enumerate((high, rest)):
-                    for r in range(8):
-                        one = rows8(value[r : r + 1])
-                        wide[part][8 * g + r].append(
-                            jnp.concatenate([one, one], axis=0).astype(jnp.bfloat16)
+                items = [grads[a][b] for b in (2 * g, 2 * g + 1) for a in range(4)]
+                plain = jnp.where(rank > limits[g], walker_sums(items) * coef, 0.0)
+                merged = plain
+                for hit, other in zip(same, others):
+                    merged = merged + jnp.where(hit, along_rows(plain, other), 0.0)
+                high = merged.astype(jnp.bfloat16).astype(jnp.float32)
+                both = (high, merged - high)
+                sources.append([jnp.where(upper, x, 0.0) for x in both])
+                sources.append([jnp.where(upper, pltpu.roll(x, 4, 0), 0.0) for x in both])
+            slots = [rows8(occ[a : a + 1, lanes]) for a in range(4)]
+            for k in range(8):
+                index = []
+                for block in (2 * k, 2 * k + 1):
+                    place = sub + 8 * block
+                    found = jnp.full((8, LANES), 4, jnp.int32)
+                    for a in range(4):
+                        found = jnp.where(slots[a] == place, a, found)
+                    index.append(found)
+                for b in range(4):
+                    for part in range(2):
+                        rows = [along_rows(sources[b][part], x) for x in index]
+                        left[b][8 * part + k].append(
+                            jnp.concatenate(rows, axis=0).astype(jnp.bfloat16)
                         )
-        wide = [[jnp.concatenate(x, axis=1) for x in rows] for rows in wide]
-        left = [[None] * 16 for _ in range(4)]
-        for k in range(8):
-            hits = [occ16[a] == iota16() + jnp.int16(16 * k) for a in range(4)]
-            for part in range(2):
-                for b in range(4):
-                    value = zero
-                    for a in range(4):
-                        value = jnp.where(hits[a], wide[part][4 * a + b], value)
-                    left[b][part * 8 + k] = value
+        left = [[jnp.concatenate(x, axis=1) for x in left[b]] for b in range(4)]
         left = jnp.concatenate([jnp.concatenate(left[b], axis=0) for b in range(4)], axis=1)
         right = jnp.concatenate(
             [one_hot(rows16(virt[b : b + 1]), (1.0,)) for b in range(4)], axis=1
@@ -342,7 +346,7 @@
     acc[...] = jnp.zeros_like(acc)
     if packed:
         orb_ref[...] = jnp.zeros_like(orb_ref)
-    lax.fori_loop(0, tiles, backward, 0, unroll=4)
+    lax.fori_loop(0, tiles, backward, 0, unroll=8)
     total = acc[0:128, :] + acc[128:256, :]
     if packed:
         for dest in range(orb_ref.shape[0]):
@@ -387,15 +391,18 @@
     params = pltpu.CompilerParams(vmem_limit_bytes=32 << 20)
 
     inverse2 = lax.ppermute(inverse, "walk", partner)
-    payload, aux = pl.pallas_call(
+    payload = pl.pallas_call(
         payload_kernel,
-        out_shape=(
-            jax.ShapeDtypeStruct((blocks, 6, half), jnp.float32),
-            jax.ShapeDtypeStruct((8, LANES), jnp.bfloat16),
-        ),
-        in_specs=[vmem] * 5 + [smem],
-        out_specs=(vmem, vmem),
-    )(occ_list, virt_list, exc_rank[None], coefficient[None], new_rows, moved_electron)
+        out_shape=jax.ShapeDtypeStruct((blocks, 6, half), jnp.float32),
+        in_specs=[vmem] * 4,
+        out_specs=vmem,
+    )(occ_list, virt_list, exc_rank[None], coefficient[None])
+    aux = pl.pallas_call(
+        aux_kernel,
+        out_shape=jax.ShapeDtypeStruct((8, LANES), jnp.bfloat16),
+        in_specs=[vmem, smem],
+        out_specs=vmem,
+    )(new_rows, moved_electron)
     aux2 = lax.ppermute(aux, "walk", partner)
     gathered = lax.all_to_all(payload, DET_AXES, 0, 0)
 

time: 69.3 us -> 67.5 us (0.974)
  waiting for transfers between devices: 12 us -> 10.6 us
    all_to_all x1, waiting for transfers between devices: 6.11 us -> 4.75 us  [per_device(): gathered = lax.all_to_all(payload, DET_AXES, 0, 0)]
    pallas_call x1, Pallas kernels: 9.76 us -> 8.43 us  [per_device(): pl.pallas_call(lambda *refs: gradient_kernel(float(walkers_total), *refs)...]
    pallas_call x1 -> x2, Pallas kernels: 1.55 us -> 2.86 us  [the longest x1 1.48 us: per_device(): pl.pallas_call(payload_kernel, out_shape=jax.ShapeDtypeStruct((blocks, 6,...]
  transfers between devices with their start and end apart: 5 -> 5, of which waited for: 4 -> 4; matrix products, arithmetic and copies ran while one was open for 3% -> 3% of each run, Pallas kernels for 1% -> 3%
where the time goes in v5:
time: 67.5 us; the launch traced here: 67 us
  Pallas kernels  26.5 us (39%)
  starting transfers between devices  12.4 us (18%)
  blocking collectives  12 us (18%)
  waiting for transfers between devices  10.6 us (16%)
  local copies, waits for them, and re-layouts  4.88 us (7%)
  between operations  0.68 us (1%)
    pallas_call x1, Pallas kernels, per_device(): pl.pallas_call(select_kernel, out_shape=(jax.ShapeDtypeStruct((ndet // LA...  13.1 us
    all_to_all x1, blocking collectives, per_device(): pieces = lax.all_to_all(orb_part, ALL_AXES, 0, 0)  10.3 us
    pallas_call x1, Pallas kernels, per_device(): pl.pallas_call(lambda *refs: gradient_kernel(float(walkers_total), *refs)...  8.43 us
    all_to_all x1, starting transfers between devices, per_device(): gathered = lax.all_to_all(payload, DET_AXES, 0, 0)  8.31 us
    all_to_all x1, waiting for transfers between devices, per_device(): gathered = lax.all_to_all(payload, DET_AXES, 0, 0)  4.75 us
    all_to_all x1, waiting for transfers between devices, per_device(): orb_all = lax.all_to_all(orb_rows, DET_AXES, 0, 0, tiled=True)  3.63 us
    unnamed x8, local copies, waits for them, and re-layouts  3.56 us
    all_to_all x1, starting transfers between devices, per_device(): orb_all = lax.all_to_all(orb_rows, DET_AXES, 0, 0, tiled=True)  3.5 us
  transfers between devices with their start and end apart: 5, of which 4 were waited for; matrix products, arithmetic and copies ran while one was open for 3% of the time, Pallas kernels for 3%

profile of v5, /device:TPU:0, one launch (start us, length us, event | category | flops | bytes accessed | tf_op | source)
XLA Modules:
  0.0 67.0 jit_solution(12832022120630730140)
XLA Ops:
  0.6 1.5 %shard_map.105 = f32[16,6,512]{2,1,0:T(8,128)} custom-call(s32[4,1024]{1,0:T(4,128)} %occ_ref.1, s32[4,1024]{1,0:T(4,128)} %virt_ref.3, s32[1,1024]{1,0:T(1,128)} %bitcast.11, f32[1,1024]{1,0:T(1,128)} %bitcast.12), custom_call_target="tpu_custom_call" | custom-call | tf_op jit(solution)/shard_map/pallas_call | solution.py:394
  2.1 8.3 %all-to-all-start = ((f32[16,6,512]{2,1,0:T(8,128)}), f32[16,6,512]{2,1,0:T(8,128)S(1)}, u32[]{:S(2)}, u32[]{:S(2)}) async-start(f32[16,6,512]{2,1,0:T(8,128)} %shard_map.105), calls=%async_computation | async-start | bytes 524288 | tf_op jit(solution)/shard_map/all_to_all | solution.py:407
  10.4 0.1 collective-permute-start
  10.5 1.4 %shard_map.103.aux_ref = bf16[8,128]{1,0:T(8,128)(2,1)} custom-call(bf16[4,128]{1,0:T(4,128)(2,1)} %rows_ref.1, s32[4]{0:T(128)} %moved_ref.1), custom_call_target="tpu_custom_call" | custom-call | tf_op jit(solution)/shard_map/pallas_call | solution.py:400
  11.9 0.5 collective-permute-start.1
  12.4 1.0 %collective-permute-done.1.aux2_ref = bf16[8,128]{1,0:T(8,128)(2,1)S(1)} collective-permute-done((bf16[8,128]{1,0:T(8,128)(2,1)}, bf16[8,128]{1,0:T(8,128)(2,1)S(1)}, u32[]{:S(2)}, u32[]{:S(2)}) %collective-permute-start.1) | collective-permute-done | bytes 2080 | tf_op jit(solution)/shard_map/ppermute | solution.py:406
  13.4 0.0 collective-permute-done.inv2_ref
  13.4 0.0 copy-start
  13.4 0.9 %copy-done = bf16[4,128,128]{2,1,0:T(8,128)(2,1)S(1)} copy-done((bf16[4,128,128]{2,1,0:T(8,128)(2,1)S(1)}, bf16[4,128,128]{2,1,0:T(8,128)(2,1)}, u32[]{:S(2)}) %copy-start) | copy-done | bytes 131096
  14.3 0.0 copy-start.1
  14.3 0.8 %copy-done.1 = bf16[128,128]{1,0:T(8,128)(2,1)S(1)} copy-done((bf16[128,128]{1,0:T(8,128)(2,1)S(1)}, bf16[128,128]{1,0:T(8,128)(2,1)}, u32[]{:S(2)}) %copy-start.1) | copy-done | bytes 32792
  15.1 0.0 copy-start.2
  15.1 0.7 %copy-done.2 = bf16[8,128]{1,0:T(8,128)(2,1)S(1)} copy-done((bf16[8,128]{1,0:T(8,128)(2,1)S(1)}, bf16[8,128]{1,0:T(8,128)(2,1)}, u32[]{:S(2)}) %copy-start.2) | copy-done | bytes 2072
  15.8 0.5 shard_map.104
  16.3 4.7 %all-to-all-done.pay_ref.refs_3_ = f32[16,6,512]{2,1,0:T(8,128)S(1)} async-done(((f32[16,6,512]{2,1,0:T(8,128)}), f32[16,6,512]{2,1,0:T(8,128)S(1)}, u32[]{:S(2)}, u32[]{:S(2)}) %all-to-all-start) | async-done | bytes 196640 | tf_op jit(solution)/shard_map/all_to_all | solution.py:407
  21.0 13.1 %shard_map.106 = (f32[64,4,32,128]{3,2,1,0:T(8,128)S(1)}, f32[8,128]{1,0:T(8,128)S(1)}) custom-call(f8e4m3fn[1024,256]{1,0:T(32,128)(4,1)S(1)} %get-tuple-element.11.tab, f32[8,128]{1,0:T(8,128)S(1)} %get-tuple-element.12.back_ref, f32[16,6,512]{2,1,0:T(8,128)S(1)} %all-to-all-done.pay_ref.refs_3_), custom_call_target="tpu_custom_call" | custom-call | tf_op jit(solution)/shard_map/pallas_call | solution.py:420
  34.1 0.0 collective-permute-start.2
  34.2 1.2 %collective-permute-done.2.refs_1_ = f32[8,128]{1,0:T(8,128)S(1)} collective-permute-done((f32[8,128]{1,0:T(8,128)S(1)}, f32[8,128]{1,0:T(8,128)S(1)}, u32[]{:S(2)}, u32[]{:S(2)}) %collective-permute-start.2) | collective-permute-done | bytes 4128 | tf_op jit(solution)/shard_map/ppermute | solution.py:430
  35.3 8.4 %shard_map.107 = (f32[8,128]{1,0:T(8,128)S(1)}, f32[16,4,128]{2,1,0:T(4,128)}, f32[32,8,128]{2,1,0:T(8,128)S(1)}) custom-call(f32[8,128]{1,0:T(8,128)S(1)} %get-tuple-element.13.refs_0_, f32[8,128]{1,0:T(8,128)S(1)} %collective-permute-done.2.refs_1_, f32[64,4,32,128]{3,2,1,0:T(8,128)S(1)} %get-tuple-element.14.refs_2_, ...), custom_call_target="tpu_custom_call" | custom-call | tf_op jit(solution)/shard_map/pallas_call | solution.py:436
  43.7 10.3 %all_to_all.22.pieces_ref = f32[32,8,128]{2,1,0:T(8,128)} all-to-all(f32[32,8,128]{2,1,0:T(8,128)S(1)} %get-tuple-element.16), channel_id=1, replica_groups=mesh['walk'=2,'det'=4,'exc'=4] {'walk','det','exc'}, dimensions={0} | all-to-all | bytes 262144 | tf_op jit(solution)/shard_map/all_to_all | solution.py:450
  54.0 1.5 %shard_map.108 = (f32[64,128]{1,0:T(8,128)}, f32[4,128]{1,0:T(4,128)}) custom-call(f32[32,8,128]{2,1,0:T(8,128)} %all_to_all.22.pieces_ref), custom_call_target="tpu_custom_call" | custom-call | tf_op jit(solution)/shard_map/pallas_call | solution.py:451
  55.6 3.5 %all-to-all-start.2 = ((f32[16,4,128]{2,1,0:T(4,128)}), f32[16,4,128]{2,1,0:T(4,128)S(1)}, u32[]{:S(2)}, u32[]{:S(2)}) async-start(f32[16,4,128]{2,1,0:T(4,128)} %bitcast.9), calls=%async_computation.2 | async-start | bytes 65536 | tf_op jit(solution)/shard_map/all_to_all | solution.py:461
  59.1 0.6 slice_reduce_fusion
  59.7 0.7 %all_gather_reshape.3 = f32[2,1,256]{2,0,1:T(2,128)S(1)} reshape(f32[4,128]{1,0:T(4,128)} %get-tuple-element.17) | data formatting | bytes 4096 | tf_op jit(solution)/shard_map/all_gather;reshape | solution.py:473
  60.4 1.8 %all_gather.3 = f32[2,2,256]{2,0,1:T(2,128)S(1)} all-gather(f32[2,1,256]{2,0,1:T(2,128)S(1)} %all_gather_reshape.3), channel_id=1, replica_groups=mesh['walk'=2,'det'=4,'exc'=4] {'walk'}, dimensions={1}, use_global_device_ids=true | all-gather | bytes 6144 | tf_op jit(solution)/shard_map/all_gather | solution.py:473
  62.2 0.6 copy.13
  62.8 3.6 %all-to-all-done.2 = f32[16,4,128]{2,1,0:T(4,128)S(1)} async-done(((f32[16,4,128]{2,1,0:T(4,128)}), f32[16,4,128]{2,1,0:T(4,128)S(1)}, u32[]{:S(2)}, u32[]{:S(2)}) %all-to-all-start.2) | async-done | bytes 32800 | tf_op jit(solution)/shard_map/all_to_all | solution.py:461
  66.4 0.6 copy.17
  (1 shorter events, 0.0 us)
Async XLA Ops:
  2.1 18.9 %all-to-all-start = ((f32[16,6,512]{2,1,0:T(8,128)}), f32[16,6,512]{2,1,0:T(8,128)S(1)}, u32[]{:S(2)}, u32[]{:S(2)}) async-start(f32[16,6,512]{2,1,0:T(8,128)} %shard_map.105), calls=%async_computation | async-start | bytes 524288 | tf_op jit(solution)/shard_map/all_to_all | solution.py:407
  10.4 3.0 %collective-permute-start = (bf16[4,128,128]{2,1,0:T(8,128)(2,1)}, bf16[4,128,128]{2,1,0:T(8,128)(2,1)S(1)}, u32[]{:S(2)}, u32[]{:S(2)}) collective-permute-start(bf16[4,128,128]{2,1,0:T(8,128)(2,1)} %inv_ref.1), channel_id=1, source_target_pairs={{0,16},{16,0},{1,17},{17,1},{2,18},{18,2},{3,19},{19,3},{4,20},{20... | collective-permute-start | bytes 393224 | tf_op jit(solution)/shard_map/ppermute | solution.py:393
  11.9 1.5 %collective-permute-start.1 = (bf16[8,128]{1,0:T(8,128)(2,1)}, bf16[8,128]{1,0:T(8,128)(2,1)S(1)}, u32[]{:S(2)}, u32[]{:S(2)}) collective-permute-start(bf16[8,128]{1,0:T(8,128)(2,1)} %shard_map.103.aux_ref), channel_id=1, source_target_pairs={{0,16},{16,0},{1,17},{17,1},{2,18},{18,2},{3,19},{19,3},{4,20},{20... | collective-permute-start | bytes 6152 | tf_op jit(solution)/shard_map/ppermute | solution.py:406
  13.4 0.9 %copy-start = (bf16[4,128,128]{2,1,0:T(8,128)(2,1)S(1)}, bf16[4,128,128]{2,1,0:T(8,128)(2,1)}, u32[]{:S(2)}) copy-start(bf16[4,128,128]{2,1,0:T(8,128)(2,1)} %inv_ref.1) | copy-start | bytes 393220
  14.3 0.8 %copy-start.1 = (bf16[128,128]{1,0:T(8,128)(2,1)S(1)}, bf16[128,128]{1,0:T(8,128)(2,1)}, u32[]{:S(2)}) copy-start(bf16[128,128]{1,0:T(8,128)(2,1)} %virt_ref.2) | copy-start | bytes 98308
  15.1 0.7 %copy-start.2 = (bf16[8,128]{1,0:T(8,128)(2,1)S(1)}, bf16[8,128]{1,0:T(8,128)(2,1)}, u32[]{:S(2)}) copy-start(bf16[8,128]{1,0:T(8,128)(2,1)} %shard_map.103.aux_ref) | copy-start | bytes 6148
  34.1 1.2 %collective-permute-start.2 = (f32[8,128]{1,0:T(8,128)S(1)}, f32[8,128]{1,0:T(8,128)S(1)}, u32[]{:S(2)}, u32[]{:S(2)}) collective-permute-start(f32[8,128]{1,0:T(8,128)S(1)} %get-tuple-element.13.refs_0_), channel_id=1, source_target_pairs={{0,16},{16,0},{1,17},{17,1},{2,18},{18,2},{3,19},{19,3},{4,20},{20... | collective-permute-start | bytes 12296 | tf_op jit(solution)/shard_map/ppermute | solution.py:430
  55.6 10.8 %all-to-all-start.2 = ((f32[16,4,128]{2,1,0:T(4,128)}), f32[16,4,128]{2,1,0:T(4,128)S(1)}, u32[]{:S(2)}, u32[]{:S(2)}) async-start(f32[16,4,128]{2,1,0:T(4,128)} %bitcast.9), calls=%async_computation.2 | async-start | bytes 65536 | tf_op jit(solution)/shard_map/all_to_all | solution.py:461

commit v6 on v5

--- a/solution.py
+++ b/solution.py
@@ -102,6 +102,17 @@
         for value in values
         for hit in hits
     ]
+    return jnp.concatenate(parts, axis=0)
+
+
+def one_hot8(row, values):
+    kind = jnp.float8_e4m3fn
+    shape = (32, row.shape[1])
+    v8 = jnp.broadcast_to(row, shape).astype(jnp.int8)
+    base = lax.broadcasted_iota(jnp.int32, shape, 0)
+    hits = [v8 == (base + 32 * k).astype(jnp.int8) for k in range(4)]
+    zero = jnp.zeros(shape, kind)
+    parts = [jnp.where(hit, jnp.full(shape, x, kind), zero) for x in values for hit in hits]
     return jnp.concatenate(parts, axis=0)
 
 
@@ -140,41 +151,38 @@
         pay_ref[k] = rows
 
 
-def aux_kernel(rows_ref, moved_ref, aux_ref):
-    sub = lax.broadcasted_iota(jnp.int32, (4, LANES), 0)
-    moved = jnp.zeros((4, LANES), jnp.float32)
+def table_kernel(moved_ref, inv_ref, rows_ref, virt_ref, tab):
+    rows_of = lax.broadcasted_iota(jnp.int32, (128, LANES), 0)
+    fresh = rows_ref[...].astype(jnp.float32)
     for w in range(4):
-        moved = jnp.where(sub == w, moved_ref[w].astype(jnp.float32), moved)
-    aux_ref[...] = jnp.concatenate(
-        [rows_ref[...].astype(jnp.float32), moved], axis=0
-    ).astype(jnp.bfloat16)
-
-
-def table_kernel(inv_ref, inv2_ref, aux_ref, aux2_ref, virt_ref, tab, back_ref, wide):
+        basis = jnp.where(
+            rows_of == moved_ref[w],
+            jnp.broadcast_to(fresh[w : w + 1], (128, LANES)),
+            virt_ref[...].astype(jnp.float32),
+        )
+        tab[w] = jnp.dot(
+            inv_ref[w], basis.astype(jnp.bfloat16), preferred_element_type=jnp.float32
+        ).astype(jnp.bfloat16)
+
+
+def code_kernel(mine_ref, theirs_ref, code_ref, back_ref):
     sub = lax.broadcasted_iota(jnp.int32, (8, LANES), 0)
-    rows_of = lax.broadcasted_iota(jnp.int32, (128, LANES), 0).astype(jnp.float32)
+    tables = [
+        (mine_ref if w < 4 else theirs_ref)[w % 4].astype(jnp.float32) for w in range(8)
+    ]
     tops = jnp.zeros((8, LANES), jnp.float32)
     for w in range(8):
-        inv, aux = (inv_ref, aux_ref) if w < 4 else (inv2_ref, aux2_ref)
-        aux_rows = aux[...].astype(jnp.float32)
-        fresh = jnp.broadcast_to(aux_rows[w % 4 : w % 4 + 1], (128, LANES))
-        moved = jnp.broadcast_to(aux_rows[w % 4 + 4 : w % 4 + 5], (128, LANES))
-        basis = jnp.where(rows_of == moved, fresh, virt_ref[...].astype(jnp.float32))
-        table = jnp.dot(
-            inv[w % 4], basis.astype(jnp.bfloat16), preferred_element_type=jnp.float32
-        )
-        table = table.astype(jnp.bfloat16).astype(jnp.float32)
-        wide[128 * w : 128 * w + 128, :] = table
-        tops = jnp.where(sub == w, jnp.max(jnp.abs(table)), tops)
+        top = jnp.max(jnp.max(jnp.abs(tables[w]), axis=0, keepdims=True), axis=1, keepdims=True)
+        tops = jnp.where(sub == w, jnp.broadcast_to(top, (8, LANES)), tops)
     scale, back = power_scale(tops)
     back_ref[...] = back
     for w in range(8):
         rows = slice(128 * w, 128 * w + 128)
-        block = wide[rows, :] * jnp.broadcast_to(scale[w : w + 1], (128, LANES))
+        block = tables[w] * jnp.broadcast_to(scale[w : w + 1], (128, LANES))
         coarse = block.astype(jnp.float8_e4m3fn)
         rest = (block - coarse.astype(jnp.float32)) * FINE
-        tab[rows, 0:128] = coarse
-        tab[rows, 128:256] = rest.astype(jnp.float8_e4m3fn)
+        code_ref[rows, 0:128] = coarse
+        code_ref[rows, 128:256] = rest.astype(jnp.float8_e4m3fn)
 
 
 def cell_rows(ent_ref, lane_tile):
@@ -200,7 +208,7 @@
         fine = [o & 7 for o in split]
         bits = [[(o & bit) != 0 for bit in (8, 16, 32, 64)] for o in split]
         for b in range(4):
-            hot = one_hot(rows16(virt[b : b + 1]), (1.0, 1.0 / FINE)).astype(jnp.float8_e4m3fn)
+            hot = one_hot8(virt[b : b + 1], (1.0, 1.0 / FINE))
             cols = jnp.dot(tab[...], hot, preferred_element_type=jnp.float32)
             for h in range(parts):
                 lanes = slice(h * LANES, (h + 1) * LANES)
@@ -390,33 +398,30 @@
     smem = pl.BlockSpec(memory_space=pltpu.SMEM)
     params = pltpu.CompilerParams(vmem_limit_bytes=32 << 20)
 
-    inverse2 = lax.ppermute(inverse, "walk", partner)
     payload = pl.pallas_call(
         payload_kernel,
         out_shape=jax.ShapeDtypeStruct((blocks, 6, half), jnp.float32),
         in_specs=[vmem] * 4,
         out_specs=vmem,
     )(occ_list, virt_list, exc_rank[None], coefficient[None])
-    aux = pl.pallas_call(
-        aux_kernel,
-        out_shape=jax.ShapeDtypeStruct((8, LANES), jnp.bfloat16),
-        in_specs=[vmem, smem],
+    gathered = lax.all_to_all(payload, DET_AXES, 0, 0)
+    mine = pl.pallas_call(
+        table_kernel,
+        out_shape=jax.ShapeDtypeStruct(inverse.shape, jnp.bfloat16),
+        in_specs=[smem] + [vmem] * 3,
         out_specs=vmem,
-    )(new_rows, moved_electron)
-    aux2 = lax.ppermute(aux, "walk", partner)
-    gathered = lax.all_to_all(payload, DET_AXES, 0, 0)
-
+    )(moved_electron, inverse, new_rows, virt_ref)
+    theirs = lax.ppermute(mine, "walk", partner)
     table, back = pl.pallas_call(
-        table_kernel,
+        code_kernel,
         out_shape=(
             jax.ShapeDtypeStruct((1024, 2 * LANES), jnp.float8_e4m3fn),
             jax.ShapeDtypeStruct((8, LANES), jnp.float32),
         ),
-        in_specs=[vmem] * 5,
+        in_specs=[vmem] * 2,
         out_specs=(vmem, vmem),
-        scratch_shapes=[pltpu.VMEM((1024, LANES), jnp.float32)],
         compiler_params=params,
-    )(inverse, inverse2, aux, aux2, virt_ref)
+    )(mine, theirs)
     entries, part = pl.pallas_call(
         select_kernel,
         out_shape=(

time: 67.5 us -> 67.2 us (level)
  waiting for transfers between devices: 10.6 us -> 12.5 us
  local copies, waits for them, and re-layouts: 4.88 us -> 3.44 us
    unnamed x8 -> x4, local copies, waits for them, and re-layouts: 3.56 us -> 2.12 us
    all_to_all x1, waiting for transfers between devices: 4.75 us -> 6.1 us  [per_device(): gathered = lax.all_to_all(payload, DET_AXES, 0, 0)]
    ppermute x2 -> x1, waiting for transfers between devices: 1.03 us -> 1.56 us  [per_device(): theirs = lax.ppermute(mine, 'walk', partner)]
  transfers between devices with their start and end apart: 5 -> 4, of which waited for: 4 -> 4; matrix products, arithmetic and copies ran while one was open for 3% -> 3% of each run, Pallas kernels for 3% -> 3%
where the time goes in v6:
time: 67.2 us; the launch traced here: 66.7 us
  Pallas kernels  26.3 us (39%)
  waiting for transfers between devices  12.5 us (19%)
  blocking collectives  12.1 us (18%)
  starting transfers between devices  11.8 us (18%)
  local copies, waits for them, and re-layouts  3.44 us (5%)
    pallas_call x1, Pallas kernels, per_device(): pl.pallas_call(select_kernel, out_shape=(jax.ShapeDtypeStruct((ndet // LA...  12.9 us
    all_to_all x1, blocking collectives, per_device(): pieces = lax.all_to_all(orb_part, ALL_AXES, 0, 0)  10.3 us
    pallas_call x1, Pallas kernels, per_device(): pl.pallas_call(lambda *refs: gradient_kernel(float(walkers_total), *refs)...  8.43 us
    all_to_all x1, starting transfers between devices, per_device(): gathered = lax.all_to_all(payload, DET_AXES, 0, 0)  8.31 us
    all_to_all x1, waiting for transfers between devices, per_device(): gathered = lax.all_to_all(payload, DET_AXES, 0, 0)  6.1 us
    all_to_all x1, waiting for transfers between devices, per_device(): orb_all = lax.all_to_all(orb_rows, DET_AXES, 0, 0, tiled=True)  3.63 us
    all_to_all x1, starting transfers between devices, per_device(): orb_all = lax.all_to_all(orb_rows, DET_AXES, 0, 0, tiled=True)  3.5 us
    unnamed x4, local copies, waits for them, and re-layouts  2.12 us
  transfers between devices with their start and end apart: 4, of which 4 were waited for; matrix products, arithmetic and copies ran while one was open for 3% of the time, Pallas kernels for 3%

profile of v6, /device:TPU:0, one launch (start us, length us, event | category | flops | bytes accessed | tf_op | source)
XLA Modules:
  0.0 66.7 jit_solution(3499175909924992813)
XLA Ops:
  0.6 1.5 %shard_map.105 = f32[16,6,512]{2,1,0:T(8,128)} custom-call(s32[4,1024]{1,0:T(4,128)} %occ_ref.1, s32[4,1024]{1,0:T(4,128)} %virt_ref.3, s32[1,1024]{1,0:T(1,128)} %bitcast.11, f32[1,1024]{1,0:T(1,128)} %bitcast.12), custom_call_target="tpu_custom_call" | custom-call | tf_op jit(solution)/shard_map/pallas_call | solution.py:401
  2.1 8.3 %all-to-all-start = ((f32[16,6,512]{2,1,0:T(8,128)}), f32[16,6,512]{2,1,0:T(8,128)S(1)}, u32[]{:S(2)}, u32[]{:S(2)}) async-start(f32[16,6,512]{2,1,0:T(8,128)} %shard_map.105), calls=%async_computation | async-start | bytes 524288 | tf_op jit(solution)/shard_map/all_to_all | solution.py:407
  10.4 1.8 %shard_map.103.mine_ref = bf16[4,128,128]{2,1,0:T(8,128)(2,1)} custom-call(s32[4]{0:T(128)} %moved_ref.1, bf16[4,128,128]{2,1,0:T(8,128)(2,1)} %inv_ref.1, bf16[4,128]{1,0:T(4,128)(2,1)} %rows_ref.1, bf16[128,128]{1,0:T(8,128)(2,1)} %virt_ref.2), custom_call_target="tpu_custom_call" | custom-call | tf_op jit(solution)/shard_map/pallas_call | solution.py:408
  12.2 0.0 collective-permute-start
  12.2 1.6 %collective-permute-done.theirs_ref = bf16[4,128,128]{2,1,0:T(8,128)(2,1)S(1)} collective-permute-done((bf16[4,128,128]{2,1,0:T(8,128)(2,1)}, bf16[4,128,128]{2,1,0:T(8,128)(2,1)S(1)}, u32[]{:S(2)}, u32[]{:S(2)}) %collective-permute-start) | collective-permute-done | bytes 131104 | tf_op jit(solution)/shard_map/ppermute | solution.py:414
  13.7 0.0 copy-start
  13.7 0.9 %copy-done = bf16[4,128,128]{2,1,0:T(8,128)(2,1)S(1)} copy-done((bf16[4,128,128]{2,1,0:T(8,128)(2,1)S(1)}, bf16[4,128,128]{2,1,0:T(8,128)(2,1)}, u32[]{:S(2)}) %copy-start) | copy-done | bytes 131096
  14.6 0.2 shard_map.104
  14.9 6.1 %all-to-all-done.pay_ref.refs_3_ = f32[16,6,512]{2,1,0:T(8,128)S(1)} async-done(((f32[16,6,512]{2,1,0:T(8,128)}), f32[16,6,512]{2,1,0:T(8,128)S(1)}, u32[]{:S(2)}, u32[]{:S(2)}) %all-to-all-start) | async-done | bytes 196640 | tf_op jit(solution)/shard_map/all_to_all | solution.py:407
  21.0 12.9 %shard_map.106 = (f32[64,4,32,128]{3,2,1,0:T(8,128)S(1)}, f32[8,128]{1,0:T(8,128)S(1)}) custom-call(f8e4m3fn[1024,256]{1,0:T(32,128)(4,1)S(1)} %get-tuple-element.11.tab, f32[8,128]{1,0:T(8,128)S(1)} %get-tuple-element.12.back_ref, f32[16,6,512]{2,1,0:T(8,128)S(1)} %all-to-all-done.pay_ref.refs_3_), custom_call_target="tpu_custom_call" | custom-call | tf_op jit(solution)/shard_map/pallas_call | solution.py:425
  33.8 0.0 collective-permute-start.1
  33.9 1.2 %collective-permute-done.1.refs_1_ = f32[8,128]{1,0:T(8,128)S(1)} collective-permute-done((f32[8,128]{1,0:T(8,128)S(1)}, f32[8,128]{1,0:T(8,128)S(1)}, u32[]{:S(2)}, u32[]{:S(2)}) %collective-permute-start.1) | collective-permute-done | bytes 4128 | tf_op jit(solution)/shard_map/ppermute | solution.py:435
  35.0 8.4 %shard_map.107 = (f32[8,128]{1,0:T(8,128)S(1)}, f32[16,4,128]{2,1,0:T(4,128)}, f32[32,8,128]{2,1,0:T(8,128)S(1)}) custom-call(f32[8,128]{1,0:T(8,128)S(1)} %get-tuple-element.13.refs_0_, f32[8,128]{1,0:T(8,128)S(1)} %collective-permute-done.1.refs_1_, f32[64,4,32,128]{3,2,1,0:T(8,128)S(1)} %get-tuple-element.14.refs_2_, ...), custom_call_target="tpu_custom_call" | custom-call | tf_op jit(solution)/shard_map/pallas_call | solution.py:441
  43.4 10.3 %all_to_all.22.pieces_ref = f32[32,8,128]{2,1,0:T(8,128)} all-to-all(f32[32,8,128]{2,1,0:T(8,128)S(1)} %get-tuple-element.16), channel_id=1, replica_groups=mesh['walk'=2,'det'=4,'exc'=4] {'walk','det','exc'}, dimensions={0} | all-to-all | bytes 262144 | tf_op jit(solution)/shard_map/all_to_all | solution.py:455
  53.7 1.5 %shard_map.108 = (f32[64,128]{1,0:T(8,128)}, f32[4,128]{1,0:T(4,128)}) custom-call(f32[32,8,128]{2,1,0:T(8,128)} %all_to_all.22.pieces_ref), custom_call_target="tpu_custom_call" | custom-call | tf_op jit(solution)/shard_map/pallas_call | solution.py:456
  55.3 3.5 %all-to-all-start.2 = ((f32[16,4,128]{2,1,0:T(4,128)}), f32[16,4,128]{2,1,0:T(4,128)S(1)}, u32[]{:S(2)}, u32[]{:S(2)}) async-start(f32[16,4,128]{2,1,0:T(4,128)} %bitcast.9), calls=%async_computation.2 | async-start | bytes 65536 | tf_op jit(solution)/shard_map/all_to_all | solution.py:466
  58.8 0.6 slice_reduce_fusion
  59.4 0.7 %all_gather_reshape.3 = f32[2,1,256]{2,0,1:T(2,128)S(1)} reshape(f32[4,128]{1,0:T(4,128)} %get-tuple-element.17) | data formatting | bytes 4096 | tf_op jit(solution)/shard_map/all_gather;reshape | solution.py:478
  60.1 1.8 %all_gather.3 = f32[2,2,256]{2,0,1:T(2,128)S(1)} all-gather(f32[2,1,256]{2,0,1:T(2,128)S(1)} %all_gather_reshape.3), channel_id=1, replica_groups=mesh['walk'=2,'det'=4,'exc'=4] {'walk'}, dimensions={1}, use_global_device_ids=true | all-gather | bytes 6144 | tf_op jit(solution)/shard_map/all_gather | solution.py:478
  61.9 0.6 copy.13
  62.5 3.6 %all-to-all-done.2 = f32[16,4,128]{2,1,0:T(4,128)S(1)} async-done(((f32[16,4,128]{2,1,0:T(4,128)}), f32[16,4,128]{2,1,0:T(4,128)S(1)}, u32[]{:S(2)}, u32[]{:S(2)}) %all-to-all-start.2) | async-done | bytes 32800 | tf_op jit(solution)/shard_map/all_to_all | solution.py:466
  66.1 0.6 copy.17
  (1 shorter events, 0.0 us)
Async XLA Ops:
  2.1 18.9 %all-to-all-start = ((f32[16,6,512]{2,1,0:T(8,128)}), f32[16,6,512]{2,1,0:T(8,128)S(1)}, u32[]{:S(2)}, u32[]{:S(2)}) async-start(f32[16,6,512]{2,1,0:T(8,128)} %shard_map.105), calls=%async_computation | async-start | bytes 524288 | tf_op jit(solution)/shard_map/all_to_all | solution.py:407
  12.2 1.6 %collective-permute-start = (bf16[4,128,128]{2,1,0:T(8,128)(2,1)}, bf16[4,128,128]{2,1,0:T(8,128)(2,1)S(1)}, u32[]{:S(2)}, u32[]{:S(2)}) collective-permute-start(bf16[4,128,128]{2,1,0:T(8,128)(2,1)} %shard_map.103.mine_ref), channel_id=1, source_target_pairs={{0,16},{16,0},{1,17},{17,1},{2,18},{18,2},{3,19},{19,3},{4,20},{20... | collective-permute-start | bytes 393224 | tf_op jit(solution)/shard_map/ppermute | solution.py:414
  13.7 0.9 %copy-start = (bf16[4,128,128]{2,1,0:T(8,128)(2,1)S(1)}, bf16[4,128,128]{2,1,0:T(8,128)(2,1)}, u32[]{:S(2)}) copy-start(bf16[4,128,128]{2,1,0:T(8,128)(2,1)} %shard_map.103.mine_ref) | copy-start | bytes 393220
  33.8 1.2 %collective-permute-start.1 = (f32[8,128]{1,0:T(8,128)S(1)}, f32[8,128]{1,0:T(8,128)S(1)}, u32[]{:S(2)}, u32[]{:S(2)}) collective-permute-start(f32[8,128]{1,0:T(8,128)S(1)} %get-tuple-element.13.refs_0_), channel_id=1, source_target_pairs={{0,16},{16,0},{1,17},{17,1},{2,18},{18,2},{3,19},{19,3},{4,20},{20... | collective-permute-start | bytes 12296 | tf_op jit(solution)/shard_map/ppermute | solution.py:435
  55.3 10.8 %all-to-all-start.2 = ((f32[16,4,128]{2,1,0:T(4,128)}), f32[16,4,128]{2,1,0:T(4,128)S(1)}, u32[]{:S(2)}, u32[]{:S(2)}) async-start(f32[16,4,128]{2,1,0:T(4,128)} %bitcast.9), calls=%async_computation.2 | async-start | bytes 65536 | tf_op jit(solution)/shard_map/all_to_all | solution.py:466

commit v7 on v6

--- a/solution.py
+++ b/solution.py
@@ -7,6 +7,7 @@
 
 TILE = 256
 LANES = 128
+FIELDS = 6
 DET_AXES = ("det", "exc")
 ALL_AXES = ("walk", "det", "exc")
 FINE = 64.0
@@ -114,6 +115,13 @@
     zero = jnp.zeros(shape, kind)
     parts = [jnp.where(hit, jnp.full(shape, x, kind), zero) for x in values for hit in hits]
     return jnp.concatenate(parts, axis=0)
+
+
+def unpack_lists(packed_ref, pay_ref):
+    for block in range(pay_ref.shape[0]):
+        for x in range(pay_ref.shape[2] // LANES):
+            lanes = slice(x * LANES, (x + 1) * LANES)
+            pay_ref[block, 0:FIELDS, lanes] = packed_ref[block, FIELDS * x : FIELDS * (x + 1), :]
 
 
 def load_lists(pay_ref, t):
@@ -141,12 +149,16 @@
 
 
 def payload_kernel(occ_ref, virt_ref, rank_ref, coef_ref, pay_ref):
-    blocks, _, half = pay_ref.shape
+    blocks, depth, _ = pay_ref.shape
+    half = depth // FIELDS * LANES
     start = pl.multiple_of((lax.axis_index("walk") & 1) * half, LANES)
     lanes = pl.ds(start, half)
     codes = (occ_ref[:, lanes] * 128 + virt_ref[:, lanes]).astype(jnp.float32)
     rank = rank_ref[:, lanes].astype(jnp.float32)
     rows = jnp.concatenate([codes, rank, coef_ref[:, lanes]], axis=0)
+    rows = jnp.concatenate(
+        [rows[:, x : x + LANES] for x in range(0, half, LANES)], axis=0
+    )
     for k in range(blocks):
         pay_ref[k] = rows
 
@@ -191,7 +203,8 @@
     ]
 
 
-def select_kernel(tab, back_ref, pay_ref, ent_ref, amp_ref):
+def select_kernel(tab, back_ref, packed_ref, ent_ref, amp_ref, pay_ref):
+    unpack_lists(packed_ref, pay_ref)
     nblk, _, width = pay_ref.shape
     tiles = nblk * width // TILE
     parts = TILE // LANES
@@ -268,8 +281,9 @@
 
 
 def gradient_kernel(
-    walkers_total, part_ref, part2_ref, ent_ref, pay_ref, amp_ref, ci_ref, orb_ref, acc
+    walkers_total, part_ref, part2_ref, ent_ref, packed_ref, amp_ref, ci_ref, orb_ref, acc, pay_ref
 ):
+    unpack_lists(packed_ref, pay_ref)
     nblk, _, width = pay_ref.shape
     per_block = width // TILE
     tiles = nblk * per_block
@@ -396,11 +410,12 @@
     partner = [(u, u ^ 1) for u in range(walk_count)]
     vmem = pl.BlockSpec(memory_space=pltpu.VMEM)
     smem = pl.BlockSpec(memory_space=pltpu.SMEM)
+    lists = pltpu.VMEM((blocks, 8, half), jnp.float32)
     params = pltpu.CompilerParams(vmem_limit_bytes=32 << 20)
 
     payload = pl.pallas_call(
         payload_kernel,
-        out_shape=jax.ShapeDtypeStruct((blocks, 6, half), jnp.float32),
+        out_shape=jax.ShapeDtypeStruct((blocks, FIELDS * half // LANES, LANES), jnp.float32),
         in_specs=[vmem] * 4,
         out_specs=vmem,
     )(occ_list, virt_list, exc_rank[None], coefficient[None])
@@ -430,6 +445,7 @@
         ),
         in_specs=[vmem] * 3,
         out_specs=(vmem, vmem),
+        scratch_shapes=[lists],
         compiler_params=params,
     )(table, back, gathered)
     part2 = lax.ppermute(part, "walk", partner)
@@ -447,7 +463,7 @@
         ),
         in_specs=[vmem] * 4,
         out_specs=(vmem, vmem, vmem),
-        scratch_shapes=[pltpu.VMEM((256, LANES), jnp.float32)],
+        scratch_shapes=[pltpu.VMEM((256, LANES), jnp.float32), lists],
         compiler_params=params,
     )(part, part2, entries, gathered)
 

time: 67.2 us -> 65.8 us (0.979)
  waiting for transfers between devices: 12.5 us -> 11 us
    all_to_all x1, waiting for transfers between devices: 6.1 us -> 4.69 us  [per_device(): gathered = lax.all_to_all(payload, DET_AXES, 0, 0)]
where the time goes in v7:
time: 65.8 us; the launch traced here: 65.3 us
  Pallas kernels  26.3 us (40%)
  blocking collectives  12.1 us (18%)
  starting transfers between devices  11.8 us (18%)
  waiting for transfers between devices  11 us (17%)
  local copies, waits for them, and re-layouts  3.44 us (5%)
  between operations  0.67 us (1%)
    pallas_call x1, Pallas kernels, per_device(): pl.pallas_call(select_kernel, out_shape=(jax.ShapeDtypeStruct((ndet // LA...  12.9 us
    all_to_all x1, blocking collectives, per_device(): pieces = lax.all_to_all(orb_part, ALL_AXES, 0, 0)  10.3 us
    pallas_call x1, Pallas kernels, per_device(): pl.pallas_call(lambda *refs: gradient_kernel(float(walkers_total), *refs)...  8.45 us
    all_to_all x1, starting transfers between devices, per_device(): gathered = lax.all_to_all(payload, DET_AXES, 0, 0)  8.31 us
    all_to_all x1, waiting for transfers between devices, per_device(): gathered = lax.all_to_all(payload, DET_AXES, 0, 0)  4.69 us
    all_to_all x1, waiting for transfers between devices, per_device(): orb_all = lax.all_to_all(orb_rows, DET_AXES, 0, 0, tiled=True)  3.63 us
    all_to_all x1, starting transfers between devices, per_device(): orb_all = lax.all_to_all(orb_rows, DET_AXES, 0, 0, tiled=True)  3.5 us
    unnamed x4, local copies, waits for them, and re-layouts  2.12 us
  transfers between devices with their start and end apart: 4, of which 4 were waited for; matrix products, arithmetic and copies ran while one was open for 3% of the time, Pallas kernels for 3%

profile of v7, /device:TPU:0, one launch (start us, length us, event | category | flops | bytes accessed | tf_op | source)
XLA Modules:
  0.0 65.3 jit_solution(8613831603738403905)
XLA Ops:
  0.6 1.4 %shard_map.105 = f32[16,24,128]{2,1,0:T(8,128)} custom-call(s32[4,1024]{1,0:T(4,128)} %occ_ref.1, s32[4,1024]{1,0:T(4,128)} %virt_ref.3, s32[1,1024]{1,0:T(1,128)} %bitcast.12, f32[1,1024]{1,0:T(1,128)} %bitcast.13), custom_call_target="tpu_custom_call" | custom-call | tf_op jit(solution)/shard_map/pallas_call | solution.py:416
  2.1 8.3 %all-to-all-start = ((f32[16,24,128]{2,1,0:T(8,128)}), f32[16,24,128]{2,1,0:T(8,128)S(1)}, u32[]{:S(2)}, u32[]{:S(2)}) async-start(f32[16,24,128]{2,1,0:T(8,128)} %shard_map.105), calls=%async_computation | async-start | bytes 393216 | tf_op jit(solution)/shard_map/all_to_all | solution.py:422
  10.4 1.8 %shard_map.103.mine_ref = bf16[4,128,128]{2,1,0:T(8,128)(2,1)} custom-call(s32[4]{0:T(128)} %moved_ref.1, bf16[4,128,128]{2,1,0:T(8,128)(2,1)} %inv_ref.1, bf16[4,128]{1,0:T(4,128)(2,1)} %rows_ref.1, bf16[128,128]{1,0:T(8,128)(2,1)} %virt_ref.2), custom_call_target="tpu_custom_call" | custom-call | tf_op jit(solution)/shard_map/pallas_call | solution.py:423
  12.1 0.0 collective-permute-start
  12.1 1.6 %collective-permute-done.theirs_ref = bf16[4,128,128]{2,1,0:T(8,128)(2,1)S(1)} collective-permute-done((bf16[4,128,128]{2,1,0:T(8,128)(2,1)}, bf16[4,128,128]{2,1,0:T(8,128)(2,1)S(1)}, u32[]{:S(2)}, u32[]{:S(2)}) %collective-permute-start) | collective-permute-done | bytes 131104 | tf_op jit(solution)/shard_map/ppermute | solution.py:429
  13.7 0.0 copy-start
  13.7 0.9 %copy-done = bf16[4,128,128]{2,1,0:T(8,128)(2,1)S(1)} copy-done((bf16[4,128,128]{2,1,0:T(8,128)(2,1)S(1)}, bf16[4,128,128]{2,1,0:T(8,128)(2,1)}, u32[]{:S(2)}) %copy-start) | copy-done | bytes 131096
  14.6 0.2 shard_map.104
  14.9 4.7 %all-to-all-done.packed_ref.refs_3_ = f32[16,24,128]{2,1,0:T(8,128)S(1)} async-done(((f32[16,24,128]{2,1,0:T(8,128)}), f32[16,24,128]{2,1,0:T(8,128)S(1)}, u32[]{:S(2)}, u32[]{:S(2)}) %all-to-all-start) | async-done | bytes 196640 | tf_op jit(solution)/shard_map/all_to_all | solution.py:422
  19.6 12.9 %shard_map.106 = (f32[64,4,32,128]{3,2,1,0:T(8,128)S(1)}, f32[8,128]{1,0:T(8,128)S(1)}) custom-call(f8e4m3fn[1024,256]{1,0:T(32,128)(4,1)S(1)} %get-tuple-element.11.tab, f32[8,128]{1,0:T(8,128)S(1)} %get-tuple-element.12.back_ref, f32[16,24,128]{2,1,0:T(8,128)S(1)} %all-to-all-done.packed_ref.refs_3_), custom_call_target="tpu_custom_call" | custom-call | tf_op jit(solution)/shard_map/pallas_call | solution.py:440
  32.4 0.0 collective-permute-start.1
  32.5 1.2 %collective-permute-done.1.refs_1_ = f32[8,128]{1,0:T(8,128)S(1)} collective-permute-done((f32[8,128]{1,0:T(8,128)S(1)}, f32[8,128]{1,0:T(8,128)S(1)}, u32[]{:S(2)}, u32[]{:S(2)}) %collective-permute-start.1) | collective-permute-done | bytes 4128 | tf_op jit(solution)/shard_map/ppermute | solution.py:451
  33.6 8.5 %shard_map.107 = (f32[8,128]{1,0:T(8,128)S(1)}, f32[16,4,128]{2,1,0:T(4,128)}, f32[32,8,128]{2,1,0:T(8,128)S(1)}) custom-call(f32[8,128]{1,0:T(8,128)S(1)} %get-tuple-element.13.refs_0_, f32[8,128]{1,0:T(8,128)S(1)} %collective-permute-done.1.refs_1_, f32[64,4,32,128]{3,2,1,0:T(8,128)S(1)} %get-tuple-element.14.refs_2_, ...), custom_call_target="tpu_custom_call" | custom-call | tf_op jit(solution)/shard_map/pallas_call | solution.py:457
  42.1 10.3 %all_to_all.22.pieces_ref = f32[32,8,128]{2,1,0:T(8,128)} all-to-all(f32[32,8,128]{2,1,0:T(8,128)S(1)} %get-tuple-element.16), channel_id=1, replica_groups=mesh['walk'=2,'det'=4,'exc'=4] {'walk','det','exc'}, dimensions={0} | all-to-all | bytes 262144 | tf_op jit(solution)/shard_map/all_to_all | solution.py:471
  52.3 1.5 %shard_map.108 = (f32[64,128]{1,0:T(8,128)}, f32[4,128]{1,0:T(4,128)}) custom-call(f32[32,8,128]{2,1,0:T(8,128)} %all_to_all.22.pieces_ref), custom_call_target="tpu_custom_call" | custom-call | tf_op jit(solution)/shard_map/pallas_call | solution.py:472
  53.9 3.5 %all-to-all-start.2 = ((f32[16,4,128]{2,1,0:T(4,128)}), f32[16,4,128]{2,1,0:T(4,128)S(1)}, u32[]{:S(2)}, u32[]{:S(2)}) async-start(f32[16,4,128]{2,1,0:T(4,128)} %bitcast.9), calls=%async_computation.2 | async-start | bytes 65536 | tf_op jit(solution)/shard_map/all_to_all | solution.py:482
  57.4 0.6 slice_reduce_fusion
  58.0 0.7 %all_gather_reshape.3 = f32[2,1,256]{2,0,1:T(2,128)S(1)} reshape(f32[4,128]{1,0:T(4,128)} %get-tuple-element.17) | data formatting | bytes 4096 | tf_op jit(solution)/shard_map/all_gather;reshape | solution.py:494
  58.7 1.8 %all_gather.3 = f32[2,2,256]{2,0,1:T(2,128)S(1)} all-gather(f32[2,1,256]{2,0,1:T(2,128)S(1)} %all_gather_reshape.3), channel_id=1, replica_groups=mesh['walk'=2,'det'=4,'exc'=4] {'walk'}, dimensions={1}, use_global_device_ids=true | all-gather | bytes 6144 | tf_op jit(solution)/shard_map/all_gather | solution.py:494
  60.5 0.6 copy.13
  61.1 3.6 %all-to-all-done.2 = f32[16,4,128]{2,1,0:T(4,128)S(1)} async-done(((f32[16,4,128]{2,1,0:T(4,128)}), f32[16,4,128]{2,1,0:T(4,128)S(1)}, u32[]{:S(2)}, u32[]{:S(2)}) %all-to-all-start.2) | async-done | bytes 32800 | tf_op jit(solution)/shard_map/all_to_all | solution.py:482
  64.7 0.6 copy.17
  (1 shorter events, 0.0 us)
Async XLA Ops:
  2.1 17.5 %all-to-all-start = ((f32[16,24,128]{2,1,0:T(8,128)}), f32[16,24,128]{2,1,0:T(8,128)S(1)}, u32[]{:S(2)}, u32[]{:S(2)}) async-start(f32[16,24,128]{2,1,0:T(8,128)} %shard_map.105), calls=%async_computation | async-start | bytes 393216 | tf_op jit(solution)/shard_map/all_to_all | solution.py:422
  12.1 1.6 %collective-permute-start = (bf16[4,128,128]{2,1,0:T(8,128)(2,1)}, bf16[4,128,128]{2,1,0:T(8,128)(2,1)S(1)}, u32[]{:S(2)}, u32[]{:S(2)}) collective-permute-start(bf16[4,128,128]{2,1,0:T(8,128)(2,1)} %shard_map.103.mine_ref), channel_id=1, source_target_pairs={{0,16},{16,0},{1,17},{17,1},{2,18},{18,2},{3,19},{19,3},{4,20},{20... | collective-permute-start | bytes 393224 | tf_op jit(solution)/shard_map/ppermute | solution.py:429
  13.7 0.9 %copy-start = (bf16[4,128,128]{2,1,0:T(8,128)(2,1)S(1)}, bf16[4,128,128]{2,1,0:T(8,128)(2,1)}, u32[]{:S(2)}) copy-start(bf16[4,128,128]{2,1,0:T(8,128)(2,1)} %shard_map.103.mine_ref) | copy-start | bytes 393220
  32.4 1.2 %collective-permute-start.1 = (f32[8,128]{1,0:T(8,128)S(1)}, f32[8,128]{1,0:T(8,128)S(1)}, u32[]{:S(2)}, u32[]{:S(2)}) collective-permute-start(f32[8,128]{1,0:T(8,128)S(1)} %get-tuple-element.13.refs_0_), channel_id=1, source_target_pairs={{0,16},{16,0},{1,17},{17,1},{2,18},{18,2},{3,19},{19,3},{4,20},{20... | collective-permute-start | bytes 12296 | tf_op jit(solution)/shard_map/ppermute | solution.py:451
  53.9 10.8 %all-to-all-start.2 = ((f32[16,4,128]{2,1,0:T(4,128)}), f32[16,4,128]{2,1,0:T(4,128)S(1)}, u32[]{:S(2)}, u32[]{:S(2)}) async-start(f32[16,4,128]{2,1,0:T(4,128)} %bitcast.9), calls=%async_computation.2 | async-start | bytes 65536 | tf_op jit(solution)/shard_map/all_to_all | solution.py:482

commit v8 on v7

--- a/solution.py
+++ b/solution.py
@@ -412,6 +412,7 @@
     smem = pl.BlockSpec(memory_space=pltpu.SMEM)
     lists = pltpu.VMEM((blocks, 8, half), jnp.float32)
     params = pltpu.CompilerParams(vmem_limit_bytes=32 << 20)
+    small = pltpu.CompilerParams(vmem_limit_bytes=8 << 20)
 
     payload = pl.pallas_call(
         payload_kernel,
@@ -467,8 +468,10 @@
         compiler_params=params,
     )(part, part2, entries, gathered)
 
+    amplitude = amp[:4, 0]
     if packed:
         pieces = lax.all_to_all(orb_part, ALL_AXES, 0, 0)
+        pieces, amplitude = lax.optimization_barrier((pieces, amplitude))
         orb_rows, ci_mine = pl.pallas_call(
             sums_kernel,
             out_shape=(
@@ -477,6 +480,7 @@
             ),
             in_specs=[vmem],
             out_specs=(vmem, vmem),
+            compiler_params=small,
         )(pieces)
         ci_mine = ci_mine.reshape(2, ci_size)
         orb_all = lax.all_to_all(orb_rows, DET_AXES, 0, 0, tiled=True)
@@ -492,7 +496,7 @@
             jnp.broadcast_to(orb_mine[None], (blocks, orb_size)), DET_AXES, 0, 0
         )
     ci_grad = lax.all_gather(ci_mine, "walk", axis=1).reshape(local)
-    return (amp[:4, 0], ci_grad, orb_all.reshape(nocc // walk_count, nvirt))
+    return (amplitude, ci_grad, orb_all.reshape(nocc // walk_count, nvirt))
 
 
 def solution(mesh):

time: 65.8 us -> 65.7 us (level)
  blocking collectives: 12.1 us -> 1.78 us
  waiting for transfers between devices: 11 us -> 19.6 us
  starting transfers between devices: 11.8 us -> 14.4 us
  local copies, waits for them, and re-layouts: 3.44 us -> 2.76 us
    all_to_all x1 -> x0, blocking collectives: 10.3 us -> none  [per_device(): pieces = lax.all_to_all(orb_part, ALL_AXES, 0, 0)]
    all_to_all x0 -> x1, waiting for transfers between devices: none -> 7.28 us  [per_device(): pieces = lax.all_to_all(orb_part, ALL_AXES, 0, 0)]
    all_to_all x0 -> x1, starting transfers between devices: none -> 2.57 us  [per_device(): pieces = lax.all_to_all(orb_part, ALL_AXES, 0, 0)]
    all_to_all x1, waiting for transfers between devices: 3.63 us -> 4.93 us  [per_device(): orb_all = lax.all_to_all(orb_rows, DET_AXES, 0, 0, tiled=True)]
    pallas_call x1, Pallas kernels: 1.54 us -> 0.63 us  [per_device(): pl.pallas_call(sums_kernel, out_shape=(jax.ShapeDtypeStruct((blocks * 4,...]
    another operation x1, local copies, waits for them, and re-layouts: 0.69 us -> 0.01 us  [per_device(): ci_grad = lax.all_gather(ci_mine, 'walk', axis=1).reshape(local)]
  transfers between devices with their start and end apart: 4 -> 5, of which waited for: 4 -> 5; matrix products, arithmetic and copies ran while one was open for 3% -> 2% of each run, Pallas kernels for 3% -> 3%
where the time goes in v8:
time: 65.7 us; the launch traced here: 65.3 us
  Pallas kernels  26.1 us (40%)
  waiting for transfers between devices  19.6 us (30%)
  starting transfers between devices  14.4 us (22%)
  local copies, waits for them, and re-layouts  2.76 us (4%)
  blocking collectives  1.78 us (3%)
  between operations  0.68 us (1%)
    pallas_call x1, Pallas kernels, per_device(): pl.pallas_call(select_kernel, out_shape=(jax.ShapeDtypeStruct((ndet // LA...  12.9 us
    pallas_call x1, Pallas kernels, per_device(): pl.pallas_call(lambda *refs: gradient_kernel(float(walkers_total), *refs)...  9.09 us
    all_to_all x1, starting transfers between devices, per_device(): gathered = lax.all_to_all(payload, DET_AXES, 0, 0)  8.31 us
    all_to_all x1, waiting for transfers between devices, per_device(): pieces = lax.all_to_all(orb_part, ALL_AXES, 0, 0)  7.28 us
    all_to_all x1, waiting for transfers between devices, per_device(): orb_all = lax.all_to_all(orb_rows, DET_AXES, 0, 0, tiled=True)  4.93 us
    all_to_all x1, waiting for transfers between devices, per_device(): gathered = lax.all_to_all(payload, DET_AXES, 0, 0)  4.69 us
    all_to_all x1, starting transfers between devices, per_device(): orb_all = lax.all_to_all(orb_rows, DET_AXES, 0, 0, tiled=True)  3.5 us
    all_to_all x1, starting transfers between devices, per_device(): pieces = lax.all_to_all(orb_part, ALL_AXES, 0, 0)  2.57 us
  transfers between devices with their start and end apart: 5, of which 5 were waited for; matrix products, arithmetic and copies ran while one was open for 2% of the time, Pallas kernels for 3%

profile of v8, /device:TPU:0, one launch (start us, length us, event | category | flops | bytes accessed | tf_op | source)
XLA Modules:
  0.0 65.3 jit_solution(1554809349005611287)
XLA Ops:
  0.6 1.4 %shard_map.105 = f32[16,24,128]{2,1,0:T(8,128)} custom-call(s32[4,1024]{1,0:T(4,128)} %occ_ref.1, s32[4,1024]{1,0:T(4,128)} %virt_ref.3, s32[1,1024]{1,0:T(1,128)} %bitcast.11, f32[1,1024]{1,0:T(1,128)} %bitcast.12), custom_call_target="tpu_custom_call" | custom-call | tf_op jit(solution)/shard_map/pallas_call | solution.py:417
  2.1 8.3 %all-to-all-start = ((f32[16,24,128]{2,1,0:T(8,128)}), f32[16,24,128]{2,1,0:T(8,128)S(1)}, u32[]{:S(2)}, u32[]{:S(2)}) async-start(f32[16,24,128]{2,1,0:T(8,128)} %shard_map.105), calls=%async_computation | async-start | bytes 393216 | tf_op jit(solution)/shard_map/all_to_all | solution.py:423
  10.4 1.8 %shard_map.103.mine_ref = bf16[4,128,128]{2,1,0:T(8,128)(2,1)} custom-call(s32[4]{0:T(128)} %moved_ref.1, bf16[4,128,128]{2,1,0:T(8,128)(2,1)} %inv_ref.1, bf16[4,128]{1,0:T(4,128)(2,1)} %rows_ref.1, bf16[128,128]{1,0:T(8,128)(2,1)} %virt_ref.2), custom_call_target="tpu_custom_call" | custom-call | tf_op jit(solution)/shard_map/pallas_call | solution.py:424
  12.2 0.0 collective-permute-start
  12.2 1.6 %collective-permute-done.theirs_ref = bf16[4,128,128]{2,1,0:T(8,128)(2,1)S(1)} collective-permute-done((bf16[4,128,128]{2,1,0:T(8,128)(2,1)}, bf16[4,128,128]{2,1,0:T(8,128)(2,1)S(1)}, u32[]{:S(2)}, u32[]{:S(2)}) %collective-permute-start) | collective-permute-done | bytes 131104 | tf_op jit(solution)/shard_map/ppermute | solution.py:430
  13.7 0.0 copy-start
  13.7 0.9 %copy-done = bf16[4,128,128]{2,1,0:T(8,128)(2,1)S(1)} copy-done((bf16[4,128,128]{2,1,0:T(8,128)(2,1)S(1)}, bf16[4,128,128]{2,1,0:T(8,128)(2,1)}, u32[]{:S(2)}) %copy-start) | copy-done | bytes 131096
  14.6 0.2 shard_map.104
  14.9 4.7 %all-to-all-done.packed_ref.refs_3_ = f32[16,24,128]{2,1,0:T(8,128)S(1)} async-done(((f32[16,24,128]{2,1,0:T(8,128)}), f32[16,24,128]{2,1,0:T(8,128)S(1)}, u32[]{:S(2)}, u32[]{:S(2)}) %all-to-all-start) | async-done | bytes 196640 | tf_op jit(solution)/shard_map/all_to_all | solution.py:423
  19.6 12.9 %shard_map.106 = (f32[64,4,32,128]{3,2,1,0:T(8,128)S(1)}, f32[8,128]{1,0:T(8,128)S(1)}) custom-call(f8e4m3fn[1024,256]{1,0:T(32,128)(4,1)S(1)} %get-tuple-element.13.tab, f32[8,128]{1,0:T(8,128)S(1)} %get-tuple-element.14.back_ref, f32[16,24,128]{2,1,0:T(8,128)S(1)} %all-to-all-done.packed_ref.refs_3_), custom_call_target="tpu_custom_call" | custom-call | tf_op jit(solution)/shard_map/pallas_call | solution.py:441
  32.4 0.0 collective-permute-start.1
  32.5 1.2 %collective-permute-done.1.refs_1_ = f32[8,128]{1,0:T(8,128)S(1)} collective-permute-done((f32[8,128]{1,0:T(8,128)S(1)}, f32[8,128]{1,0:T(8,128)S(1)}, u32[]{:S(2)}, u32[]{:S(2)}) %collective-permute-start.1) | collective-permute-done | bytes 4128 | tf_op jit(solution)/shard_map/ppermute | solution.py:452
  33.6 9.1 %shard_map.107 = (f32[8,128]{1,0:T(8,128)S(1)}, f32[16,4,128]{2,1,0:T(4,128)}, f32[32,8,128]{2,1,0:T(8,128)}) custom-call(f32[8,128]{1,0:T(8,128)S(1)} %get-tuple-element.15.refs_0_, f32[8,128]{1,0:T(8,128)S(1)} %collective-permute-done.1.refs_1_, f32[64,4,32,128]{3,2,1,0:T(8,128)S(1)} %get-tuple-element.16.refs_2_, ...), custom_call_target="tpu_custom_call" | custom-call | tf_op jit(solution)/shard_map/pallas_call | solution.py:458
  42.7 2.6 %all-to-all-start.1 = ((f32[32,8,128]{2,1,0:T(8,128)}), f32[32,8,128]{2,1,0:T(8,128)S(1)}, u32[]{:S(2)}, u32[]{:S(2)}) async-start(f32[32,8,128]{2,1,0:T(8,128)} %get-tuple-element.17), calls=%async_computation.1 | async-start | bytes 262144 | tf_op jit(solution)/shard_map/all_to_all | solution.py:473
  45.3 0.6 slice_reduce_fusion
  45.9 7.3 %all-to-all-done.1.pieces_ref = f32[32,8,128]{2,1,0:T(8,128)S(1)} async-done(((f32[32,8,128]{2,1,0:T(8,128)}), f32[32,8,128]{2,1,0:T(8,128)S(1)}, u32[]{:S(2)}, u32[]{:S(2)}) %all-to-all-start.1) | async-done | bytes 131104 | tf_op jit(solution)/shard_map/all_to_all | solution.py:473
  53.2 0.6 shard_map.108
  53.8 3.5 %all-to-all-start.2 = ((f32[16,4,128]{2,1,0:T(4,128)}), f32[16,4,128]{2,1,0:T(4,128)S(1)}, u32[]{:S(2)}, u32[]{:S(2)}) async-start(f32[16,4,128]{2,1,0:T(4,128)} %bitcast.2), calls=%async_computation.2 | async-start | bytes 65536 | tf_op jit(solution)/shard_map/all_to_all | solution.py:486
  57.3 1.8 %all_gather.3 = f32[2,2,256]{2,0,1:T(2,128)S(1)} all-gather(f32[2,1,256]{2,0,1:T(2,128)S(1)} %all_gather_reshape.3), channel_id=1, replica_groups=mesh['walk'=2,'det'=4,'exc'=4] {'walk'}, dimensions={1}, use_global_device_ids=true | all-gather | bytes 6144 | tf_op jit(solution)/shard_map/all_gather | solution.py:498
  59.1 0.6 copy.13
  59.7 4.9 %all-to-all-done.2 = f32[16,4,128]{2,1,0:T(4,128)S(1)} async-done(((f32[16,4,128]{2,1,0:T(4,128)}), f32[16,4,128]{2,1,0:T(4,128)S(1)}, u32[]{:S(2)}, u32[]{:S(2)}) %all-to-all-start.2) | async-done | bytes 32800 | tf_op jit(solution)/shard_map/all_to_all | solution.py:486
  64.7 0.6 copy.17
  (2 shorter events, 0.0 us)
Async XLA Ops:
  2.1 17.5 %all-to-all-start = ((f32[16,24,128]{2,1,0:T(8,128)}), f32[16,24,128]{2,1,0:T(8,128)S(1)}, u32[]{:S(2)}, u32[]{:S(2)}) async-start(f32[16,24,128]{2,1,0:T(8,128)} %shard_map.105), calls=%async_computation | async-start | bytes 393216 | tf_op jit(solution)/shard_map/all_to_all | solution.py:423
  12.2 1.6 %collective-permute-start = (bf16[4,128,128]{2,1,0:T(8,128)(2,1)}, bf16[4,128,128]{2,1,0:T(8,128)(2,1)S(1)}, u32[]{:S(2)}, u32[]{:S(2)}) collective-permute-start(bf16[4,128,128]{2,1,0:T(8,128)(2,1)} %shard_map.103.mine_ref), channel_id=1, source_target_pairs={{0,16},{16,0},{1,17},{17,1},{2,18},{18,2},{3,19},{19,3},{4,20},{20... | collective-permute-start | bytes 393224 | tf_op jit(solution)/shard_map/ppermute | solution.py:430
  13.7 0.9 %copy-start = (bf16[4,128,128]{2,1,0:T(8,128)(2,1)S(1)}, bf16[4,128,128]{2,1,0:T(8,128)(2,1)}, u32[]{:S(2)}) copy-start(bf16[4,128,128]{2,1,0:T(8,128)(2,1)} %shard_map.103.mine_ref) | copy-start | bytes 393220
  32.4 1.2 %collective-permute-start.1 = (f32[8,128]{1,0:T(8,128)S(1)}, f32[8,128]{1,0:T(8,128)S(1)}, u32[]{:S(2)}, u32[]{:S(2)}) collective-permute-start(f32[8,128]{1,0:T(8,128)S(1)} %get-tuple-element.15.refs_0_), channel_id=1, source_target_pairs={{0,16},{16,0},{1,17},{17,1},{2,18},{18,2},{3,19},{19,3},{4,20},{20... | collective-permute-start | bytes 12296 | tf_op jit(solution)/shard_map/ppermute | solution.py:452
  42.7 10.5 %all-to-all-start.1 = ((f32[32,8,128]{2,1,0:T(8,128)}), f32[32,8,128]{2,1,0:T(8,128)S(1)}, u32[]{:S(2)}, u32[]{:S(2)}) async-start(f32[32,8,128]{2,1,0:T(8,128)} %get-tuple-element.17), calls=%async_computation.1 | async-start | bytes 262144 | tf_op jit(solution)/shard_map/all_to_all | solution.py:473
  53.8 10.8 %all-to-all-start.2 = ((f32[16,4,128]{2,1,0:T(4,128)}), f32[16,4,128]{2,1,0:T(4,128)S(1)}, u32[]{:S(2)}, u32[]{:S(2)}) async-start(f32[16,4,128]{2,1,0:T(4,128)} %bitcast.2), calls=%async_computation.2 | async-start | bytes 65536 | tf_op jit(solution)/shard_map/all_to_all | solution.py:486

commit v9 on v7

--- a/solution.py
+++ b/solution.py
@@ -252,7 +252,7 @@
             total = total + ratio * rows8(coef[:, lanes])
         return total
 
-    total = lax.fori_loop(0, tiles, forward, jnp.zeros((8, LANES), jnp.float32), unroll=4)
+    total = lax.fori_loop(0, tiles, forward, jnp.zeros((8, LANES), jnp.float32), unroll=8)
     amp_ref[...] = jnp.broadcast_to(jnp.sum(total, axis=1, keepdims=True), (8, LANES))
 
 
@@ -368,7 +368,7 @@
     acc[...] = jnp.zeros_like(acc)
     if packed:
         orb_ref[...] = jnp.zeros_like(orb_ref)
-    lax.fori_loop(0, tiles, backward, 0, unroll=8)
+    lax.fori_loop(0, tiles, backward, 0, unroll=32)
     total = acc[0:128, :] + acc[128:256, :]
     if packed:
         for dest in range(orb_ref.shape[0]):

time: 65.8 us -> 65.1 us (0.989)
  Pallas kernels: 26.3 us -> 25.6 us
where the time goes in v9:
time: 65.1 us; the launch traced here: 64.6 us
  Pallas kernels  25.6 us (39%)
  blocking collectives  12.1 us (19%)
  starting transfers between devices  11.8 us (18%)
  waiting for transfers between devices  11 us (17%)
  local copies, waits for them, and re-layouts  3.44 us (5%)
  between operations  0.67 us (1%)
    pallas_call x1, Pallas kernels, per_device(): pl.pallas_call(select_kernel, out_shape=(jax.ShapeDtypeStruct((ndet // LA...  12.7 us
    all_to_all x1, blocking collectives, per_device(): pieces = lax.all_to_all(orb_part, ALL_AXES, 0, 0)  10.3 us
    all_to_all x1, starting transfers between devices, per_device(): gathered = lax.all_to_all(payload, DET_AXES, 0, 0)  8.31 us
    pallas_call x1, Pallas kernels, per_device(): pl.pallas_call(lambda *refs: gradient_kernel(float(walkers_total), *refs)...  7.92 us
    all_to_all x1, waiting for transfers between devices, per_device(): gathered = lax.all_to_all(payload, DET_AXES, 0, 0)  4.69 us
    all_to_all x1, waiting for transfers between devices, per_device(): orb_all = lax.all_to_all(orb_rows, DET_AXES, 0, 0, tiled=True)  3.63 us
    all_to_all x1, starting transfers between devices, per_device(): orb_all = lax.all_to_all(orb_rows, DET_AXES, 0, 0, tiled=True)  3.5 us
    unnamed x4, local copies, waits for them, and re-layouts  2.12 us
  transfers between devices with their start and end apart: 4, of which 4 were waited for; matrix products, arithmetic and copies ran while one was open for 3% of the time, Pallas kernels for 3%

profile of v9, /device:TPU:0, one launch (start us, length us, event | category | flops | bytes accessed | tf_op | source)
XLA Modules:
  0.0 64.6 jit_solution(7783152466370690260)
XLA Ops:
  0.6 1.4 %shard_map.105 = f32[16,24,128]{2,1,0:T(8,128)} custom-call(s32[4,1024]{1,0:T(4,128)} %occ_ref.1, s32[4,1024]{1,0:T(4,128)} %virt_ref.3, s32[1,1024]{1,0:T(1,128)} %bitcast.12, f32[1,1024]{1,0:T(1,128)} %bitcast.13), custom_call_target="tpu_custom_call" | custom-call | tf_op jit(solution)/shard_map/pallas_call | solution.py:416
  2.1 8.3 %all-to-all-start = ((f32[16,24,128]{2,1,0:T(8,128)}), f32[16,24,128]{2,1,0:T(8,128)S(1)}, u32[]{:S(2)}, u32[]{:S(2)}) async-start(f32[16,24,128]{2,1,0:T(8,128)} %shard_map.105), calls=%async_computation | async-start | bytes 393216 | tf_op jit(solution)/shard_map/all_to_all | solution.py:422
  10.4 1.8 %shard_map.103.mine_ref = bf16[4,128,128]{2,1,0:T(8,128)(2,1)} custom-call(s32[4]{0:T(128)} %moved_ref.1, bf16[4,128,128]{2,1,0:T(8,128)(2,1)} %inv_ref.1, bf16[4,128]{1,0:T(4,128)(2,1)} %rows_ref.1, bf16[128,128]{1,0:T(8,128)(2,1)} %virt_ref.2), custom_call_target="tpu_custom_call" | custom-call | tf_op jit(solution)/shard_map/pallas_call | solution.py:423
  12.1 0.0 collective-permute-start
  12.1 1.6 %collective-permute-done.theirs_ref = bf16[4,128,128]{2,1,0:T(8,128)(2,1)S(1)} collective-permute-done((bf16[4,128,128]{2,1,0:T(8,128)(2,1)}, bf16[4,128,128]{2,1,0:T(8,128)(2,1)S(1)}, u32[]{:S(2)}, u32[]{:S(2)}) %collective-permute-start) | collective-permute-done | bytes 131104 | tf_op jit(solution)/shard_map/ppermute | solution.py:429
  13.7 0.0 copy-start
  13.7 0.9 %copy-done = bf16[4,128,128]{2,1,0:T(8,128)(2,1)S(1)} copy-done((bf16[4,128,128]{2,1,0:T(8,128)(2,1)S(1)}, bf16[4,128,128]{2,1,0:T(8,128)(2,1)}, u32[]{:S(2)}) %copy-start) | copy-done | bytes 131096
  14.6 0.2 shard_map.104
  14.9 4.7 %all-to-all-done.packed_ref.refs_3_ = f32[16,24,128]{2,1,0:T(8,128)S(1)} async-done(((f32[16,24,128]{2,1,0:T(8,128)}), f32[16,24,128]{2,1,0:T(8,128)S(1)}, u32[]{:S(2)}, u32[]{:S(2)}) %all-to-all-start) | async-done | bytes 196640 | tf_op jit(solution)/shard_map/all_to_all | solution.py:422
  19.6 12.7 %shard_map.106 = (f32[64,4,32,128]{3,2,1,0:T(8,128)S(1)}, f32[8,128]{1,0:T(8,128)S(1)}) custom-call(f8e4m3fn[1024,256]{1,0:T(32,128)(4,1)S(1)} %get-tuple-element.11.tab, f32[8,128]{1,0:T(8,128)S(1)} %get-tuple-element.12.back_ref, f32[16,24,128]{2,1,0:T(8,128)S(1)} %all-to-all-done.packed_ref.refs_3_), custom_call_target="tpu_custom_call" | custom-call | tf_op jit(solution)/shard_map/pallas_call | solution.py:440
  32.3 0.0 collective-permute-start.1
  32.3 1.2 %collective-permute-done.1.refs_1_ = f32[8,128]{1,0:T(8,128)S(1)} collective-permute-done((f32[8,128]{1,0:T(8,128)S(1)}, f32[8,128]{1,0:T(8,128)S(1)}, u32[]{:S(2)}, u32[]{:S(2)}) %collective-permute-start.1) | collective-permute-done | bytes 4128 | tf_op jit(solution)/shard_map/ppermute | solution.py:451
  33.4 7.9 %shard_map.107 = (f32[8,128]{1,0:T(8,128)S(1)}, f32[16,4,128]{2,1,0:T(4,128)}, f32[32,8,128]{2,1,0:T(8,128)S(1)}) custom-call(f32[8,128]{1,0:T(8,128)S(1)} %get-tuple-element.13.refs_0_, f32[8,128]{1,0:T(8,128)S(1)} %collective-permute-done.1.refs_1_, f32[64,4,32,128]{3,2,1,0:T(8,128)S(1)} %get-tuple-element.14.refs_2_, ...), custom_call_target="tpu_custom_call" | custom-call | tf_op jit(solution)/shard_map/pallas_call | solution.py:457
  41.4 10.3 %all_to_all.22.pieces_ref = f32[32,8,128]{2,1,0:T(8,128)} all-to-all(f32[32,8,128]{2,1,0:T(8,128)S(1)} %get-tuple-element.16), channel_id=1, replica_groups=mesh['walk'=2,'det'=4,'exc'=4] {'walk','det','exc'}, dimensions={0} | all-to-all | bytes 262144 | tf_op jit(solution)/shard_map/all_to_all | solution.py:471
  51.7 1.5 %shard_map.108 = (f32[64,128]{1,0:T(8,128)}, f32[4,128]{1,0:T(4,128)}) custom-call(f32[32,8,128]{2,1,0:T(8,128)} %all_to_all.22.pieces_ref), custom_call_target="tpu_custom_call" | custom-call | tf_op jit(solution)/shard_map/pallas_call | solution.py:472
  53.2 3.5 %all-to-all-start.2 = ((f32[16,4,128]{2,1,0:T(4,128)}), f32[16,4,128]{2,1,0:T(4,128)S(1)}, u32[]{:S(2)}, u32[]{:S(2)}) async-start(f32[16,4,128]{2,1,0:T(4,128)} %bitcast.9), calls=%async_computation.2 | async-start | bytes 65536 | tf_op jit(solution)/shard_map/all_to_all | solution.py:482
  56.7 0.6 slice_reduce_fusion
  57.3 0.7 %all_gather_reshape.3 = f32[2,1,256]{2,0,1:T(2,128)S(1)} reshape(f32[4,128]{1,0:T(4,128)} %get-tuple-element.17) | data formatting | bytes 4096 | tf_op jit(solution)/shard_map/all_gather;reshape | solution.py:494
  58.0 1.8 %all_gather.3 = f32[2,2,256]{2,0,1:T(2,128)S(1)} all-gather(f32[2,1,256]{2,0,1:T(2,128)S(1)} %all_gather_reshape.3), channel_id=1, replica_groups=mesh['walk'=2,'det'=4,'exc'=4] {'walk'}, dimensions={1}, use_global_device_ids=true | all-gather | bytes 6144 | tf_op jit(solution)/shard_map/all_gather | solution.py:494
  59.8 0.6 copy.13
  60.4 3.6 %all-to-all-done.2 = f32[16,4,128]{2,1,0:T(4,128)S(1)} async-done(((f32[16,4,128]{2,1,0:T(4,128)}), f32[16,4,128]{2,1,0:T(4,128)S(1)}, u32[]{:S(2)}, u32[]{:S(2)}) %all-to-all-start.2) | async-done | bytes 32800 | tf_op jit(solution)/shard_map/all_to_all | solution.py:482
  64.0 0.6 copy.17
  (1 shorter events, 0.0 us)
Async XLA Ops:
  2.1 17.5 %all-to-all-start = ((f32[16,24,128]{2,1,0:T(8,128)}), f32[16,24,128]{2,1,0:T(8,128)S(1)}, u32[]{:S(2)}, u32[]{:S(2)}) async-start(f32[16,24,128]{2,1,0:T(8,128)} %shard_map.105), calls=%async_computation | async-start | bytes 393216 | tf_op jit(solution)/shard_map/all_to_all | solution.py:422
  12.1 1.6 %collective-permute-start = (bf16[4,128,128]{2,1,0:T(8,128)(2,1)}, bf16[4,128,128]{2,1,0:T(8,128)(2,1)S(1)}, u32[]{:S(2)}, u32[]{:S(2)}) collective-permute-start(bf16[4,128,128]{2,1,0:T(8,128)(2,1)} %shard_map.103.mine_ref), channel_id=1, source_target_pairs={{0,16},{16,0},{1,17},{17,1},{2,18},{18,2},{3,19},{19,3},{4,20},{20... | collective-permute-start | bytes 393224 | tf_op jit(solution)/shard_map/ppermute | solution.py:429
  13.7 0.9 %copy-start = (bf16[4,128,128]{2,1,0:T(8,128)(2,1)S(1)}, bf16[4,128,128]{2,1,0:T(8,128)(2,1)}, u32[]{:S(2)}) copy-start(bf16[4,128,128]{2,1,0:T(8,128)(2,1)} %shard_map.103.mine_ref) | copy-start | bytes 393220
  32.3 1.2 %collective-permute-start.1 = (f32[8,128]{1,0:T(8,128)S(1)}, f32[8,128]{1,0:T(8,128)S(1)}, u32[]{:S(2)}, u32[]{:S(2)}) collective-permute-start(f32[8,128]{1,0:T(8,128)S(1)} %get-tuple-element.13.refs_0_), channel_id=1, source_target_pairs={{0,16},{16,0},{1,17},{17,1},{2,18},{18,2},{3,19},{19,3},{4,20},{20... | collective-permute-start | bytes 12296 | tf_op jit(solution)/shard_map/ppermute | solution.py:451
  53.2 10.8 %all-to-all-start.2 = ((f32[16,4,128]{2,1,0:T(4,128)}), f32[16,4,128]{2,1,0:T(4,128)S(1)}, u32[]{:S(2)}, u32[]{:S(2)}) async-start(f32[16,4,128]{2,1,0:T(4,128)} %bitcast.9), calls=%async_computation.2 | async-start | bytes 65536 | tf_op jit(solution)/shard_map/all_to_all | solution.py:482

commit v10 on v9

--- a/solution.py
+++ b/solution.py
@@ -412,6 +412,7 @@
     smem = pl.BlockSpec(memory_space=pltpu.SMEM)
     lists = pltpu.VMEM((blocks, 8, half), jnp.float32)
     params = pltpu.CompilerParams(vmem_limit_bytes=32 << 20)
+    small = pltpu.CompilerParams(vmem_limit_bytes=8 << 20)
 
     payload = pl.pallas_call(
         payload_kernel,
@@ -477,6 +478,7 @@
             ),
             in_specs=[vmem],
             out_specs=(vmem, vmem),
+            compiler_params=small,
         )(pieces)
         ci_mine = ci_mine.reshape(2, ci_size)
         orb_all = lax.all_to_all(orb_rows, DET_AXES, 0, 0, tiled=True)

time: 65.1 us -> 63.5 us (0.975)
  Pallas kernels: 25.6 us -> 24.7 us
  blocking collectives: 12.1 us -> 11.4 us
  waiting for transfers between devices: 11 us -> 11.7 us
  local copies, waits for them, and re-layouts: 3.44 us -> 2.76 us
    pallas_call x1, Pallas kernels: 1.54 us -> 0.63 us  [per_device(): pl.pallas_call(sums_kernel, out_shape=(jax.ShapeDtypeStruct((blocks * 4,...]
    all_to_all x1, blocking collectives: 10.3 us -> 9.62 us  [per_device(): pieces = lax.all_to_all(orb_part, ALL_AXES, 0, 0)]
    all_to_all x1, waiting for transfers between devices: 3.63 us -> 4.32 us  [per_device(): orb_all = lax.all_to_all(orb_rows, DET_AXES, 0, 0, tiled=True)]
    another operation x1, local copies, waits for them, and re-layouts: 0.69 us -> 0.01 us  [per_device(): ci_grad = lax.all_gather(ci_mine, 'walk', axis=1).reshape(local)]
  transfers between devices with their start and end apart: 4 -> 4, of which waited for: 4 -> 4; matrix products, arithmetic and copies ran while one was open for 3% -> 2% of each run, Pallas kernels for 3% -> 3%
where the time goes in v10:
time: 63.5 us; the launch traced here: 63.1 us
  Pallas kernels  24.7 us (39%)
  starting transfers between devices  11.8 us (19%)
  waiting for transfers between devices  11.7 us (18%)
  blocking collectives  11.4 us (18%)
  local copies, waits for them, and re-layouts  2.76 us (4%)
  between operations  0.67 us (1%)
    pallas_call x1, Pallas kernels, per_device(): pl.pallas_call(select_kernel, out_shape=(jax.ShapeDtypeStruct((ndet // LA...  12.7 us
    all_to_all x1, blocking collectives, per_device(): pieces = lax.all_to_all(orb_part, ALL_AXES, 0, 0)  9.62 us
    all_to_all x1, starting transfers between devices, per_device(): gathered = lax.all_to_all(payload, DET_AXES, 0, 0)  8.31 us
    pallas_call x1, Pallas kernels, per_device(): pl.pallas_call(lambda *refs: gradient_kernel(float(walkers_total), *refs)...  7.92 us
    all_to_all x1, waiting for transfers between devices, per_device(): gathered = lax.all_to_all(payload, DET_AXES, 0, 0)  4.69 us
    all_to_all x1, waiting for transfers between devices, per_device(): orb_all = lax.all_to_all(orb_rows, DET_AXES, 0, 0, tiled=True)  4.32 us
    all_to_all x1, starting transfers between devices, per_device(): orb_all = lax.all_to_all(orb_rows, DET_AXES, 0, 0, tiled=True)  3.5 us
    unnamed x4, local copies, waits for them, and re-layouts  2.12 us
  transfers between devices with their start and end apart: 4, of which 4 were waited for; matrix products, arithmetic and copies ran while one was open for 2% of the time, Pallas kernels for 3%

profile of v10, /device:TPU:0, one launch (start us, length us, event | category | flops | bytes accessed | tf_op | source)
XLA Modules:
  0.0 63.1 jit_solution(9239173274632333408)
XLA Ops:
  0.6 1.4 %shard_map.105 = f32[16,24,128]{2,1,0:T(8,128)} custom-call(s32[4,1024]{1,0:T(4,128)} %occ_ref.1, s32[4,1024]{1,0:T(4,128)} %virt_ref.3, s32[1,1024]{1,0:T(1,128)} %bitcast.11, f32[1,1024]{1,0:T(1,128)} %bitcast.12), custom_call_target="tpu_custom_call" | custom-call | tf_op jit(solution)/shard_map/pallas_call | solution.py:417
  2.1 8.3 %all-to-all-start = ((f32[16,24,128]{2,1,0:T(8,128)}), f32[16,24,128]{2,1,0:T(8,128)S(1)}, u32[]{:S(2)}, u32[]{:S(2)}) async-start(f32[16,24,128]{2,1,0:T(8,128)} %shard_map.105), calls=%async_computation | async-start | bytes 393216 | tf_op jit(solution)/shard_map/all_to_all | solution.py:423
  10.4 1.8 %shard_map.103.mine_ref = bf16[4,128,128]{2,1,0:T(8,128)(2,1)} custom-call(s32[4]{0:T(128)} %moved_ref.1, bf16[4,128,128]{2,1,0:T(8,128)(2,1)} %inv_ref.1, bf16[4,128]{1,0:T(4,128)(2,1)} %rows_ref.1, bf16[128,128]{1,0:T(8,128)(2,1)} %virt_ref.2), custom_call_target="tpu_custom_call" | custom-call | tf_op jit(solution)/shard_map/pallas_call | solution.py:424
  12.1 0.0 collective-permute-start
  12.1 1.6 %collective-permute-done.theirs_ref = bf16[4,128,128]{2,1,0:T(8,128)(2,1)S(1)} collective-permute-done((bf16[4,128,128]{2,1,0:T(8,128)(2,1)}, bf16[4,128,128]{2,1,0:T(8,128)(2,1)S(1)}, u32[]{:S(2)}, u32[]{:S(2)}) %collective-permute-start) | collective-permute-done | bytes 131104 | tf_op jit(solution)/shard_map/ppermute | solution.py:430
  13.7 0.0 copy-start
  13.7 0.9 %copy-done = bf16[4,128,128]{2,1,0:T(8,128)(2,1)S(1)} copy-done((bf16[4,128,128]{2,1,0:T(8,128)(2,1)S(1)}, bf16[4,128,128]{2,1,0:T(8,128)(2,1)}, u32[]{:S(2)}) %copy-start) | copy-done | bytes 131096
  14.6 0.2 shard_map.104
  14.9 4.7 %all-to-all-done.packed_ref.refs_3_ = f32[16,24,128]{2,1,0:T(8,128)S(1)} async-done(((f32[16,24,128]{2,1,0:T(8,128)}), f32[16,24,128]{2,1,0:T(8,128)S(1)}, u32[]{:S(2)}, u32[]{:S(2)}) %all-to-all-start) | async-done | bytes 196640 | tf_op jit(solution)/shard_map/all_to_all | solution.py:423
  19.6 12.7 %shard_map.106 = (f32[64,4,32,128]{3,2,1,0:T(8,128)S(1)}, f32[8,128]{1,0:T(8,128)S(1)}) custom-call(f8e4m3fn[1024,256]{1,0:T(32,128)(4,1)S(1)} %get-tuple-element.11.tab, f32[8,128]{1,0:T(8,128)S(1)} %get-tuple-element.12.back_ref, f32[16,24,128]{2,1,0:T(8,128)S(1)} %all-to-all-done.packed_ref.refs_3_), custom_call_target="tpu_custom_call" | custom-call | tf_op jit(solution)/shard_map/pallas_call | solution.py:441
  32.3 0.0 collective-permute-start.1
  32.3 1.2 %collective-permute-done.1.refs_1_ = f32[8,128]{1,0:T(8,128)S(1)} collective-permute-done((f32[8,128]{1,0:T(8,128)S(1)}, f32[8,128]{1,0:T(8,128)S(1)}, u32[]{:S(2)}, u32[]{:S(2)}) %collective-permute-start.1) | collective-permute-done | bytes 4128 | tf_op jit(solution)/shard_map/ppermute | solution.py:452
  33.4 7.9 %shard_map.107 = (f32[8,128]{1,0:T(8,128)S(1)}, f32[16,4,128]{2,1,0:T(4,128)}, f32[32,8,128]{2,1,0:T(8,128)S(1)}) custom-call(f32[8,128]{1,0:T(8,128)S(1)} %get-tuple-element.13.refs_0_, f32[8,128]{1,0:T(8,128)S(1)} %collective-permute-done.1.refs_1_, f32[64,4,32,128]{3,2,1,0:T(8,128)S(1)} %get-tuple-element.14.refs_2_, ...), custom_call_target="tpu_custom_call" | custom-call | tf_op jit(solution)/shard_map/pallas_call | solution.py:458
  41.4 9.6 %all_to_all.22.pieces_ref = f32[32,8,128]{2,1,0:T(8,128)S(1)} all-to-all(f32[32,8,128]{2,1,0:T(8,128)S(1)} %get-tuple-element.16), channel_id=1, replica_groups=mesh['walk'=2,'det'=4,'exc'=4] {'walk','det','exc'}, dimensions={0} | all-to-all | bytes 262144 | tf_op jit(solution)/shard_map/all_to_all | solution.py:472
  51.0 0.6 shard_map.108
  51.6 3.5 %all-to-all-start.2 = ((f32[16,4,128]{2,1,0:T(4,128)}), f32[16,4,128]{2,1,0:T(4,128)S(1)}, u32[]{:S(2)}, u32[]{:S(2)}) async-start(f32[16,4,128]{2,1,0:T(4,128)} %bitcast.2), calls=%async_computation.2 | async-start | bytes 65536 | tf_op jit(solution)/shard_map/all_to_all | solution.py:484
  55.1 0.6 slice_reduce_fusion
  55.8 1.8 %all_gather.3 = f32[2,2,256]{2,0,1:T(2,128)S(1)} all-gather(f32[2,1,256]{2,0,1:T(2,128)S(1)} %all_gather_reshape.3), channel_id=1, replica_groups=mesh['walk'=2,'det'=4,'exc'=4] {'walk'}, dimensions={1}, use_global_device_ids=true | all-gather | bytes 6144 | tf_op jit(solution)/shard_map/all_gather | solution.py:496
  57.5 0.6 copy.13
  58.1 4.3 %all-to-all-done.2 = f32[16,4,128]{2,1,0:T(4,128)S(1)} async-done(((f32[16,4,128]{2,1,0:T(4,128)}), f32[16,4,128]{2,1,0:T(4,128)S(1)}, u32[]{:S(2)}, u32[]{:S(2)}) %all-to-all-start.2) | async-done | bytes 32800 | tf_op jit(solution)/shard_map/all_to_all | solution.py:484
  62.4 0.6 copy.17
  (2 shorter events, 0.0 us)
Async XLA Ops:
  2.1 17.5 %all-to-all-start = ((f32[16,24,128]{2,1,0:T(8,128)}), f32[16,24,128]{2,1,0:T(8,128)S(1)}, u32[]{:S(2)}, u32[]{:S(2)}) async-start(f32[16,24,128]{2,1,0:T(8,128)} %shard_map.105), calls=%async_computation | async-start | bytes 393216 | tf_op jit(solution)/shard_map/all_to_all | solution.py:423
  12.1 1.6 %collective-permute-start = (bf16[4,128,128]{2,1,0:T(8,128)(2,1)}, bf16[4,128,128]{2,1,0:T(8,128)(2,1)S(1)}, u32[]{:S(2)}, u32[]{:S(2)}) collective-permute-start(bf16[4,128,128]{2,1,0:T(8,128)(2,1)} %shard_map.103.mine_ref), channel_id=1, source_target_pairs={{0,16},{16,0},{1,17},{17,1},{2,18},{18,2},{3,19},{19,3},{4,20},{20... | collective-permute-start | bytes 393224 | tf_op jit(solution)/shard_map/ppermute | solution.py:430
  13.7 0.9 %copy-start = (bf16[4,128,128]{2,1,0:T(8,128)(2,1)S(1)}, bf16[4,128,128]{2,1,0:T(8,128)(2,1)}, u32[]{:S(2)}) copy-start(bf16[4,128,128]{2,1,0:T(8,128)(2,1)} %shard_map.103.mine_ref) | copy-start | bytes 393220
  32.3 1.2 %collective-permute-start.1 = (f32[8,128]{1,0:T(8,128)S(1)}, f32[8,128]{1,0:T(8,128)S(1)}, u32[]{:S(2)}, u32[]{:S(2)}) collective-permute-start(f32[8,128]{1,0:T(8,128)S(1)} %get-tuple-element.13.refs_0_), channel_id=1, source_target_pairs={{0,16},{16,0},{1,17},{17,1},{2,18},{18,2},{3,19},{19,3},{4,20},{20... | collective-permute-start | bytes 12296 | tf_op jit(solution)/shard_map/ppermute | solution.py:452
  51.6 10.8 %all-to-all-start.2 = ((f32[16,4,128]{2,1,0:T(4,128)}), f32[16,4,128]{2,1,0:T(4,128)S(1)}, u32[]{:S(2)}, u32[]{:S(2)}) async-start(f32[16,4,128]{2,1,0:T(4,128)} %bitcast.2), calls=%async_computation.2 | async-start | bytes 65536 | tf_op jit(solution)/shard_map/all_to_all | solution.py:484

commit v11 on v10

--- a/solution.py
+++ b/solution.py
@@ -268,9 +268,7 @@
     n = len(items) // 2
     out = []
     for x, y in zip(items[:n], items[n:]):
-        x = x + pltpu.roll(x, 8 - dist, 0)
-        y = y + pltpu.roll(y, dist, 0)
-        out.append(jnp.where(first, x, y))
+        out.append(jnp.where(first, x, y) + along_rows(jnp.where(first, y, x), sub ^ dist))
     return out
 
 

time: 63.5 us -> 63.4 us (level)
  no operation moved by 1% of the time
where the time goes in v11:
time: 63.4 us; the launch traced here: 63 us
  Pallas kernels  24.7 us (39%)
  starting transfers between devices  11.8 us (19%)
  waiting for transfers between devices  11.7 us (18%)
  blocking collectives  11.4 us (18%)
  local copies, waits for them, and re-layouts  2.76 us (4%)
  between operations  0.67 us (1%)
    pallas_call x1, Pallas kernels, per_device(): pl.pallas_call(select_kernel, out_shape=(jax.ShapeDtypeStruct((ndet // LA...  12.7 us
    all_to_all x1, blocking collectives, per_device(): pieces = lax.all_to_all(orb_part, ALL_AXES, 0, 0)  9.62 us
    all_to_all x1, starting transfers between devices, per_device(): gathered = lax.all_to_all(payload, DET_AXES, 0, 0)  8.31 us
    pallas_call x1, Pallas kernels, per_device(): pl.pallas_call(lambda *refs: gradient_kernel(float(walkers_total), *refs)...  7.87 us
    all_to_all x1, waiting for transfers between devices, per_device(): gathered = lax.all_to_all(payload, DET_AXES, 0, 0)  4.69 us
    all_to_all x1, waiting for transfers between devices, per_device(): orb_all = lax.all_to_all(orb_rows, DET_AXES, 0, 0, tiled=True)  4.32 us
    all_to_all x1, starting transfers between devices, per_device(): orb_all = lax.all_to_all(orb_rows, DET_AXES, 0, 0, tiled=True)  3.5 us
    unnamed x4, local copies, waits for them, and re-layouts  2.12 us
  transfers between devices with their start and end apart: 4, of which 4 were waited for; matrix products, arithmetic and copies ran while one was open for 2% of the time, Pallas kernels for 3%

profile of v11, /device:TPU:0, one launch (start us, length us, event | category | flops | bytes accessed | tf_op | source)
XLA Modules:
  0.0 63.0 jit_solution(7065848679532692483)
XLA Ops:
  0.6 1.4 %shard_map.105 = f32[16,24,128]{2,1,0:T(8,128)} custom-call(s32[4,1024]{1,0:T(4,128)} %occ_ref.1, s32[4,1024]{1,0:T(4,128)} %virt_ref.3, s32[1,1024]{1,0:T(1,128)} %bitcast.11, f32[1,1024]{1,0:T(1,128)} %bitcast.12), custom_call_target="tpu_custom_call" | custom-call | tf_op jit(solution)/shard_map/pallas_call | solution.py:415
  2.1 8.3 %all-to-all-start = ((f32[16,24,128]{2,1,0:T(8,128)}), f32[16,24,128]{2,1,0:T(8,128)S(1)}, u32[]{:S(2)}, u32[]{:S(2)}) async-start(f32[16,24,128]{2,1,0:T(8,128)} %shard_map.105), calls=%async_computation | async-start | bytes 393216 | tf_op jit(solution)/shard_map/all_to_all | solution.py:421
  10.4 1.8 %shard_map.103.mine_ref = bf16[4,128,128]{2,1,0:T(8,128)(2,1)} custom-call(s32[4]{0:T(128)} %moved_ref.1, bf16[4,128,128]{2,1,0:T(8,128)(2,1)} %inv_ref.1, bf16[4,128]{1,0:T(4,128)(2,1)} %rows_ref.1, bf16[128,128]{1,0:T(8,128)(2,1)} %virt_ref.2), custom_call_target="tpu_custom_call" | custom-call | tf_op jit(solution)/shard_map/pallas_call | solution.py:422
  12.1 0.0 collective-permute-start
  12.1 1.6 %collective-permute-done.theirs_ref = bf16[4,128,128]{2,1,0:T(8,128)(2,1)S(1)} collective-permute-done((bf16[4,128,128]{2,1,0:T(8,128)(2,1)}, bf16[4,128,128]{2,1,0:T(8,128)(2,1)S(1)}, u32[]{:S(2)}, u32[]{:S(2)}) %collective-permute-start) | collective-permute-done | bytes 131104 | tf_op jit(solution)/shard_map/ppermute | solution.py:428
  13.7 0.0 copy-start
  13.7 0.9 %copy-done = bf16[4,128,128]{2,1,0:T(8,128)(2,1)S(1)} copy-done((bf16[4,128,128]{2,1,0:T(8,128)(2,1)S(1)}, bf16[4,128,128]{2,1,0:T(8,128)(2,1)}, u32[]{:S(2)}) %copy-start) | copy-done | bytes 131096
  14.6 0.2 shard_map.104
  14.9 4.7 %all-to-all-done.packed_ref.refs_3_ = f32[16,24,128]{2,1,0:T(8,128)S(1)} async-done(((f32[16,24,128]{2,1,0:T(8,128)}), f32[16,24,128]{2,1,0:T(8,128)S(1)}, u32[]{:S(2)}, u32[]{:S(2)}) %all-to-all-start) | async-done | bytes 196640 | tf_op jit(solution)/shard_map/all_to_all | solution.py:421
  19.6 12.7 %shard_map.106 = (f32[64,4,32,128]{3,2,1,0:T(8,128)S(1)}, f32[8,128]{1,0:T(8,128)S(1)}) custom-call(f8e4m3fn[1024,256]{1,0:T(32,128)(4,1)S(1)} %get-tuple-element.11.tab, f32[8,128]{1,0:T(8,128)S(1)} %get-tuple-element.12.back_ref, f32[16,24,128]{2,1,0:T(8,128)S(1)} %all-to-all-done.packed_ref.refs_3_), custom_call_target="tpu_custom_call" | custom-call | tf_op jit(solution)/shard_map/pallas_call | solution.py:439
  32.3 0.0 collective-permute-start.1
  32.3 1.2 %collective-permute-done.1.refs_1_ = f32[8,128]{1,0:T(8,128)S(1)} collective-permute-done((f32[8,128]{1,0:T(8,128)S(1)}, f32[8,128]{1,0:T(8,128)S(1)}, u32[]{:S(2)}, u32[]{:S(2)}) %collective-permute-start.1) | collective-permute-done | bytes 4128 | tf_op jit(solution)/shard_map/ppermute | solution.py:450
  33.4 7.9 %shard_map.107 = (f32[8,128]{1,0:T(8,128)S(1)}, f32[16,4,128]{2,1,0:T(4,128)}, f32[32,8,128]{2,1,0:T(8,128)S(1)}) custom-call(f32[8,128]{1,0:T(8,128)S(1)} %get-tuple-element.13.refs_0_, f32[8,128]{1,0:T(8,128)S(1)} %collective-permute-done.1.refs_1_, f32[64,4,32,128]{3,2,1,0:T(8,128)S(1)} %get-tuple-element.14.refs_2_, ...), custom_call_target="tpu_custom_call" | custom-call | tf_op jit(solution)/shard_map/pallas_call | solution.py:456
  41.3 9.6 %all_to_all.22.pieces_ref = f32[32,8,128]{2,1,0:T(8,128)S(1)} all-to-all(f32[32,8,128]{2,1,0:T(8,128)S(1)} %get-tuple-element.16), channel_id=1, replica_groups=mesh['walk'=2,'det'=4,'exc'=4] {'walk','det','exc'}, dimensions={0} | all-to-all | bytes 262144 | tf_op jit(solution)/shard_map/all_to_all | solution.py:470
  50.9 0.6 shard_map.108
  51.6 3.5 %all-to-all-start.2 = ((f32[16,4,128]{2,1,0:T(4,128)}), f32[16,4,128]{2,1,0:T(4,128)S(1)}, u32[]{:S(2)}, u32[]{:S(2)}) async-start(f32[16,4,128]{2,1,0:T(4,128)} %bitcast.2), calls=%async_computation.2 | async-start | bytes 65536 | tf_op jit(solution)/shard_map/all_to_all | solution.py:482
  55.1 0.6 slice_reduce_fusion
  55.7 1.8 %all_gather.3 = f32[2,2,256]{2,0,1:T(2,128)S(1)} all-gather(f32[2,1,256]{2,0,1:T(2,128)S(1)} %all_gather_reshape.3), channel_id=1, replica_groups=mesh['walk'=2,'det'=4,'exc'=4] {'walk'}, dimensions={1}, use_global_device_ids=true | all-gather | bytes 6144 | tf_op jit(solution)/shard_map/all_gather | solution.py:494
  57.5 0.6 copy.13
  58.1 4.3 %all-to-all-done.2 = f32[16,4,128]{2,1,0:T(4,128)S(1)} async-done(((f32[16,4,128]{2,1,0:T(4,128)}), f32[16,4,128]{2,1,0:T(4,128)S(1)}, u32[]{:S(2)}, u32[]{:S(2)}) %all-to-all-start.2) | async-done | bytes 32800 | tf_op jit(solution)/shard_map/all_to_all | solution.py:482
  62.4 0.6 copy.17
  (2 shorter events, 0.0 us)
Async XLA Ops:
  2.1 17.5 %all-to-all-start = ((f32[16,24,128]{2,1,0:T(8,128)}), f32[16,24,128]{2,1,0:T(8,128)S(1)}, u32[]{:S(2)}, u32[]{:S(2)}) async-start(f32[16,24,128]{2,1,0:T(8,128)} %shard_map.105), calls=%async_computation | async-start | bytes 393216 | tf_op jit(solution)/shard_map/all_to_all | solution.py:421
  12.1 1.6 %collective-permute-start = (bf16[4,128,128]{2,1,0:T(8,128)(2,1)}, bf16[4,128,128]{2,1,0:T(8,128)(2,1)S(1)}, u32[]{:S(2)}, u32[]{:S(2)}) collective-permute-start(bf16[4,128,128]{2,1,0:T(8,128)(2,1)} %shard_map.103.mine_ref), channel_id=1, source_target_pairs={{0,16},{16,0},{1,17},{17,1},{2,18},{18,2},{3,19},{19,3},{4,20},{20... | collective-permute-start | bytes 393224 | tf_op jit(solution)/shard_map/ppermute | solution.py:428
  13.7 0.9 %copy-start = (bf16[4,128,128]{2,1,0:T(8,128)(2,1)S(1)}, bf16[4,128,128]{2,1,0:T(8,128)(2,1)}, u32[]{:S(2)}) copy-start(bf16[4,128,128]{2,1,0:T(8,128)(2,1)} %shard_map.103.mine_ref) | copy-start | bytes 393220
  32.3 1.2 %collective-permute-start.1 = (f32[8,128]{1,0:T(8,128)S(1)}, f32[8,128]{1,0:T(8,128)S(1)}, u32[]{:S(2)}, u32[]{:S(2)}) collective-permute-start(f32[8,128]{1,0:T(8,128)S(1)} %get-tuple-element.13.refs_0_), channel_id=1, source_target_pairs={{0,16},{16,0},{1,17},{17,1},{2,18},{18,2},{3,19},{19,3},{4,20},{20... | collective-permute-start | bytes 12296 | tf_op jit(solution)/shard_map/ppermute | solution.py:450
  51.6 10.8 %all-to-all-start.2 = ((f32[16,4,128]{2,1,0:T(4,128)}), f32[16,4,128]{2,1,0:T(4,128)S(1)}, u32[]{:S(2)}, u32[]{:S(2)}) async-start(f32[16,4,128]{2,1,0:T(4,128)} %bitcast.2), calls=%async_computation.2 | async-start | bytes 65536 | tf_op jit(solution)/shard_map/all_to_all | solution.py:482
